TPU v7x, 32 devices: a whole 2x2x4 slice. The times are simulated.
32 devices in a mesh: dp: 8 (over z, y), fsdp: 4 (over x, core).
Axes of the slice: x: 2, y: 2, z: 4, core: 2. Of those that a mesh axis runs over, the one named last changes fastest.
Arguments:
- tokens: bfloat16 [1024, 40, 768], P(('dp', 'fsdp')), may hold values from -6 to 6
- patches: bfloat16 [128, 145, 1024], P(('dp', 'fsdp')), may hold values from -6 to 6
- segments: int32 [1024, 40], P(('dp', 'fsdp')), may hold values from 0 to 3, never falling along the last dimension, each value on 1 to 20 neighbouring positions
- owner: int32 [1024], P(('dp', 'fsdp')), may hold values from 0 to 7, as said below
- image_slot: int32 [1024], P(('dp', 'fsdp')), may hold values from 0 to 3
- out_grad: bfloat16 [1024, 40, 768], P(('dp', 'fsdp')), may hold values from -6 to 6
- self_query: bfloat16 [768, 768], P(('dp', 'fsdp')), may hold values from -0.21875 to 0.21875
- query_bias: bfloat16 [768], P(('dp', 'fsdp')), may hold values from -3 to 3
- self_key: bfloat16 [768, 768], P(('dp', 'fsdp')), may hold values from -0.21875 to 0.21875
- self_value: bfloat16 [768, 768], P(('dp', 'fsdp')), may hold values from -0.21875 to 0.21875
- value_bias: bfloat16 [768], P(('dp', 'fsdp')), may hold values from -3 to 3
- self_output: bfloat16 [768, 768], P(('dp', 'fsdp')), may hold values from -0.625 to 0.625
- output_bias: bfloat16 [768], P(('dp', 'fsdp')), may hold values from -3 to 3
- first_gain: bfloat16 [768], P(('dp', 'fsdp')), may hold values from 0.25 to 1.75
- first_norm_bias: bfloat16 [768], P(('dp', 'fsdp')), may hold values from -3 to 3
- patch_proj: bfloat16 [1024, 768], P(('dp', 'fsdp')), may hold values from -0.1875 to 0.1875
- patch_bias: bfloat16 [768], P(('dp', 'fsdp')), may hold values from -3 to 3
- cross_query: bfloat16 [768, 768], P(('dp', 'fsdp')), may hold values from -0.21875 to 0.21875
- probe_bias: bfloat16 [768], P(('dp', 'fsdp')), may hold values from -3 to 3
- cross_key: bfloat16 [768, 768], P(('dp', 'fsdp')), may hold values from -0.21875 to 0.21875
- cross_value: bfloat16 [768, 768], P(('dp', 'fsdp')), may hold values from -0.21875 to 0.21875
- content_bias: bfloat16 [768], P(('dp', 'fsdp')), may hold values from -3 to 3
- cross_output: bfloat16 [768, 768], P(('dp', 'fsdp')), may hold values from -1.25 to 1.25
- cross_bias: bfloat16 [768], P(('dp', 'fsdp')), may hold values from -3 to 3
- second_gain: bfloat16 [768], P(('dp', 'fsdp')), may hold values from 0.25 to 1.75
- second_shift: bfloat16 [768], P(('dp', 'fsdp')), may hold values from -3 to 3
- widen_weight: bfloat16 [768, 3072], P(('dp', 'fsdp')), may hold values from -0.21875 to 0.21875
- widen_bias: bfloat16 [3072], P(('dp', 'fsdp')), may hold values from -3 to 3
- narrow_weight: bfloat16 [3072, 768], P(('dp', 'fsdp')), may hold values from -0.15625 to 0.15625
- narrow_bias: bfloat16 [768], P(('dp', 'fsdp')), may hold values from -3 to 3
- third_gain: bfloat16 [768], P(('dp', 'fsdp')), may hold values from 0.25 to 1.75
- third_shift: bfloat16 [768], P(('dp', 'fsdp')), may hold values from -3 to 3
Outputs:
- output: bfloat16 [1024, 40, 768], P(('dp', 'fsdp'))
- tokens_grad: bfloat16 [1024, 40, 768], P(('dp', 'fsdp'))
- patches_grad: bfloat16 [128, 145, 1024], P(('dp', 'fsdp'))
- self_query_grad: float32 [768, 768], P(('dp', 'fsdp'))
- query_bias_grad: float32 [768], P(('dp', 'fsdp'))
- self_key_grad: float32 [768, 768], P(('dp', 'fsdp'))
- self_value_grad: float32 [768, 768], P(('dp', 'fsdp'))
- value_bias_grad: float32 [768], P(('dp', 'fsdp'))
- self_output_grad: float32 [768, 768], P(('dp', 'fsdp'))
- output_bias_grad: float32 [768], P(('dp', 'fsdp'))
- first_norm_gain_gradient: float32 [768], P(('dp', 'fsdp'))
- first_shift_grad: float32 [768], P(('dp', 'fsdp'))
- patch_proj_grad: float32 [1024, 768], P(('dp', 'fsdp'))
- patch_bias_grad: float32 [768], P(('dp', 'fsdp'))
- cross_query_grad: float32 [768, 768], P(('dp', 'fsdp'))
- probe_bias_grad: float32 [768], P(('dp', 'fsdp'))
- cross_key_grad: float32 [768, 768], P(('dp', 'fsdp'))
- cross_value_grad: float32 [768, 768], P(('dp', 'fsdp'))
- content_bias_grad: float32 [768], P(('dp', 'fsdp'))
- cross_output_grad: float32 [768, 768], P(('dp', 'fsdp'))
- cross_attention_bias_gradient: float32 [768], P(('dp', 'fsdp'))
- second_gain_grad: float32 [768], P(('dp', 'fsdp'))
- second_shift_grad: float32 [768], P(('dp', 'fsdp'))
- widen_weight_grad: float32 [768, 3072], P(('dp', 'fsdp'))
- widen_bias_grad: float32 [3072], P(('dp', 'fsdp'))
- narrow_weight_grad: float32 [3072, 768], P(('dp', 'fsdp'))
- narrow_bias_grad: float32 [768], P(('dp', 'fsdp'))
- third_gain_grad: float32 [768], P(('dp', 'fsdp'))
- third_shift_grad: float32 [768], P(('dp', 'fsdp'))
Inputs may be any that keep to these rules, and one draw needn't show every extreme that they name: Among the 32 rows of one device at most 8 name the same owner, and among the devices with one fsdp index one owner is named by exactly 8 rows of each of them.
All inputs are finite; a program needn't handle non-finite values.
Results may differ from a plain program's by a relative error of at most 0.024.
Values may be sent and summed in bfloat16 or wider, within the bound.
A program may use at most 384 MiB of HBM per device.

v0:
```python
import jax
import jax.numpy as jnp
from jax import lax
from jax.sharding import PartitionSpec as P

HEADS = 12


norm_eps = 1e-06
neg_fill = -1000000000.0
slot_block = 16


def product(left, right):
    return jnp.dot(left, right, preferred_element_type=jnp.float32)


def product_rows(left, right):
    return lax.dot_general(
        left, right, (((0,), (0,)), ((), ())), preferred_element_type=jnp.float32
    )


def product_back(left, right):
    return lax.dot_general(
        left, right, (((1,), (1,)), ((), ())), preferred_element_type=jnp.float32
    )


def column_total(values):
    return jnp.sum(values.astype(jnp.float32), 0)


def layer_norm(value, gain, shift):
    mean = jnp.mean(value, -1, keepdims=True)
    centred = value - mean
    spread = jnp.mean(centred * centred, -1, keepdims=True)
    return centred * lax.rsqrt(spread + norm_eps) * gain + shift


def exact_gelu(value):
    return jax.nn.gelu(value, approximate=False)


def split_heads(values, heads):
    count, length, width = values.shape
    return values.reshape(count, length, heads, width // heads)


def scores_of(query, keys, mask, heads):
    scale = (query.shape[-1] // heads) ** (-0.5)
    scores = (
        jnp.einsum(
            "blhe,bmhe->bhlm",
            split_heads(query, heads),
            split_heads(keys, heads),
            preferred_element_type=jnp.float32,
        )
        * scale
    )
    if mask is not None:
        scores = jnp.where(mask[:, None], scores, neg_fill)
    return scores


def attend(query, keys, values, mask, heads):
    scores = scores_of(query, keys, mask, heads)
    top = jnp.max(scores, -1, keepdims=True)
    expd = jnp.exp(scores - top)
    total = jnp.sum(expd, -1, keepdims=True)
    probs = (expd / total).astype(jnp.bfloat16)
    mixed = jnp.einsum(
        "bhlm,bmhe->blhe", probs, split_heads(values, heads), preferred_element_type=jnp.float32
    )
    return (mixed.reshape(query.shape).astype(jnp.bfloat16), top + jnp.log(total))


def attend_back(query, keys, values, mask, logsum, grad_mixed, heads):
    scale = (query.shape[-1] // heads) ** (-0.5)
    probs = jnp.exp(scores_of(query, keys, mask, heads) - logsum)
    grad_heads = split_heads(grad_mixed, heads)
    grad_probs = jnp.einsum(
        "blhe,bmhe->bhlm",
        grad_heads,
        split_heads(values, heads),
        preferred_element_type=jnp.float32,
    )
    weighted = jnp.sum(grad_probs * probs, -1, keepdims=True)
    grad_scores = (probs * (grad_probs - weighted)).astype(jnp.bfloat16)
    grad_query = (
        jnp.einsum(
            "bhlm,bmhe->blhe",
            grad_scores,
            split_heads(keys, heads),
            preferred_element_type=jnp.float32,
        )
        * scale
    )
    grad_keys = (
        jnp.einsum(
            "bhlm,blhe->bmhe",
            grad_scores,
            split_heads(query, heads),
            preferred_element_type=jnp.float32,
        )
        * scale
    )
    grad_values = jnp.einsum(
        "bhlm,blhe->bmhe",
        probs.astype(jnp.bfloat16),
        grad_heads,
        preferred_element_type=jnp.float32,
    )
    return (
        grad_query.reshape(query.shape),
        grad_keys.reshape(keys.shape),
        grad_values.reshape(values.shape),
    )


def on_device(
    tokens,
    patches,
    segments,
    owner,
    image_slot,
    out_grad,
    self_query,
    query_bias,
    self_key,
    self_value,
    value_bias,
    self_output,
    output_bias,
    first_gain,
    first_norm_bias,
    patch_proj,
    patch_bias,
    cross_query,
    probe_bias,
    cross_key,
    cross_value,
    content_bias,
    cross_output,
    cross_bias,
    second_gain,
    second_shift,
    widen_weight,
    widen_bias,
    narrow_weight,
    narrow_bias,
    third_gain,
    third_shift,
):
    gathered = (
        lax.all_gather(self_query, ("dp", "fsdp"), axis=0, tiled=True),
        lax.all_gather(query_bias, ("dp", "fsdp"), axis=0, tiled=True),
        lax.all_gather(self_key, ("dp", "fsdp"), axis=0, tiled=True),
        lax.all_gather(self_value, ("dp", "fsdp"), axis=0, tiled=True),
        lax.all_gather(value_bias, ("dp", "fsdp"), axis=0, tiled=True),
        lax.all_gather(self_output, ("dp", "fsdp"), axis=0, tiled=True),
        lax.all_gather(output_bias, ("dp", "fsdp"), axis=0, tiled=True),
        lax.all_gather(first_gain, ("dp", "fsdp"), axis=0, tiled=True),
        lax.all_gather(first_norm_bias, ("dp", "fsdp"), axis=0, tiled=True),
        lax.all_gather(patch_proj, ("dp", "fsdp"), axis=0, tiled=True),
        lax.all_gather(patch_bias, ("dp", "fsdp"), axis=0, tiled=True),
        lax.all_gather(cross_query, ("dp", "fsdp"), axis=0, tiled=True),
        lax.all_gather(probe_bias, ("dp", "fsdp"), axis=0, tiled=True),
        lax.all_gather(cross_key, ("dp", "fsdp"), axis=0, tiled=True),
        lax.all_gather(cross_value, ("dp", "fsdp"), axis=0, tiled=True),
        lax.all_gather(content_bias, ("dp", "fsdp"), axis=0, tiled=True),
        lax.all_gather(cross_output, ("dp", "fsdp"), axis=0, tiled=True),
        lax.all_gather(cross_bias, ("dp", "fsdp"), axis=0, tiled=True),
        lax.all_gather(second_gain, ("dp", "fsdp"), axis=0, tiled=True),
        lax.all_gather(second_shift, ("dp", "fsdp"), axis=0, tiled=True),
        lax.all_gather(widen_weight, ("dp", "fsdp"), axis=0, tiled=True),
        lax.all_gather(widen_bias, ("dp", "fsdp"), axis=0, tiled=True),
        lax.all_gather(narrow_weight, ("dp", "fsdp"), axis=0, tiled=True),
        lax.all_gather(narrow_bias, ("dp", "fsdp"), axis=0, tiled=True),
        lax.all_gather(third_gain, ("dp", "fsdp"), axis=0, tiled=True),
        lax.all_gather(third_shift, ("dp", "fsdp"), axis=0, tiled=True),
    )
    float_of = [item.astype(jnp.float32) for item in gathered]
    query_full, key_full, value_full, output_full = (
        gathered[0],
        gathered[2],
        gathered[3],
        gathered[5],
    )
    patch_full, probe_full, ckey_full, cvalue_full, cout_full = (
        gathered[9],
        gathered[11],
        gathered[13],
        gathered[14],
        gathered[16],
    )
    widen_full, narrow_full = (gathered[20], gathered[22])
    rows, length, width = tokens.shape
    groups = lax.axis_size("dp")
    slots = 2 * rows
    capacity = slots // groups
    member = (owner[:, None] == jnp.arange(groups)[None, :]).astype(jnp.int32)
    earlier = jnp.cumsum(member, 0) - member
    position = owner * capacity + jnp.sum(earlier * member, 1)
    placing = (position[None, :] == jnp.arange(slots)[:, None]).astype(jnp.bfloat16)
    send_images = jnp.zeros((slots,), jnp.int32).at[position].set(image_slot)
    send_rows = product(placing, tokens.reshape(rows, -1)).astype(jnp.bfloat16)
    send_segments = jnp.zeros((slots, length), jnp.int32).at[position].set(segments)
    got_rows, got_segments, got_images = (
        lax.all_to_all(
            send_rows.reshape(groups, capacity, length, width),
            "dp",
            split_axis=0,
            concat_axis=0,
            tiled=True,
        ),
        lax.all_to_all(
            send_segments.reshape(groups, capacity, length),
            "dp",
            split_axis=0,
            concat_axis=0,
            tiled=True,
        ),
        lax.all_to_all(
            send_images.reshape(groups, capacity), "dp", split_axis=0, concat_axis=0, tiled=True
        ),
    )
    rows_in = got_rows.reshape(slots, length, width)
    row_segments = got_segments.reshape(slots, length)
    count = rows_in.shape[0]
    flat_in = rows_in.reshape(count * length, width)
    query = (
        (product(flat_in, query_full) + float_of[1])
        .astype(jnp.bfloat16)
        .reshape(count, length, width)
    )
    key = product(flat_in, key_full).astype(jnp.bfloat16).reshape(count, length, width)
    value = (
        (product(flat_in, value_full) + float_of[4])
        .astype(jnp.bfloat16)
        .reshape(count, length, width)
    )
    mask = row_segments[:, :, None] == row_segments[:, None, :]
    attended, logsum = attend(query, key, value, mask, HEADS)
    attended_flat = attended.reshape(-1, width)
    first_in = flat_in.astype(jnp.float32) + product(attended_flat, output_full) + float_of[6]
    first_val, first_back = jax.vjp(layer_norm, first_in, float_of[7], float_of[8])
    first_low = first_val.astype(jnp.bfloat16)
    images, points = (patches.shape[0], patches.shape[1])
    patch_flat = patches.reshape(images * points, -1)
    projected = (product(patch_flat, patch_full) + float_of[10]).astype(jnp.bfloat16)
    image_keys = product(projected, ckey_full).astype(jnp.bfloat16).reshape(images, points, width)
    image_values = (
        (product(projected, cvalue_full) + float_of[15])
        .astype(jnp.bfloat16)
        .reshape(images, points, width)
    )
    blocks = slots // slot_block
    probe = (product(first_low, probe_full) + float_of[12]).astype(jnp.bfloat16)
    probe_blocks = probe.reshape(blocks, slot_block, length, width)
    image_blocks = got_images.reshape(blocks, slot_block)

    def cross_block(pieces):
        block_probe, block_images = pieces
        return attend(
            block_probe,
            jnp.take(image_keys, block_images, 0),
            jnp.take(image_values, block_images, 0),
            None,
            HEADS,
        )

    crossed, cross_logsum = lax.map(cross_block, (probe_blocks, image_blocks))
    crossed_flat = crossed.reshape(-1, width)
    second_in = first_val + product(crossed_flat, cout_full) + float_of[17]
    second, second_back = jax.vjp(layer_norm, second_in, float_of[18], float_of[19])
    returned_outputs = lax.all_to_all(
        second.astype(jnp.bfloat16).reshape(groups, capacity, length, width),
        "dp",
        split_axis=0,
        concat_axis=0,
        tiled=True,
    )
    hidden_in = jnp.take(returned_outputs.reshape(slots, length, width), position, 0).reshape(
        rows * length, width
    )
    inner = product(hidden_in, widen_full) + float_of[21]
    active, gelu_back = jax.vjp(exact_gelu, inner)
    active_low = active.astype(jnp.bfloat16)
    third_in = hidden_in.astype(jnp.float32) + product(active_low, narrow_full) + float_of[23]
    third, third_back = jax.vjp(layer_norm, third_in, float_of[24], float_of[25])
    output = third.astype(jnp.bfloat16).reshape(rows, length, width)
    again = (
        lax.all_gather(self_query, ("dp", "fsdp"), axis=0, tiled=True),
        lax.all_gather(query_bias, ("dp", "fsdp"), axis=0, tiled=True),
        lax.all_gather(self_key, ("dp", "fsdp"), axis=0, tiled=True),
        lax.all_gather(self_value, ("dp", "fsdp"), axis=0, tiled=True),
        lax.all_gather(value_bias, ("dp", "fsdp"), axis=0, tiled=True),
        lax.all_gather(self_output, ("dp", "fsdp"), axis=0, tiled=True),
        lax.all_gather(output_bias, ("dp", "fsdp"), axis=0, tiled=True),
        lax.all_gather(first_gain, ("dp", "fsdp"), axis=0, tiled=True),
        lax.all_gather(first_norm_bias, ("dp", "fsdp"), axis=0, tiled=True),
        lax.all_gather(patch_proj, ("dp", "fsdp"), axis=0, tiled=True),
        lax.all_gather(patch_bias, ("dp", "fsdp"), axis=0, tiled=True),
        lax.all_gather(cross_query, ("dp", "fsdp"), axis=0, tiled=True),
        lax.all_gather(probe_bias, ("dp", "fsdp"), axis=0, tiled=True),
        lax.all_gather(cross_key, ("dp", "fsdp"), axis=0, tiled=True),
        lax.all_gather(cross_value, ("dp", "fsdp"), axis=0, tiled=True),
        lax.all_gather(content_bias, ("dp", "fsdp"), axis=0, tiled=True),
        lax.all_gather(cross_output, ("dp", "fsdp"), axis=0, tiled=True),
        lax.all_gather(cross_bias, ("dp", "fsdp"), axis=0, tiled=True),
        lax.all_gather(second_gain, ("dp", "fsdp"), axis=0, tiled=True),
        lax.all_gather(second_shift, ("dp", "fsdp"), axis=0, tiled=True),
        lax.all_gather(widen_weight, ("dp", "fsdp"), axis=0, tiled=True),
        lax.all_gather(widen_bias, ("dp", "fsdp"), axis=0, tiled=True),
        lax.all_gather(narrow_weight, ("dp", "fsdp"), axis=0, tiled=True),
        lax.all_gather(narrow_bias, ("dp", "fsdp"), axis=0, tiled=True),
        lax.all_gather(third_gain, ("dp", "fsdp"), axis=0, tiled=True),
        lax.all_gather(third_shift, ("dp", "fsdp"), axis=0, tiled=True),
    )
    query_back, key_back, value_back, output_back = (again[0], again[2], again[3], again[5])
    patch_back, probe_back, ckey_back, cvalue_back, cout_back = (
        again[9],
        again[11],
        again[13],
        again[14],
        again[16],
    )
    widen_back, narrow_back = (again[20], again[22])
    grad_summed, grad_gain_third, grad_shift_third = third_back(
        out_grad.reshape(-1, width).astype(jnp.float32)
    )
    grad_branch_three = grad_summed.astype(jnp.bfloat16)
    grad_narrow_bias = column_total(grad_branch_three)
    grad_narrow = product_rows(active_low, grad_branch_three)
    grad_inner = gelu_back(product_back(grad_branch_three, narrow_back))[0].astype(jnp.bfloat16)
    grad_widen_bias = column_total(grad_inner)
    grad_widen = product_rows(hidden_in, grad_inner)
    grad_hidden = (grad_summed + product_back(grad_inner, widen_back)).astype(jnp.bfloat16)
    send_grad = product(placing, grad_hidden.reshape(rows, -1)).astype(jnp.bfloat16)
    got_grad = lax.all_to_all(
        send_grad.reshape(groups, capacity, length, width),
        "dp",
        split_axis=0,
        concat_axis=0,
        tiled=True,
    )
    grad_mid, grad_gain_second, grad_shift_second = second_back(
        got_grad.reshape(-1, width).astype(jnp.float32)
    )
    grad_branch_two = grad_mid.astype(jnp.bfloat16)
    grad_cross_bias = column_total(grad_branch_two)
    grad_cross_output = product_rows(crossed_flat, grad_branch_two)
    grad_crossed = (
        product_back(grad_branch_two, cout_back)
        .astype(jnp.bfloat16)
        .reshape(blocks, slot_block, length, width)
    )

    def cross_back(carry, pieces):
        key_total, value_total = carry
        block_probe, block_images, block_logsum, block_grad = pieces
        grad_probe_part, grad_keys, grad_values = attend_back(
            block_probe,
            jnp.take(image_keys, block_images, 0),
            jnp.take(image_values, block_images, 0),
            None,
            block_logsum,
            block_grad,
            HEADS,
        )
        picker = (block_images[:, None] == jnp.arange(images)[None, :]).astype(jnp.float32)
        key_total = key_total + jnp.einsum(
            "si,spd->ipd", picker, grad_keys, precision=lax.Precision.HIGHEST
        )
        value_total = value_total + jnp.einsum(
            "si,spd->ipd", picker, grad_values, precision=lax.Precision.HIGHEST
        )
        return ((key_total, value_total), grad_probe_part.astype(jnp.bfloat16))

    zero_total = jnp.zeros((images, points, width), jnp.float32)
    (image_key_grad, image_value_grad), grad_probe_blocks = lax.scan(
        cross_back,
        (zero_total, zero_total),
        (probe_blocks, image_blocks, cross_logsum, grad_crossed),
    )
    grad_probe = grad_probe_blocks.reshape(-1, width)
    grad_probe_bias = column_total(grad_probe)
    grad_cross_query = product_rows(first_low, grad_probe)
    grad_first = grad_mid + product_back(grad_probe, probe_back)
    keys_low = image_key_grad.astype(jnp.bfloat16).reshape(-1, width)
    values_low = image_value_grad.astype(jnp.bfloat16).reshape(-1, width)
    grad_content_bias = column_total(values_low)
    grad_cross_key = product_rows(projected, keys_low)
    grad_cross_value = product_rows(projected, values_low)
    grad_projected = (
        product_back(keys_low, ckey_back) + product_back(values_low, cvalue_back)
    ).astype(jnp.bfloat16)
    grad_patch_bias = column_total(grad_projected)
    grad_patch_proj = product_rows(patch_flat, grad_projected)
    patches_grad = (
        product_back(grad_projected, patch_back).astype(jnp.bfloat16).reshape(patches.shape)
    )
    flat_in, query, key, value, mask, attended_flat, logsum, first_back = (
        flat_in,
        query,
        key,
        value,
        mask,
        attended_flat,
        logsum,
        first_back,
    )
    grad_low, grad_gain_first, grad_shift_first = first_back(grad_first)
    grad_branch_one = grad_low.astype(jnp.bfloat16)
    grad_output_bias = column_total(grad_branch_one)
    grad_self_output = product_rows(attended_flat, grad_branch_one)
    grad_attended = (
        product_back(grad_branch_one, output_back).astype(jnp.bfloat16).reshape(query.shape)
    )
    grad_query, grad_key, grad_value = attend_back(
        query, key, value, mask, logsum, grad_attended, HEADS
    )
    grad_query = grad_query.astype(jnp.bfloat16).reshape(-1, width)
    grad_key = grad_key.astype(jnp.bfloat16).reshape(-1, width)
    grad_value = grad_value.astype(jnp.bfloat16).reshape(-1, width)
    terms = (
        product_rows(flat_in, grad_query),
        column_total(grad_query),
        product_rows(flat_in, grad_key),
        product_rows(flat_in, grad_value),
        column_total(grad_value),
        grad_self_output,
        grad_output_bias,
        grad_gain_first,
        grad_shift_first,
    )
    grad_flat = (
        grad_low
        + product_back(grad_query, query_back)
        + product_back(grad_key, key_back)
        + product_back(grad_value, value_back)
    )
    self_terms, grad_flat = (terms, grad_flat)
    back_rows = lax.all_to_all(
        grad_flat.astype(jnp.bfloat16).reshape(groups, capacity, length, width),
        "dp",
        split_axis=0,
        concat_axis=0,
        tiled=True,
    )
    tokens_grad = jnp.take(back_rows.reshape(slots, length, width), position, 0)
    (
        term_squery,
        term_qbias,
        self_key_gradient_term,
        term_svalue,
        term_vbias,
        term_soutput,
        term_obias,
        term_gain_first,
        term_shift_first,
    ) = self_terms
    shard_grads = (
        lax.psum_scatter(term_squery, ("dp", "fsdp"), scatter_dimension=0, tiled=True),
        lax.psum_scatter(term_qbias, ("dp", "fsdp"), scatter_dimension=0, tiled=True),
        lax.psum_scatter(self_key_gradient_term, ("dp", "fsdp"), scatter_dimension=0, tiled=True),
        lax.psum_scatter(term_svalue, ("dp", "fsdp"), scatter_dimension=0, tiled=True),
        lax.psum_scatter(term_vbias, ("dp", "fsdp"), scatter_dimension=0, tiled=True),
        lax.psum_scatter(term_soutput, ("dp", "fsdp"), scatter_dimension=0, tiled=True),
        lax.psum_scatter(term_obias, ("dp", "fsdp"), scatter_dimension=0, tiled=True),
        lax.psum_scatter(term_gain_first, ("dp", "fsdp"), scatter_dimension=0, tiled=True),
        lax.psum_scatter(term_shift_first, ("dp", "fsdp"), scatter_dimension=0, tiled=True),
        lax.psum_scatter(grad_patch_proj, ("dp", "fsdp"), scatter_dimension=0, tiled=True),
        lax.psum_scatter(grad_patch_bias, ("dp", "fsdp"), scatter_dimension=0, tiled=True),
        lax.psum_scatter(grad_cross_query, ("dp", "fsdp"), scatter_dimension=0, tiled=True),
        lax.psum_scatter(grad_probe_bias, ("dp", "fsdp"), scatter_dimension=0, tiled=True),
        lax.psum_scatter(grad_cross_key, ("dp", "fsdp"), scatter_dimension=0, tiled=True),
        lax.psum_scatter(grad_cross_value, ("dp", "fsdp"), scatter_dimension=0, tiled=True),
        lax.psum_scatter(grad_content_bias, ("dp", "fsdp"), scatter_dimension=0, tiled=True),
        lax.psum_scatter(grad_cross_output, ("dp", "fsdp"), scatter_dimension=0, tiled=True),
        lax.psum_scatter(grad_cross_bias, ("dp", "fsdp"), scatter_dimension=0, tiled=True),
        lax.psum_scatter(grad_gain_second, ("dp", "fsdp"), scatter_dimension=0, tiled=True),
        lax.psum_scatter(grad_shift_second, ("dp", "fsdp"), scatter_dimension=0, tiled=True),
        lax.psum_scatter(grad_widen, ("dp", "fsdp"), scatter_dimension=0, tiled=True),
        lax.psum_scatter(grad_widen_bias, ("dp", "fsdp"), scatter_dimension=0, tiled=True),
        lax.psum_scatter(grad_narrow, ("dp", "fsdp"), scatter_dimension=0, tiled=True),
        lax.psum_scatter(grad_narrow_bias, ("dp", "fsdp"), scatter_dimension=0, tiled=True),
        lax.psum_scatter(grad_gain_third, ("dp", "fsdp"), scatter_dimension=0, tiled=True),
        lax.psum_scatter(grad_shift_third, ("dp", "fsdp"), scatter_dimension=0, tiled=True),
    )
    return (output, tokens_grad, patches_grad, *shard_grads)


def solution(mesh):
    placed = (
        P(("dp", "fsdp"), None, None),
        P(("dp", "fsdp"), None, None),
        P(("dp", "fsdp"), None),
        P(("dp", "fsdp")),
        P(("dp", "fsdp")),
        P(("dp", "fsdp"), None, None),
        P(("dp", "fsdp"), None),
        P(("dp", "fsdp")),
        P(("dp", "fsdp"), None),
        P(("dp", "fsdp"), None),
        P(("dp", "fsdp")),
        P(("dp", "fsdp"), None),
        P(("dp", "fsdp")),
        P(("dp", "fsdp")),
        P(("dp", "fsdp")),
        P(("dp", "fsdp"), None),
        P(("dp", "fsdp")),
        P(("dp", "fsdp"), None),
        P(("dp", "fsdp")),
        P(("dp", "fsdp"), None),
        P(("dp", "fsdp"), None),
        P(("dp", "fsdp")),
        P(("dp", "fsdp"), None),
        P(("dp", "fsdp")),
        P(("dp", "fsdp")),
        P(("dp", "fsdp")),
        P(("dp", "fsdp"), None),
        P(("dp", "fsdp")),
        P(("dp", "fsdp"), None),
        P(("dp", "fsdp")),
        P(("dp", "fsdp")),
        P(("dp", "fsdp")),
    )
    return jax.shard_map(
        on_device,
        mesh=mesh,
        in_specs=placed,
        out_specs=(
            P(("dp", "fsdp"), None, None),
            P(("dp", "fsdp"), None, None),
            P(("dp", "fsdp"), None, None),
            P(("dp", "fsdp"), None),
            P(("dp", "fsdp")),
            P(("dp", "fsdp"), None),
            P(("dp", "fsdp"), None),
            P(("dp", "fsdp")),
            P(("dp", "fsdp"), None),
            P(("dp", "fsdp")),
            P(("dp", "fsdp")),
            P(("dp", "fsdp")),
            P(("dp", "fsdp"), None),
            P(("dp", "fsdp")),
            P(("dp", "fsdp"), None),
            P(("dp", "fsdp")),
            P(("dp", "fsdp"), None),
            P(("dp", "fsdp"), None),
            P(("dp", "fsdp")),
            P(("dp", "fsdp"), None),
            P(("dp", "fsdp")),
            P(("dp", "fsdp")),
            P(("dp", "fsdp")),
            P(("dp", "fsdp"), None),
            P(("dp", "fsdp")),
            P(("dp", "fsdp"), None),
            P(("dp", "fsdp")),
            P(("dp", "fsdp")),
            P(("dp", "fsdp")),
        ),
        check_vma=False,
    )
```

profile of v0, /device:TPU:0, one launch (start us, length us, event | category | flops | bytes accessed | tf_op | source)
XLA Modules:
  0.0 2737.5 jit_solution(15889692145840456793)
XLA Ops:
  49.9 106.7 %all-reduce.31 = (bf16[768]{0:T(1024)(128)(2,1)S(1)}, bf16[768]{0:T(1024)(128)(2,1)S(1)}, bf16[768]{0:T(1024)(128)(2,1)S(1)}, bf16[768]{0:T(1024)(128)(2,1)S(1)}...) all-reduce(bf16[768]{0:T(1024)(128)(2,1)S(1)} %dynamic-update-slice, ...), channel_id=1, replica_groups=mesh['dp'=8,'fsdp'=4] {'dp','fsdp'}, use_global_device_ids=true, to_apply=%add.1 | all-reduce | flops 13824 | bytes 55296
  174.8 53.5 %all-gather.26.cloned.1.call-done = bf16[768,768]{1,0:T(8,128)(2,1)} async-done(((bf16[24,768]{1,0:T(8,128)(2,1)}), bf16[768,768]{1,0:T(8,128)(2,1)}) %all-gather.26.cloned.1.call-update) | async-done | bytes 1179664 | tf_op jit(solution)/shard_map/all_gather | solution.py:169
  235.8 48.3 %all-gather.16.cloned.1.call-done = bf16[768,768]{1,0:T(8,128)(2,1)} async-done(((bf16[24,768]{1,0:T(8,128)(2,1)}), bf16[768,768]{1,0:T(8,128)(2,1)}) %all-gather.16.cloned.1.call-update) | async-done | bytes 1179664 | tf_op jit(solution)/shard_map/all_gather | solution.py:158
  291.6 13.1 reshape_reshape.23
  304.7 35.1 %all-gather.12.cloned.1.call-done = bf16[768,768]{1,0:T(8,128)(2,1)} async-done(((bf16[24,768]{1,0:T(8,128)(2,1)}), bf16[768,768]{1,0:T(8,128)(2,1)}) %all-gather.12.cloned.1.call-update) | async-done | bytes 1179664 | tf_op jit(solution)/shard_map/all_gather | solution.py:159
  347.3 12.8 reshape_reshape.21
  360.1 35.4 %all-gather.14.cloned.1.call-done = bf16[768,768]{1,0:T(8,128)(2,1)} async-done(((bf16[24,768]{1,0:T(8,128)(2,1)}), bf16[768,768]{1,0:T(8,128)(2,1)}) %all-gather.14.cloned.1.call-update) | async-done | bytes 1179664 | tf_op jit(solution)/shard_map/all_gather | solution.py:156
  403.1 12.8 reshape_reshape.22
  415.9 14.7 fusion.78
  441.3 13.8 convert_bitcast_fusion.2
  465.4 13.6 convert_element_type.289
  493.2 14.1 all-gather.24.cloned.1.call-done
  517.1 202.5 %while.27 = (s32[]{:T(128)}, bf16[4,16,40,768]{3,2,1,0:T(8,128)(2,1)}, f32[4,16,12,40,1]{3,2,1,4,0:T(8,128)}, s32[4,16]{1,0:T(4,128)S(1)}, bf16[4,145,768]{2,1,0...) while((s32[]{:T(128)}, ...), condition=%wide.region_11.13_spmd, body=%wide.region_8.12_spmd.sunk | while | flops 299152480 | bytes 94274040 | solution.py:273
  742.2 95.2 %all-to-all-done.3 = bf16[8,8,40,768]{3,2,1,0:T(8,128)(2,1)} async-done(((bf16[8,8,40,768]{3,2,1,0:T(8,128)(2,1)}), bf16[8,8,40,768]{3,2,1,0:T(8,128)(2,1)}, u32[]{:S(2)}, u32[]{:S(2)}) %all-to-all-start.3) | async-done | bytes 3932192 | tf_op jit(solution)/shard_map/all_to_all | solution.py:277
  841.7 45.6 %multiply_convert_fusion.5 = (bf16[1280,3072]{1,0:T(8,128)(2,1)}, f32[1280,3072]{1,0:T(8,128)}, f32[1280,3072]{1,0:T(8,128)}) fusion(f32[3072]{0:T(1024)S(1)} %convert_element_type.306, bf16[1280,768]{1,0:T(8,128)(2,1)} %bitcast.247, bf16[768,3072]{1,0:T(8,128)(2,1)} %all-gather.30.cloned.1.call-done), kind=kOutput, calls=%fused_computation.74 | convolution fusion | flops 6299320320 | bytes 46018560 | tf_op jit(solution)/shard_map/dot_general | solution.py:15
  906.9 20.8 convert_reduce_fusion
  950.0 87.1 %all-to-all-done.4 = bf16[8,8,40,768]{3,2,1,0:T(8,128)(2,1)} async-done(((bf16[8,8,40,768]{3,2,1,0:T(8,128)(2,1)}), bf16[8,8,40,768]{3,2,1,0:T(8,128)(2,1)}, u32[]{:S(2)}, u32[]{:S(2)}) %all-to-all-start.4) | async-done | bytes 3932192 | tf_op jit(solution)/shard_map/all_to_all | solution.py:341
  1072.7 516.9 %while.28 = (s32[]{:T(128)}, f32[4,145,768]{2,0,1:T(4,128)}, f32[4,145,768]{2,0,1:T(4,128)}, bf16[4,16,40,768]{3,2,1,0:T(8,128)(2,1)}, s32[4,16]{1,0:T(4,128)}, ...) while((s32[]{:T(128)}, f32[4,145,768]{2,0,1:T(4,128)}, ...), condition=%wide.region_22.25_spmd.clone, body=%wide.region_20.24_spmd.clone.sunk | while | flops 905219840 | bytes 219434896 | solution.py:382
  1606.2 13.4 multiply_reduce_fusion.3
  1662.5 21.2 multiply_reduce_fusion.2
  1683.8 14.2 multiply_convert_fusion.4
  1718.7 13.5 convert_element_type.330
  1761.7 13.4 convert_element_type.327
  1783.2 14.1 convert_reduce_fusion.1
  1807.6 13.5 convert_element_type.334
  1907.2 103.5 %all-reduce.30 = (f32[768]{0:T(1024)S(1)}, f32[768]{0:T(1024)S(1)}, f32[768]{0:T(1024)S(1)}, f32[768]{0:T(1024)S(1)}, f32[768]{0:T(1024)S(1)}, /*index=5*/f32[76...) all-reduce(f32[768]{0:T(1024)S(1)} %reduce_sum.356, ...), channel_id=3, replica_groups=mesh['dp'=8,'fsdp'=4] {'dp','fsdp'}, use_global_device_ids=true, to_apply=%region_28.31.clone | all-reduce | flops 13824 | bytes 110592
  2027.5 104.5 %reduce-scatter.16.cloned.1.call-done = f32[24,768]{1,0:T(8,128)} async-done(((f32[768,768]{1,0:T(8,128)}), f32[24,768]{1,0:T(8,128)}) %reduce-scatter.16.cloned.1.call-update) | async-done | bytes 73744 | tf_op jit(solution)/shard_map/reduce_scatter | solution.py:467
  2132.0 103.9 %reduce-scatter.14.cloned.1.call-done = f32[24,768]{1,0:T(8,128)} async-done(((f32[768,768]{1,0:T(8,128)}), f32[24,768]{1,0:T(8,128)}) %reduce-scatter.14.cloned.1.call-update) | async-done | bytes 73744 | tf_op jit(solution)/shard_map/reduce_scatter | solution.py:465
  2235.9 104.8 %reduce-scatter.18.cloned.1.call-done = f32[24,768]{1,0:T(8,128)} async-done(((f32[768,768]{1,0:T(8,128)}), f32[24,768]{1,0:T(8,128)}) %reduce-scatter.18.cloned.1.call-update) | async-done | bytes 73744 | tf_op jit(solution)/shard_map/reduce_scatter | solution.py:468
  2340.7 106.4 %reduce-scatter.34.cloned.1.call-done = f32[32,768]{1,0:T(8,128)} async-done(((f32[1024,768]{1,0:T(8,128)}), f32[32,768]{1,0:T(8,128)}) %reduce-scatter.34.cloned.1.call-update) | async-done | bytes 98320
  2447.1 140.9 %reduce-scatter.32.cloned.1.call-done = f32[96,768]{1,0:T(8,128)} async-done(((f32[3072,768]{1,0:T(8,128)}), f32[96,768]{1,0:T(8,128)}) %reduce-scatter.32.cloned.1.call-update) | async-done | bytes 294928 | tf_op jit(solution)/shard_map/reduce_scatter | solution.py:487
  2588.0 142.2 %reduce-scatter.30.cloned.1.call-done = f32[24,3072]{1,0:T(8,128)} async-done(((f32[768,3072]{1,0:T(8,128)}), f32[24,3072]{1,0:T(8,128)}) %reduce-scatter.30.cloned.1.call-update) | async-done | bytes 294928 | tf_op jit(solution)/shard_map/reduce_scatter | solution.py:485
  (676 shorter events, 1187.7 us)
Async XLA Ops:
  7.2 155.6 %all-gather.20.cloned.1.call-start = ((), (), s32[]{:S(2)}) async-start(), calls=%async_computation.21 | async-start | bytes 1622016 | tf_op jit(solution)/shard_map/all_gather | solution.py:165
  7.9 164.4 %all-gather.22.cloned.1.call-start = ((), (), s32[]{:S(2)}) async-start(), calls=%async_computation.22 | async-start | bytes 1216512 | tf_op jit(solution)/shard_map/all_gather | solution.py:170
  8.7 219.6 %all-gather.26.cloned.1.call-start = ((), (), s32[]{:S(2)}) async-start(), calls=%async_computation.24 | async-start | bytes 1216512 | tf_op jit(solution)/shard_map/all_gather | solution.py:169
  9.4 274.6 %all-gather.16.cloned.1.call-start = ((), (), s32[]{:S(2)}) async-start(), calls=%async_computation.19 | async-start | bytes 1216512 | tf_op jit(solution)/shard_map/all_gather | solution.py:158
  10.0 329.8 %all-gather.12.cloned.1.call-start = ((), (), s32[]{:S(2)}) async-start(), calls=%async_computation.17 | async-start | bytes 1216512 | tf_op jit(solution)/shard_map/all_gather | solution.py:159
  10.6 384.9 %all-gather.14.cloned.1.call-start = ((), (), s32[]{:S(2)}) async-start(), calls=%async_computation.18 | async-start | bytes 1216512 | tf_op jit(solution)/shard_map/all_gather | solution.py:156
  11.2 467.8 %all-gather.18.cloned.1.call-start = ((), (), s32[]{:S(2)}) async-start(), calls=%async_computation.20 | async-start | bytes 1216512 | tf_op jit(solution)/shard_map/all_gather | solution.py:161
  16.2 13.7 all-to-all-start.2
  29.8 9.8 all-to-all-start.1
  39.7 191.3 %all-to-all-start = ((bf16[8,8,40,768]{3,1,2,0:T(8,128)(2,1)}), bf16[8,8,40,768]{3,1,2,0:T(8,128)(2,1)}, u32[]{:S(2)}, u32[]{:S(2)}) async-start(bf16[8,8,40,768]{3,1,2,0:T(8,128)(2,1)} %bitcast.230), calls=%async_computation | async-start | bytes 7864320 | tf_op jit(solution)/shard_map/all_to_all | solution.py:210
  44.2 463.1 %all-gather.24.cloned.1.call-start = ((), (), s32[]{:S(2)}) async-start(), calls=%async_computation.23 | async-start | bytes 1216512 | tf_op jit(solution)/shard_map/all_gather | solution.py:167
  45.0 674.7 %all-gather.28.cloned.1.call-start = ((), (), s32[]{:S(2)}) async-start(), calls=%async_computation.25 | async-start | bytes 1216512 | tf_op jit(solution)/shard_map/all_gather | solution.py:172
  45.7 796.0 %all-gather.30.cloned.1.call-start = ((), (), s32[]{:S(2)}) async-start(), calls=%async_computation.26 | async-start | bytes 4866048 | tf_op jit(solution)/shard_map/all_gather | solution.py:176
  156.6 333.1 %copy-start.51 = (f32[768]{0:T(1024)}, f32[768]{0:T(1024)S(1)}, u32[]{:S(2)}) copy-start(f32[768]{0:T(1024)S(1)} %convert_element_type.291) | copy-start | bytes 9220
  157.2 332.5 %copy-start.61 = (f32[768]{0:T(1024)}, f32[768]{0:T(1024)S(1)}, u32[]{:S(2)}) copy-start(f32[768]{0:T(1024)S(1)} %convert_element_type.292) | copy-start | bytes 9220
  517.1 202.6 %copy-start.62 = (f32[768]{0:T(1024)S(1)}, f32[768]{0:T(1024)}, u32[]{:S(2)}) copy-start(f32[768]{0:T(1024)} %copy-done.61) | copy-start | bytes 9220
  517.1 202.6 %copy-start.74 = (f32[768]{0:T(1024)S(1)}, f32[768]{0:T(1024)}, u32[]{:S(2)}) copy-start(f32[768]{0:T(1024)} %convert_element_type.301) | copy-start | bytes 9220
  734.9 102.5 %all-to-all-start.3 = ((bf16[8,8,40,768]{3,2,1,0:T(8,128)(2,1)}), bf16[8,8,40,768]{3,2,1,0:T(8,128)(2,1)}, u32[]{:S(2)}, u32[]{:S(2)}) async-start(bf16[8,8,40,768]{3,2,1,0:T(8,128)(2,1)} %bitcast.231), calls=%async_computation.3 | async-start | bytes 7864320 | tf_op jit(solution)/shard_map/all_to_all | solution.py:277
  739.6 147.7 %all-gather.32.cloned.1.call-start = ((), (), s32[]{:S(2)}) async-start(), calls=%async_computation.27 | async-start | bytes 4866048 | tf_op jit(solution)/shard_map/all_gather | solution.py:178
  945.4 91.7 %all-to-all-start.4 = ((bf16[8,8,40,768]{3,2,1,0:T(8,128)(2,1)}), bf16[8,8,40,768]{3,2,1,0:T(8,128)(2,1)}, u32[]{:S(2)}, u32[]{:S(2)}) async-start(bf16[8,8,40,768]{3,2,1,0:T(8,128)(2,1)} %copy.167), calls=%async_computation.4 | async-start | bytes 7864320 | tf_op jit(solution)/shard_map/all_to_all | solution.py:341
  950.0 1073.9 %reduce-scatter.28.cloned.1.call-start = ((), (), s32[]{:S(2)}) async-start(), calls=%async_computation.35 | async-start | bytes 2433024 | tf_op jit(solution)/shard_map/reduce_scatter | solution.py:481
  1063.0 960.9 %reduce-scatter.22.cloned.1.call-start = ((), (), s32[]{:S(2)}) async-start(), calls=%async_computation.32 | async-start | bytes 2433024 | tf_op jit(solution)/shard_map/reduce_scatter | solution.py:476
  1597.8 426.1 %reduce-scatter.26.cloned.1.call-start = ((), (), s32[]{:S(2)}) async-start(), calls=%async_computation.34 | async-start | bytes 2433024 | tf_op jit(solution)/shard_map/reduce_scatter | solution.py:479
  1604.3 419.7 %reduce-scatter.24.cloned.1.call-start = ((), (), s32[]{:S(2)}) async-start(), calls=%async_computation.33 | async-start | bytes 2433024 | tf_op jit(solution)/shard_map/reduce_scatter | solution.py:478
  1622.2 405.3 %reduce-scatter.20.cloned.1.call-start = ((), (), s32[]{:S(2)}) async-start(), calls=%async_computation.31 | async-start | bytes 2433024 | tf_op jit(solution)/shard_map/reduce_scatter | solution.py:470
  1662.5 469.5 %reduce-scatter.16.cloned.1.call-start = ((), (), s32[]{:S(2)}) async-start(), calls=%async_computation.29 | async-start | bytes 2433024 | tf_op jit(solution)/shard_map/reduce_scatter | solution.py:467
  1740.3 495.5 %reduce-scatter.14.cloned.1.call-start = ((), (), s32[]{:S(2)}) async-start(), calls=%async_computation.28 | async-start | bytes 2433024 | tf_op jit(solution)/shard_map/reduce_scatter | solution.py:465
  1783.1 557.5 %reduce-scatter.18.cloned.1.call-start = ((), (), s32[]{:S(2)}) async-start(), calls=%async_computation.30 | async-start | bytes 2433024 | tf_op jit(solution)/shard_map/reduce_scatter | solution.py:468
  1829.2 617.9 %reduce-scatter.34.cloned.1.call-start = ((), (), s32[]{:S(2)}) async-start(), calls=%async_computation.38 | async-start | bytes 3244032
  1838.6 749.4 %reduce-scatter.32.cloned.1.call-start = ((), (), s32[]{:S(2)}) async-start(), calls=%async_computation.37 | async-start | bytes 9732096 | tf_op jit(solution)/shard_map/reduce_scatter | solution.py:487
  1850.5 879.8 %reduce-scatter.30.cloned.1.call-start = ((), (), s32[]{:S(2)}) async-start(), calls=%async_computation.36 | async-start | bytes 9732096 | tf_op jit(solution)/shard_map/reduce_scatter | solution.py:485
  1891.0 128.5 %all-to-all-start.5 = ((bf16[8,8,40,768]{3,2,1,0:T(8,128)(2,1)}), bf16[8,8,40,768]{3,2,1,0:T(8,128)(2,1)}, u32[]{:S(2)}, u32[]{:S(2)}) async-start(bf16[8,8,40,768]{3,2,1,0:T(8,128)(2,1)} %bitcast.242), calls=%async_computation.5 | async-start | bytes 7864320 | tf_op jit(solution)/shard_map/all_to_all | solution.py:445
  (128 other events, 2659.7 us)
Sparse Core Ops, SparseCore 0:
  10.9 105.7 all-gather.19
  119.6 52.7 all-gather.21
  175.3 52.9 all-gather.25
  231.0 52.9 all-gather.15
  286.8 52.9 all-gather.11
  342.5 52.9 all-gather.13
  398.4 52.9 all-gather.17
  454.3 52.9 all-gather.23
  510.2 52.9 all-gather.27
  566.0 62.5 all-gather.29
  743.3 118.4 all-gather.31
  1063.1 98.0 reduce-scatter.27
  1597.9 98.3 reduce-scatter.21
  1702.0 98.0 reduce-scatter.25
  1806.7 98.3 reduce-scatter.23
  1910.8 116.6 reduce-scatter.19
  2034.1 97.8 reduce-scatter.15
  2137.7 98.0 reduce-scatter.13
  2242.6 98.0 reduce-scatter.17
  2346.5 100.5 reduce-scatter.33
  2453.6 134.3 reduce-scatter.31
  2595.5 134.7 reduce-scatter.29
where the time goes:
time: 2750 us; the launch traced here: 2740 us
  waiting for transfers between devices  1100 us (40%)
  matrix products  619 us (23%)
  local copies, waits for them, and re-layouts  580 us (21%)
  blocking collectives  210 us (8%)
  other arithmetic  185 us (7%)
  starting transfers between devices  30.1 us (1%)
    unnamed x2, blocking collectives  210 us
    reduce_scatter x1, waiting for transfers between devices, on_device(): lax.psum_scatter(grad_widen, ('dp', 'fsdp'), scatter_dimension=0, tiled=T...  142 us
    reduce_scatter x1, waiting for transfers between devices, on_device(): lax.psum_scatter(grad_narrow, ('dp', 'fsdp'), scatter_dimension=0, tiled=...  141 us
    dot_general x13, matrix products, product(): return jnp.dot(left, right, preferred_element_type=jnp.float32)  114 us
    unnamed x23, waiting for transfers between devices  114 us
    reduce_scatter x1, waiting for transfers between devices, on_device(): lax.psum_scatter(term_svalue, ('dp', 'fsdp'), scatter_dimension=0, tiled=...  105 us
    reduce_scatter x1, waiting for transfers between devices, on_device(): lax.psum_scatter(self_key_gradient_term, ('dp', 'fsdp'), scatter_dimensio...  104 us
    reduce_scatter x1, waiting for transfers between devices, on_device(): lax.psum_scatter(term_squery, ('dp', 'fsdp'), scatter_dimension=0, tiled=...  104 us
  transfers between devices with their start and end apart: 28, of which 17 were waited for; matrix products, arithmetic and copies ran while one was open for 47% of the time, Pallas kernels for 0%

commit v1 on v0

v1 whole, which is shorter than its diff:
```python
import functools

import jax
import jax.numpy as jnp
from jax import lax
from jax.experimental import pallas as pl
from jax.experimental.pallas import tpu as pltpu
from jax.sharding import PartitionSpec as P

HEADS = 12
AXES = ("dp", "fsdp")
BF = jnp.bfloat16
F32 = jnp.float32
norm_eps = 1e-06
mask_fill = -1000000000.0

WINDOWS = ((0, 0), (128, 64), (384, 0), (512, 64))

ERFC_POLE = 0.3
ERFC_POLY = (
    0.16918935391840687,
    0.17069093065701252,
    0.14852123834149009,
    0.214181489197379,
    -0.09282620690981414,
    0.5449671942862269,
    -0.5097726086693966,
    0.4843018450108595,
    -0.12925324449453648,
)
INV_SQRT2 = 0.7071067811865476
INV_SQRT2PI = 0.3989422804014327


def nn(left, right):
    return lax.dot_general(left, right, (((1,), (0,)), ((), ())), preferred_element_type=F32)


def nt(left, right):
    return lax.dot_general(left, right, (((1,), (1,)), ((), ())), preferred_element_type=F32)


def tn(left, right):
    return lax.dot_general(left, right, (((0,), (0,)), ((), ())), preferred_element_type=F32)


def norm_parts(value):
    mean = jnp.mean(value, -1, keepdims=True)
    centred = value - mean
    spread = jnp.mean(centred * centred, -1, keepdims=True)
    inv = lax.rsqrt(spread + norm_eps)
    return centred * inv, inv


def norm_back(grad, gain, xhat, inv):
    scaled = grad * gain
    first = jnp.mean(scaled, -1, keepdims=True)
    second = jnp.mean(scaled * xhat, -1, keepdims=True)
    return inv * (scaled - first - xhat * second)


def gelu_parts(v):
    z = jnp.abs(v) * INV_SQRT2
    t = 1.0 / (1.0 + ERFC_POLE * z)
    poly = jnp.full_like(t, ERFC_POLY[-1])
    for c in ERFC_POLY[-2::-1]:
        poly = poly * t + c
    bell = jnp.exp(-0.5 * (v * v))
    half = (0.5 * bell) * (t * poly)
    cdf = jnp.where(v >= 0, 1.0 - half, half)
    return v * cdf, cdf + (v * INV_SQRT2PI) * bell


def stack_heads(full, index):
    base, off = WINDOWS[index]
    win = full[:, base : base + 256]
    lane = lax.broadcasted_iota(jnp.int32, win.shape, 1)
    blocks = []
    for h in range(3):
        lo = off + 64 * h
        blocks.append(jnp.where((lane >= lo) & (lane < lo + 64), win, 0.0))
    return jnp.concatenate(blocks, 0).astype(BF)


def unstack_heads(stacked, index, rows):
    _, off = WINDOWS[index]
    lane = lax.broadcasted_iota(jnp.int32, (rows, 256), 1)
    out = None
    for h in range(3):
        lo = off + 64 * h
        part = jnp.where((lane >= lo) & (lane < lo + 64), stacked[rows * h : rows * (h + 1)], 0.0)
        out = part if out is None else out + part
    return out


def join_windows(parts):
    a, b, c, d = parts
    return jnp.concatenate(
        [
            a[:, :128],
            a[:, 128:] + b[:, :128],
            b[:, 128:],
            c[:, :128],
            c[:, 128:] + d[:, :128],
            d[:, 128:],
        ],
        1,
    )


def self_forward(
    tok, bias, wq, wk, wv, wo, wc, qb, vb, ob, g1, b1, pb, q_o, k_o, v_o, p_o, att_o, u1_o, f_o, pr_o, att_s
):
    rb, length, width = tok.shape
    n = rb * length
    x32 = tok[...].astype(F32).reshape(n, width)
    x = x32.astype(BF)
    q = (nn(x, wq[...]) + qb[...]).astype(BF)
    k = nn(x, wk[...]).astype(BF)
    v = (nn(x, wv[...]) + vb[...]).astype(BF)
    q_o[...] = q.astype(F32).reshape(rb, length, width).astype(BF)
    k_o[...] = k.astype(F32).reshape(rb, length, width).astype(BF)
    v_o[...] = v.astype(F32).reshape(rb, length, width).astype(BF)

    def row(r, carry):
        qr = q_o[r].astype(F32) * 0.125
        kr = k_o[r].astype(F32)
        vr = v_o[r].astype(F32)
        outs = []
        for i in range(4):
            base = WINDOWS[i][0]
            qs = stack_heads(qr, i)
            kw = kr[:, base : base + 256].astype(BF)
            vw = vr[:, base : base + 256].astype(BF)
            st = nt(kw, qs) + bias[r]
            top = jnp.max(st, 0, keepdims=True)
            e = jnp.exp(st - top)
            p = (e * (1.0 / jnp.sum(e, 0, keepdims=True))).astype(BF)
            p_o[r, i] = p
            outs.append(unstack_heads(tn(p, vw), i, length))
        att_s[r] = join_windows(outs)
        return carry

    lax.fori_loop(0, rb, row, 0)
    att32 = att_s[...]
    att_o[...] = att32.astype(BF)
    att = att32.reshape(n, width).astype(BF)
    u1 = x32 + nn(att, wo[...]) + ob[...]
    u1_o[...] = u1.reshape(rb, length, width)
    xhat, _ = norm_parts(u1)
    first = (xhat * g1[...] + b1[...]).astype(BF)
    f_o[...] = first.astype(F32).reshape(rb, length, width).astype(BF)
    pr_o[...] = (nn(first, wc[...]) + pb[...]).reshape(rb, length, width).astype(BF)


def cross_forward(starts, order, proj, wk, wv, cb, probe, k_o, v_o, p_o, mix_o, pr_s):
    i = pl.program_id(0)
    points = proj.shape[1]
    padded = k_o.shape[1]
    length = probe.shape[1]

    @pl.when(i == 0)
    def _():
        pr_s[...] = jnp.zeros_like(pr_s)

    lo, hi = starts[i], starts[i + 1]

    @pl.when(hi > lo)
    def _():
        pr_s[0:points, :] = proj[0]
        pr = pr_s[...]
        k_o[0] = nn(pr, wk[...]).astype(BF)
        v_o[0] = (nn(pr, wv[...]) + cb[...]).astype(BF)

        def row(j, carry):
            r = order[j]
            qr = probe[r].astype(F32) * 0.125
            outs = []
            for g in range(4):
                base = WINDOWS[g][0]
                qs = stack_heads(qr, g)
                st = nt(k_o[0, :, base : base + 256], qs)
                point = lax.broadcasted_iota(jnp.int32, st.shape, 0)
                st = jnp.where(point < points, st, -1e30)
                top = jnp.max(st, 0, keepdims=True)
                e = jnp.exp(st - top)
                p = (e * (1.0 / jnp.sum(e, 0, keepdims=True))).astype(BF)
                p_o[r, g] = p
                outs.append(unstack_heads(tn(p, v_o[0, :, base : base + 256]), g, length))
            mix_o[r] = join_windows(outs).astype(BF)
            return carry

        lax.fori_loop(lo, hi, row, 0)


def tail_kernel(
    u1, mix, og, wco, w1, w2, g1, b1, cb, g2, s2, wb, nb, g3, s3,
    out_o, act_o, gi_o, sec_o, gb3_o, gm_o, gb2_o, gc_o, vec_o, wbg_o,
    act_s, gp_s, acc_s,
):
    step = pl.program_id(0)
    rb, length, width = u1.shape
    n = rb * length
    chunks = w1.shape[0]

    @pl.when(step == 0)
    def _():
        vec_o[...] = jnp.zeros_like(vec_o)
        wbg_o[...] = jnp.zeros_like(wbg_o)

    def flat(ref):
        return ref[...].astype(F32).reshape(n, width)

    def fold(value):
        return value.reshape(rb, length, width)

    xhat1, _ = norm_parts(flat(u1))
    first = xhat1 * g1[...] + b1[...]
    u2 = first + nn(flat(mix).astype(BF), wco[...]) + cb[...]
    xhat2, inv2 = norm_parts(u2)
    second = (xhat2 * g2[...] + s2[...]).astype(BF)
    sec32 = second.astype(F32)
    sec_o[...] = fold(sec32).astype(BF)
    acc_s[...] = sec32 + nb[...]

    def up(c, carry):
        inner = nn(second, w1[c]) + wb[c]
        act, slope = gelu_parts(inner)
        act = act.astype(BF)
        gp_s[c] = slope
        act_o[c] = act
        acc_s[...] += nn(act, w2[c])
        return carry

    lax.fori_loop(0, chunks, up, 0)
    xhat3, inv3 = norm_parts(acc_s[...])
    out_o[...] = fold(xhat3 * g3[...] + s3[...]).astype(BF)
    y = flat(og)
    grad_summed = norm_back(y, g3[...], xhat3, inv3)
    gb3 = grad_summed.astype(BF)
    gb3f = gb3.astype(F32)
    gb3_o[...] = fold(gb3f).astype(BF)
    vec_o[0:1] += jnp.sum(y * xhat3, 0, keepdims=True)
    vec_o[1:2] += jnp.sum(y, 0, keepdims=True)
    vec_o[2:3] += jnp.sum(gb3f, 0, keepdims=True)
    acc_s[...] = grad_summed

    def down(c, carry):
        gi = (nt(gb3, w2[c]) * gp_s[c]).astype(BF)
        gi_o[c] = gi
        wbg_o[c] += jnp.sum(gi.astype(F32), 0, keepdims=True)
        acc_s[...] += nt(gi, w1[c])
        return carry

    lax.fori_loop(0, chunks, down, 0)
    y2 = acc_s[...].astype(BF).astype(F32)
    gm = norm_back(y2, g2[...], xhat2, inv2)
    gm_o[...] = fold(gm)
    gb2 = gm.astype(BF)
    gb2f = gb2.astype(F32)
    gb2_o[...] = fold(gb2f).astype(BF)
    vec_o[3:4] += jnp.sum(y2 * xhat2, 0, keepdims=True)
    vec_o[4:5] += jnp.sum(y2, 0, keepdims=True)
    vec_o[5:6] += jnp.sum(gb2f, 0, keepdims=True)
    gc_o[...] = fold(nt(gb2, wco[...])).astype(BF)


def cross_backward(
    starts, order, proj, keys, values, wk, wv, probe, grad, probs,
    dpr_o, dproj_o, dwk_o, dwv_o, dcb_o,
    pr_s, dk_s, dv_s, dwk_s, dwv_s,
):
    i = pl.program_id(0)
    points = proj.shape[1]
    length = probe.shape[1]

    @pl.when(i == 0)
    def _():
        pr_s[...] = jnp.zeros_like(pr_s)
        dwk_s[...] = jnp.zeros_like(dwk_s)
        dwv_s[...] = jnp.zeros_like(dwv_s)
        dcb_o[...] = jnp.zeros_like(dcb_o)

    lo, hi = starts[i], starts[i + 1]

    @pl.when(hi == lo)
    def _():
        dproj_o[...] = jnp.zeros_like(dproj_o)

    @pl.when(hi > lo)
    def _():
        dk_s[...] = jnp.zeros_like(dk_s)
        dv_s[...] = jnp.zeros_like(dv_s)

        def row(j, carry):
            r = order[j]
            qr = probe[r].astype(F32) * 0.125
            gr = grad[r].astype(F32)
            outs = []
            for g in range(4):
                base = WINDOWS[g][0]
                qs = stack_heads(qr, g)
                gs = stack_heads(gr, g)
                pb = probs[r, g]
                p = pb.astype(F32)
                dp = nt(values[0, :, base : base + 256], gs)
                w = jnp.sum(dp * p, 0, keepdims=True)
                ds = (p * (dp - w)).astype(BF)
                dk_s[:, base : base + 256] += nn(ds, qs)
                dv_s[:, base : base + 256] += nn(pb, gs)
                outs.append(unstack_heads(tn(ds, keys[0, :, base : base + 256]), g, length))
            dpr_o[r] = (join_windows(outs) * 0.125).astype(BF)
            return carry

        lax.fori_loop(lo, hi, row, 0)
        pr_s[0:points, :] = proj[0]
        pr = pr_s[...]
        dk = dk_s[...].astype(BF)
        dv = dv_s[...].astype(BF)
        dcb_o[0:1] += jnp.sum(dv.astype(F32), 0, keepdims=True)
        dproj = (nt(dk, wk[...]) + nt(dv, wv[...])).astype(BF)
        dproj_o[0] = dproj[0:points]
        dwk_s[...] += tn(pr, dk)
        dwv_s[...] += tn(pr, dv)

    @pl.when(i == pl.num_programs(0) - 1)
    def _():
        dwk_o[...] = dwk_s[...].astype(BF)
        dwv_o[...] = dwv_s[...].astype(BF)


def self_backward(
    gm, dpr, u1, q, k, v, probs, wq, wk, wv, wo, wc, g1,
    gb1_o, dq_o, dk_o, dv_o, tg_o, vec_o,
    ga_s, dq_s, dk_s, dv_s,
):
    step = pl.program_id(0)
    rb, length, width = u1.shape
    n = rb * length

    @pl.when(step == 0)
    def _():
        vec_o[...] = jnp.zeros_like(vec_o)

    def flat(ref):
        return ref[...].astype(F32).reshape(n, width)

    def fold(value):
        return value.reshape(rb, length, width)

    dpr32 = flat(dpr)
    grad_first = flat(gm) + nt(dpr32.astype(BF), wc[...])
    xhat, inv = norm_parts(flat(u1))
    low = norm_back(grad_first, g1[...], xhat, inv)
    gb1 = low.astype(BF)
    gb1f = gb1.astype(F32)
    gb1_o[...] = fold(gb1f).astype(BF)
    vec_o[0:1] += jnp.sum(grad_first * xhat, 0, keepdims=True)
    vec_o[1:2] += jnp.sum(grad_first, 0, keepdims=True)
    vec_o[2:3] += jnp.sum(gb1f, 0, keepdims=True)
    vec_o[3:4] += jnp.sum(dpr32, 0, keepdims=True)
    ga_s[...] = fold(nt(gb1, wo[...]).astype(BF).astype(F32))

    def row(r, carry):
        qr = q[r].astype(F32) * 0.125
        kr = k[r].astype(F32)
        vr = v[r].astype(F32)
        gr = ga_s[r]
        dqs, dks, dvs = [], [], []
        for i in range(4):
            base = WINDOWS[i][0]
            qs = stack_heads(qr, i)
            gs = stack_heads(gr, i)
            kw = kr[:, base : base + 256].astype(BF)
            vw = vr[:, base : base + 256].astype(BF)
            pb = probs[r, i]
            p = pb.astype(F32)
            dp = nt(vw, gs)
            w = jnp.sum(dp * p, 0, keepdims=True)
            ds = (p * (dp - w)).astype(BF)
            dks.append(nn(ds, qs))
            dvs.append(nn(pb, gs))
            dqs.append(unstack_heads(tn(ds, kw), i, length))
        dq_s[r] = join_windows(dqs) * 0.125
        dk_s[r] = join_windows(dks)
        dv_s[r] = join_windows(dvs)
        return carry

    lax.fori_loop(0, rb, row, 0)
    dq = dq_s[...].reshape(n, width).astype(BF)
    dk = dk_s[...].reshape(n, width).astype(BF)
    dv = dv_s[...].reshape(n, width).astype(BF)
    dq_o[...] = dq_s[...].astype(BF)
    dk_o[...] = dk_s[...].astype(BF)
    dv_o[...] = dv_s[...].astype(BF)
    vec_o[4:5] += jnp.sum(dq.astype(F32), 0, keepdims=True)
    vec_o[5:6] += jnp.sum(dv.astype(F32), 0, keepdims=True)
    total = low + nt(dq, wq[...]) + nt(dk, wk[...]) + nt(dv, wv[...])
    tg_o[...] = fold(total).astype(BF)


def sds(shape, dtype):
    return jax.ShapeDtypeStruct(shape, dtype)


def whole(shape, *, single=True):
    zeros = (0,) * len(shape)
    mode = pl.Buffered(1) if single else None
    return pl.BlockSpec(shape, lambda i, *_: zeros, pipeline_mode=mode)


def rows_block(shape, rb):
    rest = tuple(shape[1:])
    return pl.BlockSpec((rb,) + rest, lambda i, *_: (i,) + (0,) * len(rest))


def params(mib):
    return pltpu.CompilerParams(
        dimension_semantics=("arbitrary",), vmem_limit_bytes=mib * 1024 * 1024
    )


def cost(flops, bytes_accessed):
    return pl.CostEstimate(flops=int(flops), bytes_accessed=int(bytes_accessed), transcendentals=0)


def gather(value, axis):
    return lax.all_gather(value, AXES, axis=axis, tiled=True)


def on_device(
    tokens, patches, segments, owner, image_slot, out_grad,
    self_query, query_bias, self_key, self_value, value_bias, self_output, output_bias,
    first_gain, first_norm_bias, patch_proj, patch_bias, cross_query, probe_bias, cross_key,
    cross_value, content_bias, cross_output, cross_bias, second_gain, second_shift,
    widen_weight, widen_bias, narrow_weight, narrow_bias, third_gain, third_shift,
):
    rows, length, width = tokens.shape
    images, points, pwidth = patches.shape
    groups = lax.axis_size("dp")
    shards = groups * lax.axis_size("fsdp")
    total_images = groups * images
    hidden = widen_weight.shape[1]
    chunks = hidden // width
    sr = self_query.shape[0]
    wr = widen_bias.shape[0]

    vec_list = (
        query_bias, value_bias, output_bias, first_gain, first_norm_bias, patch_bias, probe_bias,
        content_bias, cross_bias, second_gain, second_shift, narrow_bias, third_gain, third_shift,
    )
    packed = jnp.concatenate(vec_list + (widen_bias,))
    packed = jnp.pad(packed, (0, width - packed.shape[0]))[None]
    packed_all = gather(jnp.pad(packed, ((0, 7), (0, 0))), 0).reshape(shards, 8, width)[:, 0].astype(F32)
    vecs = [packed_all[:, sr * j : sr * (j + 1)].reshape(1, width) for j in range(len(vec_list))]
    (qb, vb, ob, g1, b1, pab, prb, cob, crb, g2, s2, nab, g3, s3) = vecs
    wb = packed_all[:, sr * len(vec_list) : sr * len(vec_list) + wr]
    wb = wb.reshape(shards, chunks, sr).transpose(1, 0, 2).reshape(chunks, 1, width)

    patch_full = gather(patch_proj, 0)
    w_a = gather(
        jnp.stack([self_query, self_key, self_value, self_output, cross_query, cross_key, cross_value, cross_output]), 1
    )
    widen_slabs = widen_weight.reshape(sr, shards, chunks, sr).transpose(2, 0, 1, 3).reshape(chunks, sr, width)
    narrow_slabs = narrow_weight.reshape(chunks, sr, width)
    w_b = gather(jnp.concatenate([widen_slabs, narrow_slabs], 0), 1)

    projected = (
        lax.dot_general(patches, patch_full, (((2,), (0,)), ((), ())), preferred_element_type=F32) + pab
    ).astype(BF)
    proj_all = lax.all_gather(projected, "dp", axis=0, tiled=True)

    image = owner * images + image_slot
    idx = jnp.arange(rows, dtype=jnp.int32)
    before = (image[None, :] < image[:, None]) | ((image[None, :] == image[:, None]) & (idx[None, :] < idx[:, None]))
    rank = jnp.sum(before.astype(jnp.int32), 1)
    order = jnp.sum(jnp.where(rank[:, None] == idx[None, :], idx[:, None], 0), 0).astype(jnp.int32)
    starts = jnp.sum((image[None, :] < jnp.arange(total_images + 1, dtype=jnp.int32)[:, None]).astype(jnp.int32), 1)

    same = segments[:, :, None] == segments[:, None, :]
    bias = jnp.where(same, 0.0, mask_fill).astype(F32)
    bias = jnp.concatenate([bias, bias, bias], 2)

    rb = 8 if rows % 8 == 0 else 1
    grid = (rows // rb,)
    tok_sh = (rows, length, width)
    slab = (width, width)

    def wspec(j):
        return pl.BlockSpec((None, width, width), lambda i, *_: (j, 0, 0), pipeline_mode=pl.Buffered(1))

    vspec = whole((1, width))
    tb = rows_block(tok_sh, rb)
    self_p = (rows, 4, length, 3 * length)
    q, k, v, probs, attended, u1, first_low, probe = pl.pallas_call(
        self_forward,
        grid=grid,
        in_specs=[tb, rows_block((rows, length, 3 * length), rb)]
        + [wspec(0), wspec(1), wspec(2), wspec(3), wspec(4)]
        + [vspec] * 6,
        out_specs=[tb, tb, tb, rows_block(self_p, rb), tb, tb, tb, tb],
        out_shape=[
            sds(tok_sh, BF), sds(tok_sh, BF), sds(tok_sh, BF), sds(self_p, BF),
            sds(tok_sh, BF), sds(tok_sh, F32), sds(tok_sh, BF), sds(tok_sh, BF),
        ],
        scratch_shapes=[pltpu.VMEM((rb, length, width), F32)],
        compiler_params=params(48),
        cost_estimate=cost(11 * rows * length * width * width, 30e6),
        name="self_forward",
    )(tokens, bias, w_a, w_a, w_a, w_a, w_a, qb, vb, ob, g1, b1, prb)

    padded = -(-points // 16) * 16
    kv_sh = (total_images, padded, width)
    cross_p = (rows, 4, padded, 3 * length)
    img_spec = pl.BlockSpec((1, points, width), lambda i, *_: (i, 0, 0))
    kv_spec = pl.BlockSpec((1, padded, width), lambda i, *_: (i, 0, 0))
    image_keys, image_values, cprobs, mixed = pl.pallas_call(
        cross_forward,
        grid_spec=pltpu.PrefetchScalarGridSpec(
            num_scalar_prefetch=2,
            grid=(total_images,),
            in_specs=[img_spec, wspec(5), wspec(6), vspec, whole(tok_sh)],
            out_specs=[kv_spec, kv_spec, whole(cross_p), whole(tok_sh)],
            scratch_shapes=[pltpu.VMEM((padded, width), BF)],
        ),
        out_shape=[sds(kv_sh, BF), sds(kv_sh, BF), sds(cross_p, BF), sds(tok_sh, BF)],
        compiler_params=params(48),
        cost_estimate=cost(4 * total_images * points * width * width, 40e6),
        name="cross_forward",
    )(starts, order, proj_all, w_a, w_a, cob, probe)

    def chunk_w(j):
        return pl.BlockSpec((chunks, width, width), lambda i, *_: (j, 0, 0), pipeline_mode=pl.Buffered(1))

    n_tok = rows * length
    hid_sh = (chunks, n_tok, width)
    hid_spec = pl.BlockSpec((chunks, rb * length, width), lambda i, *_: (0, i, 0))
    (output, active, grad_inner, second, gb3, grad_mid, gb2, grad_crossed, vec_t, wb_grad) = pl.pallas_call(
        tail_kernel,
        grid=grid,
        in_specs=[tb, tb, tb, wspec(7), chunk_w(0), chunk_w(1)]
        + [vspec] * 5
        + [whole((chunks, 1, width))]
        + [vspec] * 3,
        out_specs=[tb, hid_spec, hid_spec, tb, tb, tb, tb, tb, whole((8, width)), whole((chunks, 1, width))],
        out_shape=[
            sds(tok_sh, BF), sds(hid_sh, BF), sds(hid_sh, BF), sds(tok_sh, BF), sds(tok_sh, BF),
            sds(tok_sh, F32), sds(tok_sh, BF), sds(tok_sh, BF), sds((8, width), F32), sds((chunks, 1, width), F32),
        ],
        scratch_shapes=[
            pltpu.VMEM((8, 128), BF),
            pltpu.VMEM((chunks, rb * length, width), F32),
            pltpu.VMEM((rb * length, width), F32),
        ],
        compiler_params=params(56),
        cost_estimate=cost(18 * n_tok * width * width + 8 * n_tok * width * hidden, 50e6),
        name="tail",
    )(u1, mixed, out_grad, w_a, w_b, w_b, g1, b1, crb, g2, s2, wb, nab, g3, s3)

    dprobe, dproj, dwk, dwv, dcb = pl.pallas_call(
        cross_backward,
        grid_spec=pltpu.PrefetchScalarGridSpec(
            num_scalar_prefetch=2,
            grid=(total_images,),
            in_specs=[img_spec, kv_spec, kv_spec, wspec(5), wspec(6), whole(tok_sh), whole(tok_sh), whole(cross_p)],
            out_specs=[whole(tok_sh), img_spec, whole(slab), whole(slab), whole((8, width))],
            scratch_shapes=[
                pltpu.VMEM((padded, width), BF),
                pltpu.VMEM((padded, width), F32),
                pltpu.VMEM((padded, width), F32),
                pltpu.VMEM((width, width), F32),
                pltpu.VMEM((width, width), F32),
            ],
        ),
        out_shape=[sds(tok_sh, BF), sds((total_images, points, width), BF), sds(slab, BF), sds(slab, BF), sds((8, width), F32)],
        compiler_params=params(52),
        cost_estimate=cost(8 * total_images * points * width * width, 50e6),
        name="cross_backward",
    )(starts, order, proj_all, image_keys, image_values, w_a, w_a, probe, grad_crossed, cprobs)
    grad_projected = lax.psum_scatter(dproj, "dp", scatter_dimension=0, tiled=True)

    gb1, dq, dk, dv, tokens_grad, vec_s = pl.pallas_call(
        self_backward,
        grid=grid,
        in_specs=[tb, tb, tb, tb, tb, tb, rows_block(self_p, rb)]
        + [wspec(0), wspec(1), wspec(2), wspec(3), wspec(4)]
        + [vspec],
        out_specs=[tb, tb, tb, tb, tb, whole((8, width))],
        out_shape=[sds(tok_sh, BF)] * 5 + [sds((8, width), F32)],
        scratch_shapes=[pltpu.VMEM((rb, length, width), F32)] * 4,
        compiler_params=params(52),
        cost_estimate=cost(14 * n_tok * width * width, 40e6),
        name="self_backward",
    )(grad_mid, dprobe, u1, q, k, v, probs, w_a, w_a, w_a, w_a, w_a, g1)

    def wgrad(left, right):
        return tn(left.reshape(n_tok, width), right.reshape(n_tok, width)).astype(BF)

    grad_narrow = lax.dot_general(
        active, gb3.reshape(n_tok, width), (((1,), (0,)), ((), ())), preferred_element_type=F32
    ).astype(BF)
    grad_widen = jnp.stack([wgrad(second, grad_inner[c]) for c in range(chunks)])
    ffn_shard = lax.psum_scatter(
        jnp.concatenate([grad_widen, grad_narrow], 0), AXES, scatter_dimension=1, tiled=True
    ).astype(F32)

    patch_low = grad_projected
    grad_patch_proj = lax.dot_general(
        patches, patch_low, (((0, 1), (0, 1)), ((), ())), preferred_element_type=F32
    ).astype(BF)
    grad_patch_bias = jnp.sum(patch_low.astype(F32), (0, 1))[None]
    patches_grad = lax.dot_general(
        patch_low, patch_full, (((2,), (1,)), ((), ())), preferred_element_type=F32
    ).astype(BF)

    vec_grads = [
        vec_s[4:5], vec_s[5:6], vec_s[2:3], vec_s[0:1], vec_s[1:2], grad_patch_bias, vec_s[3:4], dcb[0:1],
        vec_t[5:6], vec_t[3:4], vec_t[4:5], vec_t[2:3], vec_t[0:1], vec_t[1:2],
    ]
    wb_flat = wb_grad.reshape(chunks, shards, sr).transpose(1, 0, 2).reshape(shards, wr)
    vec_rows = jnp.concatenate([item.reshape(shards, sr) for item in vec_grads] + [wb_flat], 1)
    vec_rows = jnp.pad(vec_rows, ((0, 0), (0, width - vec_rows.shape[1])))
    vec_shard = lax.psum_scatter(vec_rows, AXES, scatter_dimension=0, tiled=True)[0]

    slabs = jnp.stack(
        [
            wgrad(tokens, dq), wgrad(tokens, dk), wgrad(tokens, dv), wgrad(attended, gb1),
            wgrad(first_low, dprobe), dwk, dwv, wgrad(mixed, gb2),
        ]
    )
    slab_shard = lax.psum_scatter(slabs, AXES, scatter_dimension=1, tiled=True).astype(F32)
    patch_shard = lax.psum_scatter(grad_patch_proj, AXES, scatter_dimension=0, tiled=True).astype(F32)

    vg = [vec_shard[sr * j : sr * (j + 1)] for j in range(len(vec_list))]
    wbg = vec_shard[sr * len(vec_list) : sr * len(vec_list) + wr]
    widen_shard = ffn_shard[:chunks].reshape(chunks, sr, shards, sr).transpose(1, 2, 0, 3).reshape(sr, hidden)
    narrow_shard = ffn_shard[chunks:].reshape(chunks * sr, width)
    return (
        output, tokens_grad, patches_grad,
        slab_shard[0], vg[0], slab_shard[1], slab_shard[2], vg[1], slab_shard[3], vg[2], vg[3], vg[4],
        patch_shard, vg[5], slab_shard[4], vg[6], slab_shard[5], slab_shard[6], vg[7], slab_shard[7],
        vg[8], vg[9], vg[10], widen_shard, wbg, narrow_shard, vg[11], vg[12], vg[13],
    )


def solution(mesh):
    three, two, one = P(AXES, None, None), P(AXES, None), P(AXES)
    in_specs = (
        three, three, two, one, one, three,
        two, one, two, two, one, two, one, one, one, two, one, two, one, two,
        two, one, two, one, one, one, two, one, two, one, one, one,
    )
    out_specs = (
        three, three, three,
        two, one, two, two, one, two, one, one, one, two, one, two, one, two, two, one, two,
        one, one, one, two, one, two, one, one, one,
    )
    return jax.shard_map(on_device, mesh=mesh, in_specs=in_specs, out_specs=out_specs, check_vma=False)
```

time: 2750 us -> 1170 us (0.43)
  matrix products: 619 us -> 46 us
  local copies, waits for them, and re-layouts: 580 us -> 76.2 us
  waiting for transfers between devices: 1100 us -> 680 us
  Pallas kernels: 0 us -> 303 us
  other arithmetic: 185 us -> 3.33 us
  blocking collectives: 210 us -> 44.6 us
  starting transfers between devices: 30.1 us -> 0.75 us
    dot_general x77 -> x14, matrix products: 619 us -> 46 us  [the longest x10 30 us: tn(): lax.dot_general(left, right, (((0,), (0,)), ((), ())), preferred_element_...]
    reduce_scatter x10 -> x1, waiting for transfers between devices: 600 us -> 32.9 us  [on_device(): lax.psum_scatter(dproj, 'dp', scatter_dimension=0, tiled=True)]
    unnamed x23 -> x13, waiting for transfers between devices: 114 us -> 491 us
    pallas_call x0 -> x5, Pallas kernels: none -> 303 us  [the longest x1 88 us: on_device(): pl.pallas_call(cross_backward, grid_spec=pltpu.PrefetchScalarGridSpec(num...]
    unnamed x2 -> x0, blocking collectives: 210 us -> none
    all_to_all x6 -> x0, waiting for transfers between devices: 188 us -> none  [the longest x1 95.2 us: on_device(): lax.all_to_all(second.astype(jnp.bfloat16).reshape(groups, capacity, leng...]
    convert_element_type x26 -> x0, local copies, waits for them, and re-layouts: 140 us -> none  [the longest x10 46.1 us: attend(): mixed.reshape(query.shape).astype(jnp.bfloat16)]
    reshape x29 -> x34, local copies, waits for them, and re-layouts: 138 us -> 12.8 us  [the longest x13 4.64 us: on_device(): packed_all[:, sr * j:sr * (j + 1)].reshape(1, width)]
  transfers between devices with their start and end apart: 28 -> 9, of which waited for: 17 -> 8; matrix products, arithmetic and copies ran while one was open for 47% -> 9% of each run, Pallas kernels for 0% -> 13%
where the time goes in v1:
time: 1170 us
  waiting for transfers between devices  680 us (58%)
  Pallas kernels  303 us (26%)
  local copies, waits for them, and re-layouts  76.2 us (7%)
  matrix products  46 us (4%)
  blocking collectives  44.6 us (4%)
  between operations  14.8 us (1%)
    unnamed x13, waiting for transfers between devices  491 us
    all_gather x3, waiting for transfers between devices, gather(): return lax.all_gather(value, AXES, axis=axis, tiled=True)  95.3 us
    pallas_call x1, Pallas kernels, on_device(): pl.pallas_call(cross_backward, grid_spec=pltpu.PrefetchScalarGridSpec(num...  88 us
    pallas_call x1, Pallas kernels, on_device(): pl.pallas_call(tail_kernel, grid=grid, in_specs=[tb, tb, tb, wspec(7), ch...  67.6 us
    all_gather x1, waiting for transfers between devices, on_device(): proj_all = lax.all_gather(projected, 'dp', axis=0, tiled=True)  60.6 us
    pallas_call x1, Pallas kernels, on_device(): pl.pallas_call(cross_forward, grid_spec=pltpu.PrefetchScalarGridSpec(num_...  54.8 us
    pallas_call x1, Pallas kernels, on_device(): pl.pallas_call(self_forward, grid=grid, in_specs=[tb, rows_block((rows, l...  51.9 us
    unnamed x86, local copies, waits for them, and re-layouts  45.3 us
  transfers between devices with their start and end apart: 9, of which 8 were waited for; matrix products, arithmetic and copies ran while one was open for 9% of the time, Pallas kernels for 13%

profile of v1, /device:TPU:0, one launch (start us, length us, event | category | flops | bytes accessed | tf_op | source)
XLA Modules:
  0.0 1168.1 jit_solution(16530459385481091344)
XLA Ops:
  15.0 10.1 concatenate.16
  25.1 44.6 %all_gather.16 = bf16[256,768]{1,0:T(8,128)(2,1)S(1)} all-gather(bf16[8,768]{1,0:T(8,128)(2,1)S(1)} %pad.13), channel_id=1, replica_groups=mesh['dp'=8,'fsdp'=4] {'dp','fsdp'}, dimensions={0}, use_global_device_ids=true | all-gather | bytes 405504 | tf_op jit(solution)/shard_map/all_gather | solution.py:428
  70.0 3.9 add_convert_fusion
  84.1 69.3 %all-gather.5.cloned.1.call-done.wq.wk.wv.wo.wc.wco = bf16[8,768,768]{2,1,0:T(8,128)(2,1)} async-done(((bf16[8,24,768]{2,1,0:T(8,128)(2,1)}), bf16[8,768,768]{2,1,0:T(8,128)(2,1)}) %all-gather.5.cloned.1.call-update) | async-done | bytes 9437200 | tf_op jit(solution)/shard_map/all_gather | solution.py:428
  153.5 51.9 %self_forward.1 = (bf16[32,40,768]{2,1,0:T(8,128)(2,1)S(1)}, bf16[32,40,768]{2,1,0:T(8,128)(2,1)S(1)}, bf16[32,40,768]{2,1,0:T(8,128)(2,1)}, bf16[32,4,40,120]{3...) custom-call(bf16[32,40,768]{2,1,0:T(8,128)(2,1)} %tok.1, ...), custom_call_target="tpu_custom_call" | custom-call | flops 8304721920 | bytes 30000000 | tf_op jit(solution)/shard_map/self_forward/pallas_call | solution.py:495
  208.0 60.6 %all-gather.9.cloned.1.call-done.proj = bf16[32,145,768]{2,1,0:T(8,128)(2,1)} async-done(((bf16[4,145,768]{2,1,0:T(8,128)(2,1)}), bf16[32,145,768]{2,1,0:T(8,128)(2,1)}) %all-gather.9.cloned.1.call-update) | async-done | bytes 7127056 | tf_op jit(solution)/shard_map/all_gather | solution.py:471
  270.1 54.8 %cross_forward.1 = (bf16[32,160,768]{2,1,0:T(8,128)(2,1)}, bf16[32,160,768]{2,1,0:T(8,128)(2,1)}, bf16[32,4,160,120]{3,2,1,0:T(8,128)(2,1)}, bf16[32,40,768]{2,1,0:T(8,128)(2,1)S(1)}) custom-call(s32[33]{0:T(128)S(1)} %convert_reduce_fusion.2.starts, s32[32]{0:T(128)S(1)} %select_reduce_fusion.order, ...), custom_call_target="tpu_custom_call" | custom-call | flops 10947133440 | bytes 40000000 | tf_op jit(solution)/shard_map/cross_forward/pallas_call | solution.py:517
  326.2 26.0 %all-gather.11.cloned.1.call-done.w1.w2 = bf16[8,768,768]{2,1,0:T(8,128)(2,1)} async-done(((bf16[8,24,768]{2,1,0:T(8,128)(2,1)}), bf16[8,768,768]{2,1,0:T(8,128)(2,1)}) %all-gather.11.cloned.1.call-update) | async-done | bytes 9437200 | tf_op jit(solution)/shard_map/all_gather | solution.py:428
  352.2 67.6 %tail.1 = (bf16[32,40,768]{2,1,0:T(8,128)(2,1)}, bf16[4,1280,768]{2,1,0:T(8,128)(2,1)}, bf16[4,1280,768]{2,1,0:T(8,128)(2,1)}, bf16[32,40,768]{2,1,0:T(8,128)(2,...) custom-call(f32[32,40,768]{2,1,0:T(8,128)} %get-tuple-element.62.u1,, ...), custom_call_target="tpu_custom_call" | custom-call | flops 37748736000 | bytes 50000000 | tf_op jit(solution)/shard_map/tail/pallas_call | solution.py:538
  419.9 88.0 %cross_backward.1 = (bf16[32,40,768]{2,1,0:T(8,128)(2,1)}, bf16[32,145,768]{2,1,0:T(8,128)(2,1)}, bf16[768,768]{1,0:T(8,128)(2,1)S(1)}, bf16[768,768]{1,0:T(8,128)(2,1)}, f32[8,768]{1,0:T(8,128)S(1)}) custom-call(s32[33]{0:T(128)S(1)} %convert_reduce_fusion.2.starts, s32[32]{0:T(128)S(1)} %select_reduce_fusion.order, ...), custom_call_target="tpu_custom_call" | custom-call | flops 21894266880 | bytes 50000000 | tf_op jit(solution)/shard_map/cross_backward/pallas_call | solution.py:560
  508.6 40.3 %self_backward.1 = (bf16[32,40,768]{2,1,0:T(8,128)(2,1)}, bf16[32,40,768]{2,1,0:T(8,128)(2,1)}, bf16[32,40,768]{2,1,0:T(8,128)(2,1)}, bf16[32,40,768]{2,1,0:T(8,...) custom-call(f32[32,40,768]{2,1,0:T(8,128)} %get-tuple-element.66.gm, ...), custom_call_target="tpu_custom_call" | custom-call | flops 10569646080 | bytes 40000000 | tf_op jit(solution)/shard_map/self_backward/pallas_call | solution.py:582
  548.9 3.5 fusion.57
  552.4 1.7 fusion.59
  556.4 1.7 fusion.63
  558.5 1.8 fusion.65
  562.2 1.8 fusion.67
  564.0 3.6 copy-done.8
  567.6 8.6 copy.126
  577.9 4.4 fusion.53
  582.3 4.3 fusion.47
  586.6 4.5 fusion.41
  591.1 4.6 fusion.35
  595.6 8.1 convert_dynamic-update-slice_fusion
  603.8 8.7 copy.128
  614.1 32.9 %reduce-scatter.11.cloned.1.call-done = bf16[4,145,768]{2,1,0:T(8,128)(2,1)} async-done(((bf16[32,145,768]{2,1,0:T(8,128)(2,1)}), bf16[4,145,768]{2,1,0:T(8,128)(2,1)}) %reduce-scatter.11.cloned.1.call-update) | async-done | bytes 890896 | tf_op jit(solution)/shard_map/reduce_scatter | solution.py:580
  649.5 2.7 fusion.31
  653.8 134.5 %reduce-scatter.13.cloned.1.call-done = bf16[24,6144]{1,0:T(8,128)(2,1)} async-done(((bf16[768,6144]{1,0:T(8,128)(2,1)}), bf16[24,6144]{1,0:T(8,128)(2,1)}) %reduce-scatter.13.cloned.1.call-update) | async-done | bytes 294928
  789.3 139.6 %reduce-scatter.17.cloned.1.call-done = bf16[24,6144]{1,0:T(8,128)(2,1)} async-done(((bf16[768,6144]{1,0:T(8,128)(2,1)}), bf16[24,6144]{1,0:T(8,128)(2,1)}) %reduce-scatter.17.cloned.1.call-update) | async-done | bytes 294928
  933.2 2.6 reshape.250
  938.6 1.9 copy.110
  940.5 115.1 %all-reduce.6.cloned.1.call-done = f32[32,768]{1,0:T(8,128)} async-done(((f32[32,768]{1,0:T(8,128)}), f32[32,768]{1,0:T(8,128)}) %all-reduce.6.cloned.1.call-update) | async-done | bytes 98320
  1058.6 101.0 %reduce-scatter.15.cloned.1.call-done = bf16[32,768]{1,0:T(8,128)(2,1)} async-done(((bf16[1024,768]{1,0:T(8,128)(2,1)}), bf16[32,768]{1,0:T(8,128)(2,1)}) %reduce-scatter.15.cloned.1.call-update) | async-done | bytes 49168
  (170 shorter events, 48.5 us)
Async XLA Ops:
  7.2 62.8 %copy-start.25 = (bf16[4,145,1024]{2,0,1:T(4,128)(2,1)S(1)}, bf16[4,145,1024]{2,0,1:T(4,128)(2,1)}, u32[]{:S(2)}) copy-start(bf16[4,145,1024]{2,0,1:T(4,128)(2,1)} %param.33) | copy-start | bytes 3563524
  7.2 62.8 %all-gather.7.cloned.1.call-start = ((), (), s32[]{:S(2)}) async-start(), calls=%async_computation.5 | async-start | bytes 1622016 | tf_op jit(solution)/shard_map/all_gather | solution.py:428
  7.9 145.5 %all-gather.5.cloned.1.call-start = ((), (), s32[]{:S(2)}) async-start(), calls=%async_computation.4 | async-start | bytes 9732096 | tf_op jit(solution)/shard_map/all_gather | solution.py:428
  14.9 253.7 %all-gather.9.cloned.1.call-start = ((), (), s32[]{:S(2)}) async-start(), calls=%async_computation.6 | async-start | bytes 8404992 | tf_op jit(solution)/shard_map/all_gather | solution.py:471
  70.0 4.1 copy-start.14
  74.0 2.7 copy-start.15
  74.0 278.3 %all-gather.11.cloned.1.call-start = ((), (), s32[]{:S(2)}) async-start(), calls=%async_computation.7 | async-start | bytes 9732096 | tf_op jit(solution)/shard_map/all_gather | solution.py:428
  75.3 7.8 copy-start.27
  75.3 7.8 copy-start.28
  75.3 8.2 copy-start.16
  77.5 569.5 %reduce-scatter.11.cloned.1.call-start = ((), (), s32[]{:S(2)}) async-start(), calls=%async_computation.8 | async-start | bytes 8404992 | tf_op jit(solution)/shard_map/reduce_scatter | solution.py:580
  78.0 127.4 %copy-start.2 = (f32[1,768]{1,0:T(1,128)}, f32[1,768]{1,0:T(1,128)S(1)}, u32[]{:S(2)}) copy-start(f32[1,768]{1,0:T(1,128)S(1)} %reshape.217.g1) | copy-start | bytes 9220
  78.1 127.3 %copy-start.4 = (f32[1,768]{1,0:T(1,128)}, f32[1,768]{1,0:T(1,128)S(1)}, u32[]{:S(2)}) copy-start(f32[1,768]{1,0:T(1,128)S(1)} %reshape.218.b1) | copy-start | bytes 9220
  507.9 280.4 %reduce-scatter.13.cloned.1.call-start = ((), (), s32[]{:S(2)}) async-start(), calls=%async_computation.9 | async-start | bytes 9732096
  508.6 40.3 %copy-start.9 = (bf16[32,40,768]{2,1,0:T(8,128)(2,1)S(1)}, bf16[32,40,768]{2,1,0:T(8,128)(2,1)}, u32[]{:S(2)}) copy-start(bf16[32,40,768]{2,1,0:T(8,128)(2,1)} %tok.1) | copy-start | bytes 5898244
  548.9 3.5 copy-start.23
  552.4 1.8 copy-start.22
  554.2 1.8 copy-start.20
  554.2 2.2 copy-start.21
  556.3 1.8 copy-start.10
  556.3 2.2 copy-start.19
  558.5 3.1 copy-start.31
  560.3 1.9 copy-start.7
  564.0 3.6 copy-start.8
  576.3 352.7 %reduce-scatter.17.cloned.1.call-start = ((), (), s32[]{:S(2)}) async-start(), calls=%async_computation.11 | async-start | bytes 9732096
  586.6 9.0 slice-start
  591.0 4.6 copy-start.29
  591.0 4.6 slice-start.1
  612.5 37.0 %copy-start.26 = (bf16[4,145,1024]{2,0,1:T(4,128)(2,1)S(1)}, bf16[4,145,1024]{2,0,1:T(4,128)(2,1)}, u32[]{:S(2)}) copy-start(bf16[4,145,1024]{2,0,1:T(4,128)(2,1)} %param.33) | copy-start | bytes 3563524
  612.5 443.1 %all-reduce.6.cloned.1.call-start = ((), (), s32[]{:S(2)}) async-start(), calls=%async_computation.12 | async-start | bytes 196608
  649.2 510.4 %reduce-scatter.15.cloned.1.call-start = ((), (), s32[]{:S(2)}) async-start(), calls=%async_computation.10 | async-start | bytes 1622016
  933.2 3.4 copy-start.12
  (11 other events, 13.5 us)
Sparse Core Ops, SparseCore 0:
  10.9 58.1 all-gather.6
  72.6 80.7 all-gather.4
  156.2 112.3 all-gather.8
  272.0 80.2 all-gather.10
  508.0 138.8 reduce-scatter.10
  653.7 134.5 reduce-scatter.12
  794.2 134.7 reduce-scatter.16
  936.0 119.4 all-reduce.5
  1061.7 97.9 reduce-scatter.14

commit v2 on v1

--- a/solution.py
+++ b/solution.py
@@ -153,22 +153,22 @@
     pr_o[...] = (nn(first, wc[...]) + pb[...]).reshape(rb, length, width).astype(BF)
 
 
-def cross_forward(starts, order, proj, wk, wv, cb, probe, k_o, v_o, p_o, mix_o, pr_s):
+def cross_forward(starts, order, pat, wp, wk, wv, pab, cb, probe, pr_o, k_o, v_o, p_o, mix_o, pat_s):
     i = pl.program_id(0)
-    points = proj.shape[1]
-    padded = k_o.shape[1]
+    points = pat.shape[1]
     length = probe.shape[1]
 
     @pl.when(i == 0)
     def _():
-        pr_s[...] = jnp.zeros_like(pr_s)
+        pat_s[...] = jnp.zeros_like(pat_s)
 
     lo, hi = starts[i], starts[i + 1]
 
     @pl.when(hi > lo)
     def _():
-        pr_s[0:points, :] = proj[0]
-        pr = pr_s[...]
+        pat_s[0:points, :] = pat[0]
+        pr = (nn(pat_s[...], wp[...]) + pab[...]).astype(BF)
+        pr_o[0] = pr
         k_o[0] = nn(pr, wk[...]).astype(BF)
         v_o[0] = (nn(pr, wv[...]) + cb[...]).astype(BF)
 
@@ -266,19 +266,20 @@
 
 
 def cross_backward(
-    starts, order, proj, keys, values, wk, wv, probe, grad, probs,
-    dpr_o, dproj_o, dwk_o, dwv_o, dcb_o,
-    pr_s, dk_s, dv_s, dwk_s, dwv_s,
+    starts, order, pat, proj, keys, values, wk, wv, probe, grad, probs,
+    dpr_o, dproj_o, dwk_o, dwv_o, dwp_o, dcb_o,
+    pat_s, dk_s, dv_s, dwk_s, dwv_s, dwp_s,
 ):
     i = pl.program_id(0)
-    points = proj.shape[1]
+    points = pat.shape[1]
     length = probe.shape[1]
 
     @pl.when(i == 0)
     def _():
-        pr_s[...] = jnp.zeros_like(pr_s)
+        pat_s[...] = jnp.zeros_like(pat_s)
         dwk_s[...] = jnp.zeros_like(dwk_s)
         dwv_s[...] = jnp.zeros_like(dwv_s)
+        dwp_s[...] = jnp.zeros_like(dwp_s)
         dcb_o[...] = jnp.zeros_like(dcb_o)
 
     lo, hi = starts[i], starts[i + 1]
@@ -313,8 +314,8 @@
             return carry
 
         lax.fori_loop(lo, hi, row, 0)
-        pr_s[0:points, :] = proj[0]
-        pr = pr_s[...]
+        pat_s[0:points, :] = pat[0]
+        pr = proj[0]
         dk = dk_s[...].astype(BF)
         dv = dv_s[...].astype(BF)
         dcb_o[0:1] += jnp.sum(dv.astype(F32), 0, keepdims=True)
@@ -322,11 +323,14 @@
         dproj_o[0] = dproj[0:points]
         dwk_s[...] += tn(pr, dk)
         dwv_s[...] += tn(pr, dv)
+        dwp_s[...] += tn(pat_s[...], dproj)
+        dcb_o[1:2] += jnp.sum(dproj.astype(F32), 0, keepdims=True)
 
     @pl.when(i == pl.num_programs(0) - 1)
     def _():
         dwk_o[...] = dwk_s[...].astype(BF)
         dwv_o[...] = dwv_s[...].astype(BF)
+        dwp_o[...] = dwp_s[...].astype(BF)
 
 
 def self_backward(
@@ -424,6 +428,265 @@
     return pl.CostEstimate(flops=int(flops), bytes_accessed=int(bytes_accessed), transcendentals=0)
 
 
+def my_place():
+    dp, fs = lax.axis_index("dp"), lax.axis_index("fsdp")
+    return dp // 2, dp % 2, fs // 2, fs % 2
+
+
+def device_at(z, y, x, c):
+    return (z * 2 + y, x * 2 + c)
+
+
+def meet(z, y, x, c):
+    sem = pltpu.get_barrier_semaphore()
+    others = [device_at((z + k) % 4, y, x, c) for k in (1, 2, 3)]
+    others += [device_at(z, 1 - y, x, c), device_at(z, y, 1 - x, c), device_at(z, y, x, 1 - c)]
+    for other in others:
+        pl.semaphore_signal(sem, inc=1, device_id=other, device_id_type=pl.DeviceIdType.MESH)
+    pl.semaphore_wait(sem, len(others))
+
+
+class Copies:
+    def __init__(self, send, recv, local):
+        self.send, self.recv, self.local = send, recv, local
+        self.far = self.near = 0
+
+    def remote(self, src, dst, device):
+        i = self.far
+        self.far += 1
+        copy = pltpu.make_async_remote_copy(
+            src_ref=src, dst_ref=dst, send_sem=self.send.at[i], recv_sem=self.recv.at[i],
+            device_id=device, device_id_type=pl.DeviceIdType.MESH,
+        )
+        copy.start()
+        return copy
+
+    def here(self, src, dst):
+        i = self.near
+        self.near += 1
+        copy = pltpu.make_async_copy(src, dst, self.local.at[i])
+        copy.start()
+        return copy
+
+
+def arrived(copies):
+    for copy in copies:
+        copy.wait()
+
+
+def drive(jobs, order):
+    for name in order:
+        next(jobs[name], None)
+    for job in jobs.values():
+        for _ in job:
+            pass
+
+
+def gather_kernel(parts, w_in, p_in, w_out, p_out, send, recv, local):
+    z, y, x, c = my_place()
+    meet(z, y, x, c)
+    copies = Copies(send, recv, local)
+
+    def slabs(lo, n):
+        pick = pl.ds(lo, n)
+        mine = w_out.at[pick, z, y, x, c]
+        pending = [copies.here(w_in.at[pick], mine)]
+        pending += [
+            copies.remote(w_in.at[pick], mine, device_at((z + k) % 4, y, x, c)) for k in (1, 3, 2)
+        ]
+        yield
+        arrived(pending)
+        line = w_out.at[pick, :, y, x, c]
+        step = copies.remote(line, line, device_at(z, 1 - y, x, c))
+        yield
+        step.wait()
+        plane = w_out.at[pick, :, :, x, c]
+        step = copies.remote(plane, plane, device_at(z, y, 1 - x, c))
+        yield
+        step.wait()
+        half = w_out.at[pick, :, :, :, c]
+        step = copies.remote(half, half, device_at(z, y, x, 1 - c))
+        yield
+        step.wait()
+
+    def image(i):
+        mine = p_out.at[z, y, i]
+        pending = [copies.here(p_in.at[i], mine)]
+        pending += [
+            copies.remote(p_in.at[i], mine, device_at((z + k) % 4, y, x, c)) for k in (1, 3, 2)
+        ]
+        yield
+        arrived(pending)
+        line = p_out.at[:, y, i]
+        step = copies.remote(line, line, device_at(z, 1 - y, x, c))
+        yield
+        step.wait()
+
+    jobs = {}
+    for j, (lo, n) in enumerate(parts):
+        jobs["w%d" % j] = slabs(lo, n)
+    for i in range(p_in.shape[0]):
+        jobs["p%d" % i] = image(i)
+    drive(jobs, ["w0", "p0", "w1", "p1", "p2", "p3", "w0", "p0", "w0", "w1", "w0", "p1", "w1", "p2", "w1", "p3"])
+
+
+def reduce_kernel(
+    parts, w_in, p_in, w_out, p_out, acc, rc, rx, ry, rz, pacc, pry, prz, send, recv, local
+):
+    z, y, x, c = my_place()
+    meet(z, y, x, c)
+    copies = Copies(send, recv, local)
+
+    def up(ref, *at):
+        return ref[at].astype(F32)
+
+    def slabs(lo, n):
+        pick = pl.ds(lo, n)
+        own = copies.here(w_in.at[pick, :, :, :, c], acc.at[pick])
+        step = copies.remote(w_in.at[pick, :, :, :, 1 - c], rc.at[pick], device_at(z, y, x, 1 - c))
+        yield
+        own.wait()
+        step.wait()
+
+        def add_x(i, carry):
+            s, zz = lo + i // 4, i % 4
+            for yy in range(2):
+                acc[s, zz, yy, 1 - x] = (up(acc, s, zz, yy, 1 - x) + up(rc, s, zz, yy, 1 - x)).astype(BF)
+            return carry
+
+        lax.fori_loop(0, 4 * n, add_x, 0)
+        step = copies.remote(acc.at[pick, :, :, 1 - x], rx.at[pick], device_at(z, y, 1 - x, c))
+        yield
+        step.wait()
+
+        def add_y(i, carry):
+            s, zz = lo + i // 4, i % 4
+            acc[s, zz, 1 - y, x] = (
+                up(acc, s, zz, 1 - y, x) + up(rc, s, zz, 1 - y, x) + up(rx, s, zz, 1 - y)
+            ).astype(BF)
+            return carry
+
+        lax.fori_loop(0, 4 * n, add_y, 0)
+        step = copies.remote(acc.at[pick, :, 1 - y, x], ry.at[pick], device_at(z, 1 - y, x, c))
+        yield
+        step.wait()
+        steps = []
+        for k in (1, 3, 2):
+            zz = (z + k) % 4
+
+            def add_z(i, carry):
+                s = lo + i
+                acc[s, zz, y, x] = (
+                    up(acc, s, zz, y, x) + up(rc, s, zz, y, x) + up(rx, s, zz, y) + up(ry, s, zz)
+                ).astype(BF)
+                return carry
+
+            lax.fori_loop(0, n, add_z, 0)
+            steps.append(
+                copies.remote(acc.at[pick, zz, y, x], rz.at[k - 1, pick], device_at(zz, y, x, c))
+            )
+        yield
+        arrived(steps)
+
+        def add_last(i, carry):
+            s = lo + i
+            w_out[s] = (
+                up(acc, s, z, y, x) + up(rc, s, z, y, x) + up(rx, s, z, y) + up(ry, s, z)
+                + up(rz, 0, s) + up(rz, 1, s) + up(rz, 2, s)
+            )
+            return carry
+
+        lax.fori_loop(0, n, add_last, 0)
+
+    def image(i):
+        own = copies.here(p_in.at[:, y, i], pacc.at[i])
+        step = copies.remote(p_in.at[:, 1 - y, i], pry.at[i], device_at(z, 1 - y, x, c))
+        yield
+        own.wait()
+        step.wait()
+        steps = []
+        for k in (1, 3, 2):
+            zz = (z + k) % 4
+            pacc[i, zz] = (up(pacc, i, zz) + up(pry, i, zz)).astype(BF)
+            steps.append(copies.remote(pacc.at[i, zz], prz.at[k - 1, i], device_at(zz, y, x, c)))
+        yield
+        arrived(steps)
+        p_out[i] = (
+            up(pacc, i, z) + up(pry, i, z) + up(prz, 0, i) + up(prz, 1, i) + up(prz, 2, i)
+        ).astype(BF)
+
+    jobs = {}
+    for i in range(p_in.shape[2]):
+        jobs["p%d" % i] = image(i)
+    for j, (lo, n) in enumerate(parts):
+        jobs["w%d" % j] = slabs(lo, n)
+    drive(
+        jobs,
+        ["w0", "p0", "p1", "w1", "p2", "p3", "w0", "w1", "p0", "w0", "p1", "w1", "p2", "w0", "p3", "w1"],
+    )
+
+
+def split_slabs(count):
+    first = (count + 1) // 2
+    return ((0, first), (first, count - first))
+
+
+def gather_all(slabs, patches):
+    n, sr, width = slabs.shape
+    images, points, pwidth = patches.shape
+    parts = split_slabs(n)
+    copies = 6 * len(parts) + 4 * images
+    w_all, p_all = pl.pallas_call(
+        functools.partial(gather_kernel, parts),
+        in_specs=[pl.BlockSpec(memory_space=pl.ANY)] * 2,
+        out_specs=[pl.BlockSpec(memory_space=pl.ANY)] * 2,
+        out_shape=[sds((n, 4, 2, 2, 2, sr, width), BF), sds((4, 2, images, points, pwidth), BF)],
+        scratch_shapes=[
+            pltpu.SemaphoreType.DMA((copies,)),
+            pltpu.SemaphoreType.DMA((copies,)),
+            pltpu.SemaphoreType.DMA((len(parts) + images,)),
+        ],
+        compiler_params=pltpu.CompilerParams(
+            collective_id=0, has_side_effects=True, vmem_limit_bytes=8 * 1024 * 1024
+        ),
+        name="gather_all",
+    )(slabs, patches)
+    return w_all.reshape(n, 32 * sr, width), p_all.reshape(8 * images, points, pwidth)
+
+
+def reduce_all(slabs, grads):
+    n, full, width = slabs.shape
+    sr = full // 32
+    total, points, _ = grads.shape
+    images = total // 8
+    parts = split_slabs(n)
+    copies = 6 * len(parts) + 4 * images
+    w_shard, p_shard = pl.pallas_call(
+        functools.partial(reduce_kernel, parts),
+        in_specs=[pl.BlockSpec(memory_space=pl.ANY)] * 2,
+        out_specs=[pl.BlockSpec(memory_space=pltpu.VMEM)] * 2,
+        out_shape=[sds((n, sr, width), F32), sds((images, points, width), BF)],
+        scratch_shapes=[
+            pltpu.VMEM((n, 4, 2, 2, sr, width), BF),
+            pltpu.VMEM((n, 4, 2, 2, sr, width), BF),
+            pltpu.VMEM((n, 4, 2, sr, width), BF),
+            pltpu.VMEM((n, 4, sr, width), BF),
+            pltpu.VMEM((3, n, sr, width), BF),
+            pltpu.VMEM((images, 4, points, width), BF),
+            pltpu.VMEM((images, 4, points, width), BF),
+            pltpu.VMEM((3, images, points, width), BF),
+            pltpu.SemaphoreType.DMA((copies,)),
+            pltpu.SemaphoreType.DMA((copies,)),
+            pltpu.SemaphoreType.DMA((len(parts) + images,)),
+        ],
+        compiler_params=pltpu.CompilerParams(
+            collective_id=1, has_side_effects=True, vmem_limit_bytes=56 * 1024 * 1024
+        ),
+        name="reduce_all",
+    )(slabs.reshape(n, 4, 2, 2, 2, sr, width), grads.reshape(4, 2, images, points, width))
+    return w_shard, p_shard
+
+
 def gather(value, axis):
     return lax.all_gather(value, AXES, axis=axis, tiled=True)
 
@@ -445,30 +708,43 @@
     sr = self_query.shape[0]
     wr = widen_bias.shape[0]
 
+    place = lax.axis_index("dp") * lax.axis_size("fsdp") + lax.axis_index("fsdp")
     vec_list = (
         query_bias, value_bias, output_bias, first_gain, first_norm_bias, patch_bias, probe_bias,
         content_bias, cross_bias, second_gain, second_shift, narrow_bias, third_gain, third_shift,
     )
-    packed = jnp.concatenate(vec_list + (widen_bias,))
-    packed = jnp.pad(packed, (0, width - packed.shape[0]))[None]
-    packed_all = gather(jnp.pad(packed, ((0, 7), (0, 0))), 0).reshape(shards, 8, width)[:, 0].astype(F32)
-    vecs = [packed_all[:, sr * j : sr * (j + 1)].reshape(1, width) for j in range(len(vec_list))]
-    (qb, vb, ob, g1, b1, pab, prb, cob, crb, g2, s2, nab, g3, s3) = vecs
-    wb = packed_all[:, sr * len(vec_list) : sr * len(vec_list) + wr]
+    nv = len(vec_list)
+    pr = patch_proj.shape[0]
+    tails = pr - sr
+    lane_block = jnp.arange(width, dtype=jnp.int32)[None, :] // sr
+    vec_rows = jnp.where(lane_block == place, jnp.tile(jnp.stack(vec_list), (1, shards)), jnp.zeros((), BF))
+    wb_row = jnp.pad(widen_bias, (0, width - wr))[None]
+    extra = jnp.concatenate([patch_proj[sr:], vec_rows, wb_row], 0)
+    er = max(sr, extra.shape[0])
+    own_rows = er == sr and groups == 8 and shards == 32
+    extra = jnp.pad(extra, ((0, er - extra.shape[0]), (0, 0)))
+    mats = [self_query, self_key, self_value, self_output, cross_query, cross_key, cross_value, cross_output, patch_proj[:sr]]
+    if own_rows:
+        w_a, patches_all = gather_all(jnp.stack(mats + [extra]), patches)
+        extra_all = w_a[len(mats)].reshape(shards, er, width)
+    else:
+        w_a = gather(jnp.stack(mats), 1)
+        extra_all = gather(extra, 0).reshape(shards, er, width)
+        patches_all = lax.all_gather(patches, "dp", axis=0, tiled=True)
+    vec_all = jnp.sum(extra_all[:, tails : tails + nv].astype(F32), 0)
+    (qb, vb, ob, g1, b1, pab, prb, cob, crb, g2, s2, nab, g3, s3) = [vec_all[j : j + 1] for j in range(nv)]
+    wb = extra_all[:, tails + nv, :wr].astype(F32)
     wb = wb.reshape(shards, chunks, sr).transpose(1, 0, 2).reshape(chunks, 1, width)
-
-    patch_full = gather(patch_proj, 0)
-    w_a = gather(
-        jnp.stack([self_query, self_key, self_value, self_output, cross_query, cross_key, cross_value, cross_output]), 1
-    )
+    patch_full = jnp.concatenate(
+        [w_a[len(mats) - 1].reshape(shards, sr, width), extra_all[:, :tails]], 1
+    ).reshape(shards * pr, width)
+
     widen_slabs = widen_weight.reshape(sr, shards, chunks, sr).transpose(2, 0, 1, 3).reshape(chunks, sr, width)
     narrow_slabs = narrow_weight.reshape(chunks, sr, width)
-    w_b = gather(jnp.concatenate([widen_slabs, narrow_slabs], 0), 1)
-
-    projected = (
-        lax.dot_general(patches, patch_full, (((2,), (0,)), ((), ())), preferred_element_type=F32) + pab
-    ).astype(BF)
-    proj_all = lax.all_gather(projected, "dp", axis=0, tiled=True)
+    w_b_in = jnp.concatenate([widen_slabs, narrow_slabs], 0)
+    if own_rows:
+        w_b_in, w_a = lax.optimization_barrier((w_b_in, w_a))
+    w_b = gather(w_b_in, 1)
 
     image = owner * images + image_slot
     idx = jnp.arange(rows, dtype=jnp.int32)
@@ -512,22 +788,23 @@
     padded = -(-points // 16) * 16
     kv_sh = (total_images, padded, width)
     cross_p = (rows, 4, padded, 3 * length)
-    img_spec = pl.BlockSpec((1, points, width), lambda i, *_: (i, 0, 0))
+    img_spec = pl.BlockSpec((1, points, pwidth), lambda i, *_: (i, 0, 0))
+    grad_spec = pl.BlockSpec((1, points, width), lambda i, *_: (i, 0, 0))
     kv_spec = pl.BlockSpec((1, padded, width), lambda i, *_: (i, 0, 0))
-    image_keys, image_values, cprobs, mixed = pl.pallas_call(
+    projected, image_keys, image_values, cprobs, mixed = pl.pallas_call(
         cross_forward,
         grid_spec=pltpu.PrefetchScalarGridSpec(
             num_scalar_prefetch=2,
             grid=(total_images,),
-            in_specs=[img_spec, wspec(5), wspec(6), vspec, whole(tok_sh)],
-            out_specs=[kv_spec, kv_spec, whole(cross_p), whole(tok_sh)],
-            scratch_shapes=[pltpu.VMEM((padded, width), BF)],
+            in_specs=[img_spec, whole(patch_full.shape), wspec(5), wspec(6), vspec, vspec, whole(tok_sh)],
+            out_specs=[kv_spec, kv_spec, kv_spec, whole(cross_p), whole(tok_sh)],
+            scratch_shapes=[pltpu.VMEM((padded, pwidth), BF)],
         ),
-        out_shape=[sds(kv_sh, BF), sds(kv_sh, BF), sds(cross_p, BF), sds(tok_sh, BF)],
+        out_shape=[sds(kv_sh, BF), sds(kv_sh, BF), sds(kv_sh, BF), sds(cross_p, BF), sds(tok_sh, BF)],
         compiler_params=params(48),
         cost_estimate=cost(4 * total_images * points * width * width, 40e6),
         name="cross_forward",
-    )(starts, order, proj_all, w_a, w_a, cob, probe)
+    )(starts, order, patches_all, patch_full, w_a, w_a, pab, cob, probe)
 
     def chunk_w(j):
         return pl.BlockSpec((chunks, width, width), lambda i, *_: (j, 0, 0), pipeline_mode=pl.Buffered(1))
@@ -557,27 +834,27 @@
         name="tail",
     )(u1, mixed, out_grad, w_a, w_b, w_b, g1, b1, crb, g2, s2, wb, nab, g3, s3)
 
-    dprobe, dproj, dwk, dwv, dcb = pl.pallas_call(
+    dprobe, dproj, dwk, dwv, dwp, dcb = pl.pallas_call(
         cross_backward,
         grid_spec=pltpu.PrefetchScalarGridSpec(
             num_scalar_prefetch=2,
             grid=(total_images,),
-            in_specs=[img_spec, kv_spec, kv_spec, wspec(5), wspec(6), whole(tok_sh), whole(tok_sh), whole(cross_p)],
-            out_specs=[whole(tok_sh), img_spec, whole(slab), whole(slab), whole((8, width))],
+            in_specs=[img_spec, kv_spec, kv_spec, kv_spec, wspec(5), wspec(6), whole(tok_sh), whole(tok_sh), whole(cross_p)],
+            out_specs=[whole(tok_sh), grad_spec, whole(slab), whole(slab), whole((pwidth, width)), whole((8, width))],
             scratch_shapes=[
-                pltpu.VMEM((padded, width), BF),
+                pltpu.VMEM((padded, pwidth), BF),
                 pltpu.VMEM((padded, width), F32),
                 pltpu.VMEM((padded, width), F32),
                 pltpu.VMEM((width, width), F32),
                 pltpu.VMEM((width, width), F32),
+                pltpu.VMEM((pwidth, width), F32),
             ],
         ),
-        out_shape=[sds(tok_sh, BF), sds((total_images, points, width), BF), sds(slab, BF), sds(slab, BF), sds((8, width), F32)],
-        compiler_params=params(52),
+        out_shape=[sds(tok_sh, BF), sds((total_images, points, width), BF), sds(slab, BF), sds(slab, BF), sds((pwidth, width), BF), sds((8, width), F32)],
+        compiler_params=params(56),
         cost_estimate=cost(8 * total_images * points * width * width, 50e6),
         name="cross_backward",
-    )(starts, order, proj_all, image_keys, image_values, w_a, w_a, probe, grad_crossed, cprobs)
-    grad_projected = lax.psum_scatter(dproj, "dp", scatter_dimension=0, tiled=True)
+    )(starts, order, patches_all, projected, image_keys, image_values, w_a, w_a, probe, grad_crossed, cprobs)
 
     gb1, dq, dk, dv, tokens_grad, vec_s = pl.pallas_call(
         self_backward,
@@ -604,35 +881,41 @@
         jnp.concatenate([grad_widen, grad_narrow], 0), AXES, scatter_dimension=1, tiled=True
     ).astype(F32)
 
-    patch_low = grad_projected
-    grad_patch_proj = lax.dot_general(
-        patches, patch_low, (((0, 1), (0, 1)), ((), ())), preferred_element_type=F32
+    vec_grads = jnp.concatenate(
+        [
+            vec_s[4:5], vec_s[5:6], vec_s[2:3], vec_s[0:1], vec_s[1:2], dcb[1:2], vec_s[3:4], dcb[0:1],
+            vec_t[5:6], vec_t[3:4], vec_t[4:5], vec_t[2:3], vec_t[0:1], vec_t[1:2],
+        ]
     ).astype(BF)
-    grad_patch_bias = jnp.sum(patch_low.astype(F32), (0, 1))[None]
+    wb_flat = wb_grad.reshape(chunks, shards, sr).transpose(1, 0, 2).reshape(shards, 1, wr).astype(BF)
+    dwp = dwp.reshape(shards, pr, width)
+    extra_grad = jnp.concatenate(
+        [
+            dwp[:, sr:],
+            jnp.broadcast_to(vec_grads[None], (shards, nv, width)),
+            jnp.pad(wb_flat, ((0, 0), (0, 0), (0, width - wr))),
+            jnp.zeros((shards, er - tails - nv - 1, width), BF),
+        ],
+        1,
+    )
+    slabs = [
+        wgrad(tokens, dq), wgrad(tokens, dk), wgrad(tokens, dv), wgrad(attended, gb1),
+        wgrad(first_low, dprobe), dwk, dwv, wgrad(mixed, gb2), dwp[:, :sr].reshape(slab),
+    ]
+    if own_rows:
+        slab_shard, grad_projected = reduce_all(jnp.stack(slabs + [extra_grad.reshape(slab)]), dproj)
+        extra_shard = slab_shard[len(slabs)]
+    else:
+        grad_projected = lax.psum_scatter(dproj, "dp", scatter_dimension=0, tiled=True)
+        slab_shard = lax.psum_scatter(jnp.stack(slabs), AXES, scatter_dimension=1, tiled=True).astype(F32)
+        extra_shard = lax.psum_scatter(extra_grad, AXES, scatter_dimension=0, tiled=True)[0].astype(F32)
+    patch_shard = jnp.concatenate([slab_shard[len(slabs) - 1], extra_shard[:tails]], 0)
     patches_grad = lax.dot_general(
-        patch_low, patch_full, (((2,), (1,)), ((), ())), preferred_element_type=F32
+        grad_projected, patch_full, (((2,), (1,)), ((), ())), preferred_element_type=F32
     ).astype(BF)
-
-    vec_grads = [
-        vec_s[4:5], vec_s[5:6], vec_s[2:3], vec_s[0:1], vec_s[1:2], grad_patch_bias, vec_s[3:4], dcb[0:1],
-        vec_t[5:6], vec_t[3:4], vec_t[4:5], vec_t[2:3], vec_t[0:1], vec_t[1:2],
-    ]
-    wb_flat = wb_grad.reshape(chunks, shards, sr).transpose(1, 0, 2).reshape(shards, wr)
-    vec_rows = jnp.concatenate([item.reshape(shards, sr) for item in vec_grads] + [wb_flat], 1)
-    vec_rows = jnp.pad(vec_rows, ((0, 0), (0, width - vec_rows.shape[1])))
-    vec_shard = lax.psum_scatter(vec_rows, AXES, scatter_dimension=0, tiled=True)[0]
-
-    slabs = jnp.stack(
-        [
-            wgrad(tokens, dq), wgrad(tokens, dk), wgrad(tokens, dv), wgrad(attended, gb1),
-            wgrad(first_low, dprobe), dwk, dwv, wgrad(mixed, gb2),
-        ]
-    )
-    slab_shard = lax.psum_scatter(slabs, AXES, scatter_dimension=1, tiled=True).astype(F32)
-    patch_shard = lax.psum_scatter(grad_patch_proj, AXES, scatter_dimension=0, tiled=True).astype(F32)
-
-    vg = [vec_shard[sr * j : sr * (j + 1)] for j in range(len(vec_list))]
-    wbg = vec_shard[sr * len(vec_list) : sr * len(vec_list) + wr]
+    vg = lax.dynamic_slice(extra_shard, (tails, place * sr), (nv, sr))
+    vg = [vg[j] for j in range(nv)]
+    wbg = extra_shard[tails + nv, :wr]
     widen_shard = ffn_shard[:chunks].reshape(chunks, sr, shards, sr).transpose(1, 2, 0, 3).reshape(sr, hidden)
     narrow_shard = ffn_shard[chunks:].reshape(chunks * sr, width)
     return (

time: 1170 us -> 818 us (0.70)
  waiting for transfers between devices: 680 us -> 0.04 us
  Pallas kernels: 303 us -> 691 us
  blocking collectives: 44.6 us -> 0 us
    unnamed x13 -> x3, waiting for transfers between devices: 491 us -> 0.03 us
    pallas_call x0 -> x2, Pallas kernels: none -> 354 us  [the longest x1 200 us: gather_all(): pl.pallas_call(functools.partial(gather_kernel, parts), in_specs=[pl.Bloc...]
    all_gather x3 -> x1, waiting for transfers between devices: 95.3 us -> 0.01 us  [gather(): return lax.all_gather(value, AXES, axis=axis, tiled=True)]
    all_gather x1 -> x0, waiting for transfers between devices: 60.6 us -> none  [on_device(): proj_all = lax.all_gather(projected, 'dp', axis=0, tiled=True)]
    all_gather x1 -> x0, blocking collectives: 44.6 us -> none  [gather(): return lax.all_gather(value, AXES, axis=axis, tiled=True)]
    reduce_scatter x1 -> x0, waiting for transfers between devices: 32.9 us -> none  [on_device(): lax.psum_scatter(dproj, 'dp', scatter_dimension=0, tiled=True)]
    pallas_call x1, Pallas kernels: 88 us -> 99.8 us  [on_device(): pl.pallas_call(cross_backward, grid_spec=pltpu.PrefetchScalarGridSpec(num...]
    unnamed x86 -> x100, local copies, waits for them, and re-layouts: 45.3 us -> 46.6 us
  transfers between devices with their start and end apart: 9 -> 2, of which waited for: 8 -> 0; matrix products, arithmetic and copies ran while one was open for 9% -> 4% of each run, Pallas kernels for 13% -> 51%
where the time goes in v2:
time: 818 us; the launch traced here: 814 us
  Pallas kernels  691 us (84%)
  local copies, waits for them, and re-layouts  66.6 us (8%)
  matrix products  37.1 us (5%)
  between operations  15 us (2%)
    pallas_call x1, Pallas kernels, gather_all(): pl.pallas_call(functools.partial(gather_kernel, parts), in_specs=[pl.Bloc...  200 us
    pallas_call x1, Pallas kernels, reduce_all(): pl.pallas_call(functools.partial(reduce_kernel, parts), in_specs=[pl.Bloc...  154 us
    pallas_call x1, Pallas kernels, on_device(): pl.pallas_call(cross_backward, grid_spec=pltpu.PrefetchScalarGridSpec(num...  99.8 us
    pallas_call x1, Pallas kernels, on_device(): pl.pallas_call(tail_kernel, grid=grid, in_specs=[tb, tb, tb, wspec(7), ch...  79.1 us
    pallas_call x1, Pallas kernels, on_device(): pl.pallas_call(cross_forward, grid_spec=pltpu.PrefetchScalarGridSpec(num_...  66.1 us
    pallas_call x1, Pallas kernels, on_device(): pl.pallas_call(self_forward, grid=grid, in_specs=[tb, rows_block((rows, l...  52 us
    unnamed x100, local copies, waits for them, and re-layouts  46.6 us
    pallas_call x1, Pallas kernels, on_device(): pl.pallas_call(self_backward, grid=grid, in_specs=[tb, tb, tb, tb, tb, tb...  40.2 us
  transfers between devices with their start and end apart: 2, of which 0 were waited for; matrix products, arithmetic and copies ran while one was open for 4% of the time, Pallas kernels for 51%

profile of v2, /device:TPU:0, one launch (start us, length us, event | category | flops | bytes accessed | tf_op | source)
XLA Modules:
  0.0 813.7 jit_solution(2669047928018664180)
XLA Ops:
  7.9 1.6 stack.144
  16.7 2.1 reshape.297
  21.4 199.9 %gather_all.1 = (bf16[10,4,2,2,2,24,768]{6,5,4,3,2,1,0:T(8,128)(2,1)S(1)}, bf16[4,2,4,145,1024]{4,3,2,1,0:T(8,128)(2,1)S(1)}) custom-call(bf16[10,24,768]{2,1,0:T(8,128)(2,1)S(1)} %constant_dynamic-update-slice_fusion.w_in, bf16[4,145,1024]{2,1,0:T(8,128)(2,1)S(1)} %copy.88.p_in), custom_call_target="tpu_custom_call" | custom-call | tf_op jit(solution)/shard_map/gather_all/pallas_call | solution.py:639
  221.3 4.3 copy-done
  225.7 3.7 copy-done.8
  229.9 1.8 fusion.78
  234.8 52.0 %self_forward.1 = (bf16[32,40,768]{2,1,0:T(8,128)(2,1)S(1)}, bf16[32,40,768]{2,1,0:T(8,128)(2,1)S(1)}, bf16[32,40,768]{2,1,0:T(8,128)(2,1)}, bf16[32,4,40,120]{3...) custom-call(bf16[32,40,768]{2,1,0:T(8,128)(2,1)} %tok.1, ...), custom_call_target="tpu_custom_call" | custom-call | flops 8304721920 | bytes 30000000 | tf_op jit(solution)/shard_map/self_forward/pallas_call | solution.py:771
  289.4 1.6 copy-done.9
  291.0 66.1 %cross_forward.1 = (bf16[32,160,768]{2,1,0:T(8,128)(2,1)}, bf16[32,160,768]{2,1,0:T(8,128)(2,1)}, bf16[32,160,768]{2,1,0:T(8,128)(2,1)}, bf16[32,4,160,120]{3,2,1,0:T(8,128)(2,1)}, bf16[32,40,768]{2,1,0:T(8,128)(2,1)S(1)}) custom-call(s32[33]{0:T(128)S(1)} %convert_reduce_fusion.2.starts, s32[32]{0:T(128)S(1)} %select_reduce_fusion.order, ...), custom_call_target="tpu_custom_call" | custom-call | flops 10947133440 | bytes 40000000 | tf_op jit(solution)/shard_map/cross_forward/pallas_call | solution.py:794
  358.3 79.1 %tail.1 = (bf16[32,40,768]{2,1,0:T(8,128)(2,1)}, bf16[4,1280,768]{2,1,0:T(8,128)(2,1)}, bf16[4,1280,768]{2,1,0:T(8,128)(2,1)}, bf16[32,40,768]{2,1,0:T(8,128)(2,...) custom-call(f32[32,40,768]{2,1,0:T(8,128)} %get-tuple-element.72.u1,, ...), custom_call_target="tpu_custom_call" | custom-call | flops 37748736000 | bytes 50000000 | tf_op jit(solution)/shard_map/tail/pallas_call | solution.py:815
  437.5 5.1 fusion.47
  442.6 2.9 fusion.41
  445.4 2.8 fusion.35
  448.3 2.8 fusion.29
  451.1 8.1 convert_dynamic-update-slice_fusion
  459.2 8.6 %copy.102 = bf16[96,8,8,768]{3,1,2,0:T(8,128)(2,1)} copy(bf16[96,8,8,768]{3,1,0,2:T(8,128)(2,1)} %bitcast.196) | data formatting | bytes 18874368
  467.9 99.8 %cross_backward.1 = (bf16[32,40,768]{2,1,0:T(8,128)(2,1)}, bf16[32,145,768]{2,1,0:T(8,128)(2,1)}, bf16[768,768]{1,0:T(8,128)(2,1)}, bf16[768,768]{1,0:T(8,128)(2...) custom-call(s32[33]{0:T(128)} %copy-done.10, s32[32]{0:T(128)} %copy-done.11, bf16[32,145,1024]{2,1,0:T(8,128)(2,1)} %bitcast.238, ...), custom_call_target="tpu_custom_call" | custom-call | flops 21894266880 | bytes 50000000 | tf_op jit(solution)/shard_map/cross_backward/pallas_call | solution.py:837
  570.2 40.2 %self_backward.1 = (bf16[32,40,768]{2,1,0:T(8,128)(2,1)}, bf16[32,40,768]{2,1,0:T(8,128)(2,1)}, bf16[32,40,768]{2,1,0:T(8,128)(2,1)}, bf16[32,40,768]{2,1,0:T(8,...) custom-call(f32[32,40,768]{2,1,0:T(8,128)} %get-tuple-element.78.gm, ...), custom_call_target="tpu_custom_call" | custom-call | flops 10569646080 | bytes 40000000 | tf_op jit(solution)/shard_map/self_backward/pallas_call | solution.py:859
  610.9 4.0 bitcast_convert_fusion.5
  615.0 1.4 copy-done.15
  616.5 1.8 bitcast_convert_fusion.4
  618.4 1.4 copy-done.29
  619.9 1.8 bitcast_convert_fusion.3
  621.8 1.4 copy-done.27
  623.3 1.8 bitcast_convert_fusion.2
  626.6 1.8 bitcast_convert_fusion.1
  631.9 1.8 bitcast_convert_fusion
  634.4 4.3 copy-done.14
  638.7 154.2 %reduce_all.1 = (f32[10,24,768]{2,1,0:T(8,128)}, bf16[4,145,768]{2,1,0:T(8,128)(2,1)}) custom-call(bf16[10,4,2,2,2,24,768]{6,5,4,3,2,1,0:T(8,128)(2,1)} %copy-done.14, bf16[4,2,4,145,768]{4,3,2,1,0:T(8,128)(2,1)} %bitcast.240), custom_call_target="tpu_custom_call" | custom-call | tf_op jit(solution)/shard_map/reduce_all/pallas_call | solution.py:664
  793.0 2.4 convolution_convert_fusion
  795.3 1.9 copy.96
  804.1 2.6 reshape.310
  (151 shorter events, 33.4 us)
Async XLA Ops:
  7.2 351.1 %all-gather.2.cloned.1.call-start = ((), (), s32[]{:S(2)}) async-start(), calls=%async_computation.1 | async-start | bytes 9732096 | tf_op jit(solution)/shard_map/all_gather | solution.py:691
  11.2 9.0 %copy-start.17 = (bf16[4,145,1024]{2,0,1:T(4,128)(2,1)S(1)}, bf16[4,145,1024]{2,0,1:T(4,128)(2,1)}, u32[]{:S(2)}) copy-start(bf16[4,145,1024]{2,0,1:T(4,128)(2,1)} %param.33) | copy-start | bytes 3563524
  19.0 1.7 copy-start.21
  19.0 2.4 slice-start
  221.3 4.3 copy-start
  225.7 3.7 copy-start.8
  229.4 3.2 copy-start.31
  229.4 3.2 copy-start.32
  229.4 3.6 copy-start.22
  229.5 570.4 %reduce-scatter.4.cloned.1.call-start = ((), (), s32[]{:S(2)}) async-start(), calls=%async_computation.2 | async-start | bytes 9732096
  232.7 56.6 %copy-start.10 = (s32[33]{0:T(128)}, s32[33]{0:T(128)S(1)}, u32[]{:S(2)}) copy-start(s32[33]{0:T(128)S(1)} %convert_reduce_fusion.2.starts) | copy-start | bytes 400
  233.0 56.4 %copy-start.11 = (s32[32]{0:T(128)}, s32[32]{0:T(128)S(1)}, u32[]{:S(2)}) copy-start(s32[32]{0:T(128)S(1)} %select_reduce_fusion.order) | copy-start | bytes 388
  233.9 55.5 %copy-start.3 = (bf16[32,32,768]{2,1,0:T(8,128)(2,1)}, bf16[32,32,768]{2,1,0:T(8,128)(2,1)S(1)}, u32[]{:S(2)}) copy-start(bf16[32,32,768]{2,1,0:T(8,128)(2,1)S(1)} %pad_maximum_fusion) | copy-start | bytes 4718596
  234.8 52.0 %copy-start.5 = (f32[1,768]{1,0:T(1,128)}, f32[1,768]{1,0:T(1,128)S(1)}, u32[]{:S(2)}) copy-start(f32[1,768]{1,0:T(1,128)S(1)} %get-tuple-element.266.g1) | copy-start | bytes 9220
  234.8 52.0 %copy-start.7 = (f32[1,768]{1,0:T(1,128)}, f32[1,768]{1,0:T(1,128)S(1)}, u32[]{:S(2)}) copy-start(f32[1,768]{1,0:T(1,128)S(1)} %get-tuple-element.265.b1) | copy-start | bytes 9220
  437.5 5.1 copy-start.34
  437.5 5.1 copy-start.35
  445.4 5.7 slice-start.1
  448.3 2.8 copy-start.33
  448.3 2.8 slice-start.2
  567.8 2.4 copy-start.6
  570.2 40.2 %copy-start.23 = (f32[8,768]{1,0:T(8,128)S(1)}, f32[8,768]{1,0:T(8,128)}, u32[]{:S(2)}) copy-start(f32[8,768]{1,0:T(8,128)} %get-tuple-element.102) | copy-start | bytes 73732
  570.2 40.3 %copy-start.24 = (f32[8,768]{1,0:T(8,128)S(1)}, f32[8,768]{1,0:T(8,128)}, u32[]{:S(2)}) copy-start(f32[8,768]{1,0:T(8,128)} %get-tuple-element.101) | copy-start | bytes 73732
  570.2 40.3 %copy-start.25 = (f32[4,1,768]{2,1,0:T(1,128)S(1)}, f32[4,1,768]{2,1,0:T(1,128)}, u32[]{:S(2)}) copy-start(f32[4,1,768]{2,1,0:T(1,128)} %get-tuple-element.103) | copy-start | bytes 36868
  610.9 4.1 copy-start.30
  619.9 2.0 copy-start.28
  623.3 1.9 copy-start.26
  629.7 1.6 copy-start.13
  629.7 2.2 copy-start.36
  634.4 4.3 copy-start.14
  638.7 154.2 %copy-start.4 = (bf16[32,32,768]{2,1,0:T(8,128)(2,1)S(1)}, bf16[32,32,768]{2,1,0:T(8,128)(2,1)}, u32[]{:S(2)}) copy-start(bf16[32,32,768]{2,1,0:T(8,128)(2,1)} %copy-done.3) | copy-start | bytes 4718596
  795.3 2.0 copy-start.20
  (10 other events, 14.5 us)
Sparse Core Ops, SparseCore 0:
  229.5 81.2 all-gather.1
  468.0 134.5 reduce-scatter.3

commit v3 on v2

--- a/solution.py
+++ b/solution.py
@@ -71,6 +71,21 @@
     return v * cdf, cdf + (v * INV_SQRT2PI) * bell
 
 
+def window(full, index):
+    base = WINDOWS[index][0]
+    return full[:, base : base + 256]
+
+
+def column_softmax(scores):
+    e = jnp.exp(scores - jnp.max(scores, 0, keepdims=True))
+    return (e * (1.0 / jnp.sum(e, 0, keepdims=True))).astype(BF)
+
+
+def score_grads(probs, grads):
+    p = probs.astype(F32)
+    return (p * (grads - jnp.sum(grads * p, 0, keepdims=True))).astype(BF)
+
+
 def stack_heads(full, index):
     base, off = WINDOWS[index]
     win = full[:, base : base + 256]
@@ -108,86 +123,87 @@
     )
 
 
-def self_forward(
-    tok, bias, wq, wk, wv, wo, wc, qb, vb, ob, g1, b1, pb, q_o, k_o, v_o, p_o, att_o, u1_o, f_o, pr_o, att_s
-):
-    rb, length, width = tok.shape
+def self_block(x32, bias, mats, vecs, put, att_s):
+    rb, length, width = x32.shape
     n = rb * length
-    x32 = tok[...].astype(F32).reshape(n, width)
+    wq, wk, wv, wo, wc = mats
+    qb, vb, ob, g1, b1, pb = vecs
+    x32 = x32.reshape(n, width)
     x = x32.astype(BF)
-    q = (nn(x, wq[...]) + qb[...]).astype(BF)
-    k = nn(x, wk[...]).astype(BF)
-    v = (nn(x, wv[...]) + vb[...]).astype(BF)
-    q_o[...] = q.astype(F32).reshape(rb, length, width).astype(BF)
-    k_o[...] = k.astype(F32).reshape(rb, length, width).astype(BF)
-    v_o[...] = v.astype(F32).reshape(rb, length, width).astype(BF)
+    q_o, k_o, v_o, p_o = put("q"), put("k"), put("v"), put("p")
+    q_o[...] = (nn(x, wq()) + qb).reshape(rb, length, width).astype(BF)
+    k_o[...] = nn(x, wk()).reshape(rb, length, width).astype(BF)
+    v_o[...] = (nn(x, wv()) + vb).reshape(rb, length, width).astype(BF)
 
     def row(r, carry):
         qr = q_o[r].astype(F32) * 0.125
         kr = k_o[r].astype(F32)
         vr = v_o[r].astype(F32)
-        outs = []
+        kws = [window(kr, i).astype(BF) for i in range(4)]
+        vws = [window(vr, i).astype(BF) for i in range(4)]
+        qss = [stack_heads(qr, i) for i in range(4)]
+        mask = bias[r]
+        scores = [nt(kws[i], qss[i]) + mask for i in range(4)]
+        ps = [column_softmax(st) for st in scores]
+        outs = [tn(ps[i], vws[i]) for i in range(4)]
         for i in range(4):
-            base = WINDOWS[i][0]
-            qs = stack_heads(qr, i)
-            kw = kr[:, base : base + 256].astype(BF)
-            vw = vr[:, base : base + 256].astype(BF)
-            st = nt(kw, qs) + bias[r]
-            top = jnp.max(st, 0, keepdims=True)
-            e = jnp.exp(st - top)
-            p = (e * (1.0 / jnp.sum(e, 0, keepdims=True))).astype(BF)
-            p_o[r, i] = p
-            outs.append(unstack_heads(tn(p, vw), i, length))
-        att_s[r] = join_windows(outs)
+            p_o[r, i] = ps[i]
+        att_s[r] = join_windows([unstack_heads(outs[i], i, length) for i in range(4)])
         return carry
 
     lax.fori_loop(0, rb, row, 0)
     att32 = att_s[...]
-    att_o[...] = att32.astype(BF)
+    put("att")[...] = att32.astype(BF)
     att = att32.reshape(n, width).astype(BF)
-    u1 = x32 + nn(att, wo[...]) + ob[...]
-    u1_o[...] = u1.reshape(rb, length, width)
+    u1 = x32 + nn(att, wo()) + ob
+    put("u1")[...] = u1.reshape(rb, length, width)
     xhat, _ = norm_parts(u1)
-    first = (xhat * g1[...] + b1[...]).astype(BF)
-    f_o[...] = first.astype(F32).reshape(rb, length, width).astype(BF)
-    pr_o[...] = (nn(first, wc[...]) + pb[...]).reshape(rb, length, width).astype(BF)
-
-
-def cross_forward(starts, order, pat, wp, wk, wv, pab, cb, probe, pr_o, k_o, v_o, p_o, mix_o, pat_s):
+    first32 = xhat * g1 + b1
+    put("first")[...] = first32.reshape(rb, length, width).astype(BF)
+    put("probe")[...] = (nn(first32.astype(BF), wc()) + pb).reshape(rb, length, width).astype(BF)
+
+
+SELF_OUTS = ("q", "k", "v", "p", "att", "u1", "first", "probe")
+
+
+def self_forward(
+    tok, bias, wq, wk, wv, wo, wc, qb, vb, ob, g1, b1, pb, q_o, k_o, v_o, p_o, att_o, u1_o, f_o, pr_o, att_s
+):
+    outs = dict(zip(SELF_OUTS, (q_o, k_o, v_o, p_o, att_o, u1_o, f_o, pr_o)))
+    mats = [lambda ref=ref: ref[...] for ref in (wq, wk, wv, wo, wc)]
+    vecs = [ref[...] for ref in (qb, vb, ob, g1, b1, pb)]
+    self_block(tok[...].astype(F32), bias, mats, vecs, lambda name: outs[name], att_s)
+
+
+def cross_forward(starts, order, proj, wk, wv, cb, probe, k_o, v_o, p_o, mix_o, pr_s):
     i = pl.program_id(0)
-    points = pat.shape[1]
+    points = proj.shape[1]
     length = probe.shape[1]
 
     @pl.when(i == 0)
     def _():
-        pat_s[...] = jnp.zeros_like(pat_s)
+        pr_s[...] = jnp.zeros_like(pr_s)
 
     lo, hi = starts[i], starts[i + 1]
 
     @pl.when(hi > lo)
     def _():
-        pat_s[0:points, :] = pat[0]
-        pr = (nn(pat_s[...], wp[...]) + pab[...]).astype(BF)
-        pr_o[0] = pr
+        pr_s[0:points, :] = proj[0]
+        pr = pr_s[...]
         k_o[0] = nn(pr, wk[...]).astype(BF)
         v_o[0] = (nn(pr, wv[...]) + cb[...]).astype(BF)
 
         def row(j, carry):
             r = order[j]
             qr = probe[r].astype(F32) * 0.125
-            outs = []
+            qss = [stack_heads(qr, g) for g in range(4)]
+            scores = [nt(k_o[0, :, WINDOWS[g][0] : WINDOWS[g][0] + 256], qss[g]) for g in range(4)]
+            point = lax.broadcasted_iota(jnp.int32, scores[0].shape, 0)
+            ps = [column_softmax(jnp.where(point < points, st, -1e30)) for st in scores]
+            outs = [tn(ps[g], v_o[0, :, WINDOWS[g][0] : WINDOWS[g][0] + 256]) for g in range(4)]
             for g in range(4):
-                base = WINDOWS[g][0]
-                qs = stack_heads(qr, g)
-                st = nt(k_o[0, :, base : base + 256], qs)
-                point = lax.broadcasted_iota(jnp.int32, st.shape, 0)
-                st = jnp.where(point < points, st, -1e30)
-                top = jnp.max(st, 0, keepdims=True)
-                e = jnp.exp(st - top)
-                p = (e * (1.0 / jnp.sum(e, 0, keepdims=True))).astype(BF)
-                p_o[r, g] = p
-                outs.append(unstack_heads(tn(p, v_o[0, :, base : base + 256]), g, length))
-            mix_o[r] = join_windows(outs).astype(BF)
+                p_o[r, g] = ps[g]
+            mix_o[r] = join_windows([unstack_heads(outs[g], g, length) for g in range(4)]).astype(BF)
             return carry
 
         lax.fori_loop(lo, hi, row, 0)
@@ -266,20 +282,19 @@
 
 
 def cross_backward(
-    starts, order, pat, proj, keys, values, wk, wv, probe, grad, probs,
-    dpr_o, dproj_o, dwk_o, dwv_o, dwp_o, dcb_o,
-    pat_s, dk_s, dv_s, dwk_s, dwv_s, dwp_s,
+    starts, order, proj, keys, values, wk, wv, probe, grad, probs,
+    dpr_o, dproj_o, dwk_o, dwv_o, dcb_o,
+    pr_s, dk_s, dv_s, dwk_s, dwv_s,
 ):
     i = pl.program_id(0)
-    points = pat.shape[1]
+    points = proj.shape[1]
     length = probe.shape[1]
 
     @pl.when(i == 0)
     def _():
-        pat_s[...] = jnp.zeros_like(pat_s)
+        pr_s[...] = jnp.zeros_like(pr_s)
         dwk_s[...] = jnp.zeros_like(dwk_s)
         dwv_s[...] = jnp.zeros_like(dwv_s)
-        dwp_s[...] = jnp.zeros_like(dwp_s)
         dcb_o[...] = jnp.zeros_like(dcb_o)
 
     lo, hi = starts[i], starts[i + 1]
@@ -297,25 +312,22 @@
             r = order[j]
             qr = probe[r].astype(F32) * 0.125
             gr = grad[r].astype(F32)
-            outs = []
-            for g in range(4):
-                base = WINDOWS[g][0]
-                qs = stack_heads(qr, g)
-                gs = stack_heads(gr, g)
-                pb = probs[r, g]
-                p = pb.astype(F32)
-                dp = nt(values[0, :, base : base + 256], gs)
-                w = jnp.sum(dp * p, 0, keepdims=True)
-                ds = (p * (dp - w)).astype(BF)
-                dk_s[:, base : base + 256] += nn(ds, qs)
-                dv_s[:, base : base + 256] += nn(pb, gs)
-                outs.append(unstack_heads(tn(ds, keys[0, :, base : base + 256]), g, length))
-            dpr_o[r] = (join_windows(outs) * 0.125).astype(BF)
+            gss = [stack_heads(gr, g) for g in range(4)]
+            dps = [nt(values[0, :, WINDOWS[g][0] : WINDOWS[g][0] + 256], gss[g]) for g in range(4)]
+            qss = [stack_heads(qr, g) for g in range(4)]
+            pbs = [probs[r, g] for g in range(4)]
+            dvs = [nn(pbs[g], gss[g]) for g in range(4)]
+            dss = [score_grads(pbs[g], dps[g]) for g in range(4)]
+            dks = [nn(dss[g], qss[g]) for g in range(4)]
+            outs = [tn(dss[g], keys[0, :, WINDOWS[g][0] : WINDOWS[g][0] + 256]) for g in range(4)]
+            dv_s[...] += join_windows(dvs)
+            dk_s[...] += join_windows(dks)
+            dpr_o[r] = (join_windows([unstack_heads(outs[g], g, length) for g in range(4)]) * 0.125).astype(BF)
             return carry
 
         lax.fori_loop(lo, hi, row, 0)
-        pat_s[0:points, :] = pat[0]
-        pr = proj[0]
+        pr_s[0:points, :] = proj[0]
+        pr = pr_s[...]
         dk = dk_s[...].astype(BF)
         dv = dv_s[...].astype(BF)
         dcb_o[0:1] += jnp.sum(dv.astype(F32), 0, keepdims=True)
@@ -323,14 +335,11 @@
         dproj_o[0] = dproj[0:points]
         dwk_s[...] += tn(pr, dk)
         dwv_s[...] += tn(pr, dv)
-        dwp_s[...] += tn(pat_s[...], dproj)
-        dcb_o[1:2] += jnp.sum(dproj.astype(F32), 0, keepdims=True)
 
     @pl.when(i == pl.num_programs(0) - 1)
     def _():
         dwk_o[...] = dwk_s[...].astype(BF)
         dwv_o[...] = dwv_s[...].astype(BF)
-        dwp_o[...] = dwp_s[...].astype(BF)
 
 
 def self_backward(
@@ -370,22 +379,17 @@
         kr = k[r].astype(F32)
         vr = v[r].astype(F32)
         gr = ga_s[r]
-        dqs, dks, dvs = [], [], []
-        for i in range(4):
-            base = WINDOWS[i][0]
-            qs = stack_heads(qr, i)
-            gs = stack_heads(gr, i)
-            kw = kr[:, base : base + 256].astype(BF)
-            vw = vr[:, base : base + 256].astype(BF)
-            pb = probs[r, i]
-            p = pb.astype(F32)
-            dp = nt(vw, gs)
-            w = jnp.sum(dp * p, 0, keepdims=True)
-            ds = (p * (dp - w)).astype(BF)
-            dks.append(nn(ds, qs))
-            dvs.append(nn(pb, gs))
-            dqs.append(unstack_heads(tn(ds, kw), i, length))
-        dq_s[r] = join_windows(dqs) * 0.125
+        gss = [stack_heads(gr, i) for i in range(4)]
+        vws = [window(vr, i).astype(BF) for i in range(4)]
+        dps = [nt(vws[i], gss[i]) for i in range(4)]
+        qss = [stack_heads(qr, i) for i in range(4)]
+        kws = [window(kr, i).astype(BF) for i in range(4)]
+        pbs = [probs[r, i] for i in range(4)]
+        dvs = [nn(pbs[i], gss[i]) for i in range(4)]
+        dss = [score_grads(pbs[i], dps[i]) for i in range(4)]
+        dks = [nn(dss[i], qss[i]) for i in range(4)]
+        outs = [tn(dss[i], kws[i]) for i in range(4)]
+        dq_s[r] = join_windows([unstack_heads(outs[i], i, length) for i in range(4)]) * 0.125
         dk_s[r] = join_windows(dks)
         dv_s[r] = join_windows(dvs)
         return carry
@@ -450,14 +454,18 @@
     def __init__(self, send, recv, local):
         self.send, self.recv, self.local = send, recv, local
         self.far = self.near = 0
-
-    def remote(self, src, dst, device):
+        self.sent = []
+
+    def prepare(self, src, dst, device):
         i = self.far
         self.far += 1
-        copy = pltpu.make_async_remote_copy(
+        return pltpu.make_async_remote_copy(
             src_ref=src, dst_ref=dst, send_sem=self.send.at[i], recv_sem=self.recv.at[i],
             device_id=device, device_id_type=pl.DeviceIdType.MESH,
         )
+
+    def remote(self, src, dst, device):
+        copy = self.prepare(src, dst, device)
         copy.start()
         return copy
 
@@ -482,68 +490,185 @@
             pass
 
 
-def gather_kernel(parts, w_in, p_in, w_out, p_out, send, recv, local):
-    z, y, x, c = my_place()
-    meet(z, y, x, c)
-    copies = Copies(send, recv, local)
-
-    def slabs(lo, n):
-        pick = pl.ds(lo, n)
-        mine = w_out.at[pick, z, y, x, c]
-        pending = [copies.here(w_in.at[pick], mine)]
-        pending += [
-            copies.remote(w_in.at[pick], mine, device_at((z + k) % 4, y, x, c)) for k in (1, 3, 2)
-        ]
-        yield
-        arrived(pending)
-        line = w_out.at[pick, :, y, x, c]
-        step = copies.remote(line, line, device_at(z, 1 - y, x, c))
-        yield
-        step.wait()
-        plane = w_out.at[pick, :, :, x, c]
-        step = copies.remote(plane, plane, device_at(z, y, 1 - x, c))
-        yield
-        step.wait()
-        half = w_out.at[pick, :, :, :, c]
-        step = copies.remote(half, half, device_at(z, y, x, 1 - c))
-        yield
-        step.wait()
-
-    def image(i):
-        mine = p_out.at[z, y, i]
-        pending = [copies.here(p_in.at[i], mine)]
-        pending += [
-            copies.remote(p_in.at[i], mine, device_at((z + k) % 4, y, x, c)) for k in (1, 3, 2)
-        ]
-        yield
-        arrived(pending)
-        line = p_out.at[:, y, i]
-        step = copies.remote(line, line, device_at(z, 1 - y, x, c))
-        yield
-        step.wait()
-
-    jobs = {}
-    for j, (lo, n) in enumerate(parts):
-        jobs["w%d" % j] = slabs(lo, n)
-    for i in range(p_in.shape[0]):
-        jobs["p%d" % i] = image(i)
-    drive(jobs, ["w0", "p0", "w1", "p1", "p2", "p3", "w0", "p0", "w0", "w1", "w0", "p1", "w1", "p2", "w1", "p3"])
-
-
-def reduce_kernel(
-    parts, w_in, p_in, w_out, p_out, acc, rc, rx, ry, rz, pacc, pry, prz, send, recv, local
+PATCH, EXTRA, QUERY, KEY, VALUE, OUT, CQ, CK, W1 = range(9)
+W2, CV, CO = 12, 16, 17
+
+
+FRONT_ORDER = (
+    "P", "Q", "P", "P", "Q", "P", "Q", "R", "P", "P", "P", "F", "Q", "P", "Q", "Q", "F", "P",
+    "weights", "F", "i0", "i1", "Q", "F", "i0", "i3", "G", "F", "R", "i1", "i3", "Q", "G", "G",
+    "i0", "i0", "F", "Q", "self", "i2", "i3", "G", "self", "R", "i2", "F", "G", "self", "i3", "i1",
+    "G", "self", "G", "R", "R", "i1", "F", "i2", "self", "R", "R", "G", "i2", "R",
+)
+REDUCE_ORDER = (
+    "p0", "p1", "w0", "p2", "p3", "w1", "p0", "w0", "p1", "p2", "w0", "p3", "p0", "p1", "w1", "p2",
+    "p3", "v", "w0", "w1", "v", "w0", "v", "w1", "v",
+)
+
+
+def front_kernel(
+    parts, tails, nv, rb, w_in, pat, tok, bias, w_out, p_out, q_o, k_o, v_o, pr_o, att_o, u1_o, f_o, prb_o, vec_o,
+    pw, ex, wm, proj_s, q_s, k_s, v_s, pr_s, att_b, u1_s, f_s, prb_s, att_s, send, recv, local,
 ):
     z, y, x, c = my_place()
     meet(z, y, x, c)
     copies = Copies(send, recv, local)
+    rows, length, width = tok.shape
+    images = pat.shape[0]
+
+    inner = (z + 1) % 4 >= 2
+    partner = z + 1 - 2 * (z % 2)
+    across = 3 - z
+    ours, theirs = 2 * (z // 2), 2 - 2 * (z // 2)
+
+    def along_z(source, view, tell, local):
+        step = copies.remote(source, view(z, 0), device_at(partner, y, x, c))
+        tell("own")
+        yield
+        step.wait()
+        if local is not None:
+            local.wait()
+        tell("partner")
+        middle = copies.prepare(view(ours, 2), view(ours, 2), device_at(across, y, x, c))
+        outward = copies.prepare(view(theirs, 2), view(theirs, 2), device_at(partner, y, x, c))
+
+        @pl.when(inner)
+        def _():
+            middle.start()
+
+        yield
+
+        @pl.when(inner)
+        def _():
+            middle.wait()
+            outward.start()
+            tell("inner")
+
+        yield
+
+        @pl.when(jnp.logical_not(inner))
+        def _():
+            outward.wait_recv()
+            tell("outer")
+
+        copies.sent.append((inner, outward))
+        yield
+
+    def exchanged(source, view, local):
+        own = copies.prepare(source, view(z, 0), device_at(z, 1 - y, x, c))
+        second = copies.prepare(view(partner, 0), view(partner, 0), device_at(z, 1 - y, x, c))
+        third = copies.prepare(view(theirs, 2), view(theirs, 2), device_at(z, 1 - y, x, c))
+        start = {"own": own, "partner": second, "inner": third, "outer": third}
+        return along_z(source, view, lambda which: start[which].start(), local), (own, second, third)
+
+    def slabs(lo, n):
+        pick = pl.ds(lo, n)
+
+        def view(at, many):
+            return w_out.at[pick, pl.ds(at, many) if many else at, y, x, c]
+
+        def plane(at, many):
+            return w_out.at[pick, pl.ds(at, many) if many else at, :, x, c]
+
+        local = copies.here(w_in.at[pick], view(z, 0))
+        moving, (own, second, third) = exchanged(w_in.at[pick], view, None)
+        next(moving)
+        yield
+        own.wait()
+        local.wait()
+        steps = [copies.remote(plane(z, 0), plane(z, 0), device_at(z, y, 1 - x, c))]
+        yield
+        for _ in range(3):
+            next(moving)
+            yield
+        second.wait()
+        steps.append(copies.remote(plane(partner, 0), plane(partner, 0), device_at(z, y, 1 - x, c)))
+        yield
+        third.wait()
+        steps.append(copies.remote(plane(theirs, 2), plane(theirs, 2), device_at(z, y, 1 - x, c)))
+        yield
+        arrived(steps)
+        half = w_out.at[pick, :, :, :, c]
+        step = copies.remote(half, half, device_at(z, y, x, 1 - c))
+        yield
+        step.wait()
+
+    def patch_weights():
+        rest = pw.shape[4] - tails
+        arrived(
+            [
+                copies.here(w_out.at[PATCH], pw.at[:, :, :, :, 0:rest]),
+                copies.here(w_out.at[EXTRA, :, :, :, :, 0:tails], pw.at[:, :, :, :, rest:]),
+                copies.here(w_out.at[EXTRA], ex),
+            ]
+        )
+        total = jnp.zeros(ex.shape[4:], F32)
+        for zz in range(4):
+            for yy in range(2):
+                for xx in range(2):
+                    for cc in range(2):
+                        total = total + ex[zz, yy, xx, cc].astype(F32)
+        vec_o[...] = total
+        yield
+
+    def vec(j):
+        return vec_o[tails + j : tails + j + 1, :]
+
+    def image(i):
+        full = pw[...].reshape(pat.shape[2], width)
+        proj_s[i] = (nn(pat[i], full) + vec(5)).astype(BF)
+
+        def view(at, many):
+            return p_out.at[pl.ds(at, many) if many else at, y, i]
+
+        moving, steps = exchanged(proj_s.at[i], view, copies.here(proj_s.at[i], view(z, 0)))
+        yield from moving
+        arrived(steps)
+
+    def attention():
+        arrived([copies.here(w_out.at[QUERY + m], wm.at[m]) for m in range(5)])
+        yield
+        scratch = dict(zip(SELF_OUTS, (q_s, k_s, v_s, pr_s, att_b, u1_s, f_s, prb_s)))
+        finals = dict(zip(SELF_OUTS, (q_o, k_o, v_o, pr_o, att_o, u1_o, f_o, prb_o)))
+        mats = [lambda m=m: wm[m].reshape(width, width) for m in range(5)]
+        outgoing = []
+        for b in range(rows // rb):
+            pick = pl.ds(b * rb, rb)
+            self_block(
+                tok[pick].astype(F32), bias.at[pick], mats, [vec(j) for j in (0, 1, 2, 3, 4, 6)],
+                lambda name: scratch[name].at[pick], att_s,
+            )
+            outgoing += [copies.here(scratch[name].at[pick], finals[name].at[pick]) for name in SELF_OUTS]
+            yield
+        arrived(outgoing)
+
+    jobs = {name: slabs(lo, n) for name, (lo, n) in parts.items()}
+    jobs["weights"] = patch_weights()
+    for i in range(images):
+        jobs["i%d" % i] = image(i)
+    jobs["self"] = attention()
+    drive(jobs, FRONT_ORDER)
+    for when, copy in copies.sent:
+
+        @pl.when(when)
+        def _(copy=copy):
+            copy.wait_send()
+
+
+def reduce_kernel(
+    parts, w_in, p_in, pat, vb_in, w_out, p_out, acc, rc, rx, ry, rz, pacc, pry, prz, dwp, pv, send, recv, local
+):
+    z, y, x, c = my_place()
+    meet(z, y, x, c)
+    copies = Copies(send, recv, local)
 
     def up(ref, *at):
         return ref[at].astype(F32)
 
-    def slabs(lo, n):
+    def slabs(lo, n, src):
         pick = pl.ds(lo, n)
-        own = copies.here(w_in.at[pick, :, :, :, c], acc.at[pick])
-        step = copies.remote(w_in.at[pick, :, :, :, 1 - c], rc.at[pick], device_at(z, y, x, 1 - c))
+        own = copies.here(src.at[:, :, :, :, c], acc.at[pick])
+        step = copies.remote(src.at[:, :, :, :, 1 - c], rc.at[pick], device_at(z, y, x, 1 - c))
         yield
         own.wait()
         step.wait()
@@ -614,16 +739,38 @@
         p_out[i] = (
             up(pacc, i, z) + up(pry, i, z) + up(prz, 0, i) + up(prz, 1, i) + up(prz, 2, i)
         ).astype(BF)
+        yield
+
+    def patch_grads(first):
+        sr, width = w_out.shape[1:]
+        images = p_in.shape[2]
+        total = tn(pat[0], p_out[0])
+        bias = jnp.sum(p_out[0].astype(F32), 0, keepdims=True)
+        for i in range(1, images):
+            total = total + tn(pat[i], p_out[i])
+            bias = bias + jnp.sum(p_out[i].astype(F32), 0, keepdims=True)
+        dwp[...] = total.reshape(dwp.shape)
+
+        def fill(d, carry):
+            zz, yy, xx, cc = d // 8, (d // 4) % 2, (d // 2) % 2, d % 2
+            rows = dwp[d]
+            pv[0, zz, yy, xx, cc] = rows[:sr].astype(BF)
+            block = vb_in[d]
+            row = lax.broadcasted_iota(jnp.int32, block.shape, 0)
+            block = jnp.where(row == 5, bias, block)
+            pv[1, zz, yy, xx, cc] = jnp.concatenate([rows[sr:], block], 0).astype(BF)
+            return carry
+
+        lax.fori_loop(0, 32, fill, 0)
+        yield from slabs(first, 2, pv)
 
     jobs = {}
     for i in range(p_in.shape[2]):
         jobs["p%d" % i] = image(i)
     for j, (lo, n) in enumerate(parts):
-        jobs["w%d" % j] = slabs(lo, n)
-    drive(
-        jobs,
-        ["w0", "p0", "p1", "w1", "p2", "p3", "w0", "w1", "p0", "w0", "p1", "w1", "p2", "w0", "p3", "w1"],
-    )
+        jobs["w%d" % j] = slabs(lo, n, w_in.at[pl.ds(lo, n)])
+    jobs["v"] = patch_grads(w_in.shape[0])
+    drive(jobs, REDUCE_ORDER)
 
 
 def split_slabs(count):
@@ -631,59 +778,80 @@
     return ((0, first), (first, count - first))
 
 
-def gather_all(slabs, patches):
+def front(slabs, patches, tokens, bias, tails, nv):
     n, sr, width = slabs.shape
     images, points, pwidth = patches.shape
-    parts = split_slabs(n)
-    copies = 6 * len(parts) + 4 * images
-    w_all, p_all = pl.pallas_call(
-        functools.partial(gather_kernel, parts),
-        in_specs=[pl.BlockSpec(memory_space=pl.ANY)] * 2,
-        out_specs=[pl.BlockSpec(memory_space=pl.ANY)] * 2,
-        out_shape=[sds((n, 4, 2, 2, 2, sr, width), BF), sds((4, 2, images, points, pwidth), BF)],
+    rows, length, _ = tokens.shape
+    rb = 8 if rows % 8 == 0 else 1
+    parts = {"P": (PATCH, 2), "Q": (QUERY, 6), "F": (W1, 4), "G": (W2, 4), "R": (CV, 2)}
+    remote = 10 * len(parts) + 6 * images
+    near = len(parts) + images + 3 + 5 + len(SELF_OUTS) * (rows // rb)
+    tok_sh = (rows, length, width)
+    probs = (rows, 4, length, 3 * length)
+    kept = [sds(tok_sh, BF), sds(tok_sh, BF), sds(tok_sh, BF), sds(probs, BF), sds(tok_sh, BF), sds(tok_sh, F32), sds(tok_sh, BF), sds(tok_sh, BF)]
+    hbm = pl.BlockSpec(memory_space=pl.ANY)
+    vmem = pl.BlockSpec(memory_space=pltpu.VMEM)
+    w_all, p_all, *rest = pl.pallas_call(
+        functools.partial(front_kernel, parts, tails, nv, rb),
+        in_specs=[hbm, vmem, vmem, vmem],
+        out_specs=[hbm] * 10 + [vmem],
+        out_shape=[
+            sds((n, 4, 2, 2, 2, sr, width), BF), sds((4, 2, images, points, width), BF), *kept, sds((sr, width), F32),
+        ],
         scratch_shapes=[
-            pltpu.SemaphoreType.DMA((copies,)),
-            pltpu.SemaphoreType.DMA((copies,)),
-            pltpu.SemaphoreType.DMA((len(parts) + images,)),
+            pltpu.VMEM((4, 2, 2, 2, pwidth // 32, width), BF),
+            pltpu.VMEM((4, 2, 2, 2, sr, width), BF),
+            pltpu.VMEM((5, 4, 2, 2, 2, sr, width), BF),
+            pltpu.VMEM((images, points, width), BF),
+            *[pltpu.VMEM(item.shape, item.dtype) for item in kept],
+            pltpu.VMEM((rb, length, width), F32),
+            pltpu.SemaphoreType.DMA((remote,)),
+            pltpu.SemaphoreType.DMA((remote,)),
+            pltpu.SemaphoreType.DMA((near,)),
         ],
         compiler_params=pltpu.CompilerParams(
-            collective_id=0, has_side_effects=True, vmem_limit_bytes=8 * 1024 * 1024
+            collective_id=0, has_side_effects=True, vmem_limit_bytes=58 * 1024 * 1024
         ),
-        name="gather_all",
-    )(slabs, patches)
-    return w_all.reshape(n, 32 * sr, width), p_all.reshape(8 * images, points, pwidth)
-
-
-def reduce_all(slabs, grads):
+        name="front",
+    )(slabs, patches, tokens, bias)
+    return w_all.reshape(n, 32 * sr, width), p_all.reshape(8 * images, points, width), rest[:8], rest[8]
+
+
+def reduce_all(slabs, grads, patches, vec_block):
     n, full, width = slabs.shape
     sr = full // 32
     total, points, _ = grads.shape
-    images = total // 8
+    images, _, pwidth = patches.shape
     parts = split_slabs(n)
-    copies = 6 * len(parts) + 4 * images
+    copies = 6 * (len(parts) + 1) + 4 * images
+    hbm = pl.BlockSpec(memory_space=pl.ANY)
+    vmem = pl.BlockSpec(memory_space=pltpu.VMEM)
+    m = n + 2
     w_shard, p_shard = pl.pallas_call(
         functools.partial(reduce_kernel, parts),
-        in_specs=[pl.BlockSpec(memory_space=pl.ANY)] * 2,
-        out_specs=[pl.BlockSpec(memory_space=pltpu.VMEM)] * 2,
-        out_shape=[sds((n, sr, width), F32), sds((images, points, width), BF)],
+        in_specs=[hbm, hbm, vmem, vmem],
+        out_specs=[vmem] * 2,
+        out_shape=[sds((m, sr, width), F32), sds((images, points, width), BF)],
         scratch_shapes=[
-            pltpu.VMEM((n, 4, 2, 2, sr, width), BF),
-            pltpu.VMEM((n, 4, 2, 2, sr, width), BF),
-            pltpu.VMEM((n, 4, 2, sr, width), BF),
-            pltpu.VMEM((n, 4, sr, width), BF),
-            pltpu.VMEM((3, n, sr, width), BF),
+            pltpu.VMEM((m, 4, 2, 2, sr, width), BF),
+            pltpu.VMEM((m, 4, 2, 2, sr, width), BF),
+            pltpu.VMEM((m, 4, 2, sr, width), BF),
+            pltpu.VMEM((m, 4, sr, width), BF),
+            pltpu.VMEM((3, m, sr, width), BF),
             pltpu.VMEM((images, 4, points, width), BF),
             pltpu.VMEM((images, 4, points, width), BF),
             pltpu.VMEM((3, images, points, width), BF),
+            pltpu.VMEM((32, pwidth // 32, width), F32),
+            pltpu.VMEM((2, 4, 2, 2, 2, sr, width), BF),
             pltpu.SemaphoreType.DMA((copies,)),
             pltpu.SemaphoreType.DMA((copies,)),
-            pltpu.SemaphoreType.DMA((len(parts) + images,)),
+            pltpu.SemaphoreType.DMA((len(parts) + 1 + images,)),
         ],
         compiler_params=pltpu.CompilerParams(
-            collective_id=1, has_side_effects=True, vmem_limit_bytes=56 * 1024 * 1024
+            collective_id=1, has_side_effects=True, vmem_limit_bytes=58 * 1024 * 1024
         ),
         name="reduce_all",
-    )(slabs.reshape(n, 4, 2, 2, 2, sr, width), grads.reshape(4, 2, images, points, width))
+    )(slabs.reshape(n, 4, 2, 2, 2, sr, width), grads.reshape(4, 2, images, points, width), patches, vec_block)
     return w_shard, p_shard
 
 
@@ -723,28 +891,19 @@
     er = max(sr, extra.shape[0])
     own_rows = er == sr and groups == 8 and shards == 32
     extra = jnp.pad(extra, ((0, er - extra.shape[0]), (0, 0)))
-    mats = [self_query, self_key, self_value, self_output, cross_query, cross_key, cross_value, cross_output, patch_proj[:sr]]
-    if own_rows:
-        w_a, patches_all = gather_all(jnp.stack(mats + [extra]), patches)
-        extra_all = w_a[len(mats)].reshape(shards, er, width)
-    else:
-        w_a = gather(jnp.stack(mats), 1)
-        extra_all = gather(extra, 0).reshape(shards, er, width)
-        patches_all = lax.all_gather(patches, "dp", axis=0, tiled=True)
-    vec_all = jnp.sum(extra_all[:, tails : tails + nv].astype(F32), 0)
-    (qb, vb, ob, g1, b1, pab, prb, cob, crb, g2, s2, nab, g3, s3) = [vec_all[j : j + 1] for j in range(nv)]
-    wb = extra_all[:, tails + nv, :wr].astype(F32)
-    wb = wb.reshape(shards, chunks, sr).transpose(1, 0, 2).reshape(chunks, 1, width)
-    patch_full = jnp.concatenate(
-        [w_a[len(mats) - 1].reshape(shards, sr, width), extra_all[:, :tails]], 1
-    ).reshape(shards * pr, width)
-
     widen_slabs = widen_weight.reshape(sr, shards, chunks, sr).transpose(2, 0, 1, 3).reshape(chunks, sr, width)
     narrow_slabs = narrow_weight.reshape(chunks, sr, width)
-    w_b_in = jnp.concatenate([widen_slabs, narrow_slabs], 0)
-    if own_rows:
-        w_b_in, w_a = lax.optimization_barrier((w_b_in, w_a))
-    w_b = gather(w_b_in, 1)
+    slabs_in = jnp.concatenate(
+        [
+            jnp.stack(
+                [
+                    patch_proj[:sr], extra[:sr], self_query, self_key, self_value, self_output,
+                    cross_query, cross_key,
+                ]
+            ),
+            widen_slabs, narrow_slabs, jnp.stack([cross_value, cross_output]),
+        ]
+    )
 
     image = owner * images + image_slot
     idx = jnp.arange(rows, dtype=jnp.int32)
@@ -768,46 +927,64 @@
     vspec = whole((1, width))
     tb = rows_block(tok_sh, rb)
     self_p = (rows, 4, length, 3 * length)
-    q, k, v, probs, attended, u1, first_low, probe = pl.pallas_call(
-        self_forward,
-        grid=grid,
-        in_specs=[tb, rows_block((rows, length, 3 * length), rb)]
-        + [wspec(0), wspec(1), wspec(2), wspec(3), wspec(4)]
-        + [vspec] * 6,
-        out_specs=[tb, tb, tb, rows_block(self_p, rb), tb, tb, tb, tb],
-        out_shape=[
-            sds(tok_sh, BF), sds(tok_sh, BF), sds(tok_sh, BF), sds(self_p, BF),
-            sds(tok_sh, BF), sds(tok_sh, F32), sds(tok_sh, BF), sds(tok_sh, BF),
-        ],
-        scratch_shapes=[pltpu.VMEM((rb, length, width), F32)],
-        compiler_params=params(48),
-        cost_estimate=cost(11 * rows * length * width * width, 30e6),
-        name="self_forward",
-    )(tokens, bias, w_a, w_a, w_a, w_a, w_a, qb, vb, ob, g1, b1, prb)
+    if own_rows:
+        w_a, proj_all, kept, vec_all = front(slabs_in, patches, tokens, bias, tails, nv)
+        vec_all = vec_all[tails : tails + nv]
+        extra_all = w_a[EXTRA].reshape(shards, er, width)
+    else:
+        w_a = gather(slabs_in, 1)
+        extra_all = gather(extra, 0).reshape(shards, er, width)
+        vec_all = jnp.sum(extra_all[:, tails : tails + nv].astype(F32), 0)
+    (qb, vb, ob, g1, b1, pab, prb, cob, crb, g2, s2, nab, g3, s3) = [vec_all[j : j + 1] for j in range(nv)]
+    wb = extra_all[:, tails + nv, :wr].astype(F32)
+    wb = wb.reshape(shards, chunks, sr).transpose(1, 0, 2).reshape(chunks, 1, width)
+    patch_full = jnp.concatenate([w_a[PATCH].reshape(shards, sr, width), extra_all[:, :tails]], 1)
+    patch_full = patch_full.reshape(shards * pr, width)
+    if not own_rows:
+        projected = lax.dot_general(patches, patch_full, (((2,), (0,)), ((), ())), preferred_element_type=F32)
+        proj_all = lax.all_gather((projected + pab).astype(BF), "dp", axis=0, tiled=True)
+        kept = pl.pallas_call(
+            self_forward,
+            grid=grid,
+            in_specs=[tb, rows_block((rows, length, 3 * length), rb)]
+            + [wspec(j) for j in (QUERY, KEY, VALUE, OUT, CQ)]
+            + [vspec] * 6,
+            out_specs=[tb, tb, tb, rows_block(self_p, rb), tb, tb, tb, tb],
+            out_shape=[
+                sds(tok_sh, BF), sds(tok_sh, BF), sds(tok_sh, BF), sds(self_p, BF),
+                sds(tok_sh, BF), sds(tok_sh, F32), sds(tok_sh, BF), sds(tok_sh, BF),
+            ],
+            scratch_shapes=[pltpu.VMEM((rb, length, width), F32)],
+            compiler_params=params(48),
+            cost_estimate=cost(11 * rows * length * width * width, 30e6),
+            name="self_forward",
+        )(tokens, bias, w_a, w_a, w_a, w_a, w_a, qb, vb, ob, g1, b1, prb)
+    q, k, v, probs, attended, u1, first_low, probe = kept
 
     padded = -(-points // 16) * 16
     kv_sh = (total_images, padded, width)
     cross_p = (rows, 4, padded, 3 * length)
-    img_spec = pl.BlockSpec((1, points, pwidth), lambda i, *_: (i, 0, 0))
-    grad_spec = pl.BlockSpec((1, points, width), lambda i, *_: (i, 0, 0))
+    img_spec = pl.BlockSpec((1, points, width), lambda i, *_: (i, 0, 0))
     kv_spec = pl.BlockSpec((1, padded, width), lambda i, *_: (i, 0, 0))
-    projected, image_keys, image_values, cprobs, mixed = pl.pallas_call(
+    image_keys, image_values, cprobs, mixed = pl.pallas_call(
         cross_forward,
         grid_spec=pltpu.PrefetchScalarGridSpec(
             num_scalar_prefetch=2,
             grid=(total_images,),
-            in_specs=[img_spec, whole(patch_full.shape), wspec(5), wspec(6), vspec, vspec, whole(tok_sh)],
-            out_specs=[kv_spec, kv_spec, kv_spec, whole(cross_p), whole(tok_sh)],
-            scratch_shapes=[pltpu.VMEM((padded, pwidth), BF)],
+            in_specs=[img_spec, wspec(CK), wspec(CV), vspec, whole(tok_sh)],
+            out_specs=[kv_spec, kv_spec, whole(cross_p), whole(tok_sh)],
+            scratch_shapes=[pltpu.VMEM((padded, width), BF)],
         ),
-        out_shape=[sds(kv_sh, BF), sds(kv_sh, BF), sds(kv_sh, BF), sds(cross_p, BF), sds(tok_sh, BF)],
+        out_shape=[sds(kv_sh, BF), sds(kv_sh, BF), sds(cross_p, BF), sds(tok_sh, BF)],
         compiler_params=params(48),
         cost_estimate=cost(4 * total_images * points * width * width, 40e6),
         name="cross_forward",
-    )(starts, order, patches_all, patch_full, w_a, w_a, pab, cob, probe)
+    )(starts, order, proj_all, w_a, w_a, cob, probe)
 
     def chunk_w(j):
-        return pl.BlockSpec((chunks, width, width), lambda i, *_: (j, 0, 0), pipeline_mode=pl.Buffered(1))
+        return pl.BlockSpec(
+            (chunks, width, width), lambda i, *_: (W1 // chunks + j, 0, 0), pipeline_mode=pl.Buffered(1)
+        )
 
     n_tok = rows * length
     hid_sh = (chunks, n_tok, width)
@@ -815,7 +992,7 @@
     (output, active, grad_inner, second, gb3, grad_mid, gb2, grad_crossed, vec_t, wb_grad) = pl.pallas_call(
         tail_kernel,
         grid=grid,
-        in_specs=[tb, tb, tb, wspec(7), chunk_w(0), chunk_w(1)]
+        in_specs=[tb, tb, tb, wspec(CO), chunk_w(0), chunk_w(1)]
         + [vspec] * 5
         + [whole((chunks, 1, width))]
         + [vspec] * 3,
@@ -832,35 +1009,34 @@
         compiler_params=params(56),
         cost_estimate=cost(18 * n_tok * width * width + 8 * n_tok * width * hidden, 50e6),
         name="tail",
-    )(u1, mixed, out_grad, w_a, w_b, w_b, g1, b1, crb, g2, s2, wb, nab, g3, s3)
-
-    dprobe, dproj, dwk, dwv, dwp, dcb = pl.pallas_call(
+    )(u1, mixed, out_grad, w_a, w_a, w_a, g1, b1, crb, g2, s2, wb, nab, g3, s3)
+
+    dprobe, dproj, dwk, dwv, dcb = pl.pallas_call(
         cross_backward,
         grid_spec=pltpu.PrefetchScalarGridSpec(
             num_scalar_prefetch=2,
             grid=(total_images,),
-            in_specs=[img_spec, kv_spec, kv_spec, kv_spec, wspec(5), wspec(6), whole(tok_sh), whole(tok_sh), whole(cross_p)],
-            out_specs=[whole(tok_sh), grad_spec, whole(slab), whole(slab), whole((pwidth, width)), whole((8, width))],
+            in_specs=[img_spec, kv_spec, kv_spec, wspec(CK), wspec(CV), whole(tok_sh), whole(tok_sh), whole(cross_p)],
+            out_specs=[whole(tok_sh), img_spec, whole(slab), whole(slab), whole((8, width))],
             scratch_shapes=[
-                pltpu.VMEM((padded, pwidth), BF),
+                pltpu.VMEM((padded, width), BF),
                 pltpu.VMEM((padded, width), F32),
                 pltpu.VMEM((padded, width), F32),
                 pltpu.VMEM((width, width), F32),
                 pltpu.VMEM((width, width), F32),
-                pltpu.VMEM((pwidth, width), F32),
             ],
         ),
-        out_shape=[sds(tok_sh, BF), sds((total_images, points, width), BF), sds(slab, BF), sds(slab, BF), sds((pwidth, width), BF), sds((8, width), F32)],
+        out_shape=[sds(tok_sh, BF), sds((total_images, points, width), BF), sds(slab, BF), sds(slab, BF), sds((8, width), F32)],
         compiler_params=params(56),
         cost_estimate=cost(8 * total_images * points * width * width, 50e6),
         name="cross_backward",
-    )(starts, order, patches_all, projected, image_keys, image_values, w_a, w_a, probe, grad_crossed, cprobs)
+    )(starts, order, proj_all, image_keys, image_values, w_a, w_a, probe, grad_crossed, cprobs)
 
     gb1, dq, dk, dv, tokens_grad, vec_s = pl.pallas_call(
         self_backward,
         grid=grid,
         in_specs=[tb, tb, tb, tb, tb, tb, rows_block(self_p, rb)]
-        + [wspec(0), wspec(1), wspec(2), wspec(3), wspec(4)]
+        + [wspec(j) for j in (QUERY, KEY, VALUE, OUT, CQ)]
         + [vspec],
         out_specs=[tb, tb, tb, tb, tb, whole((8, width))],
         out_shape=[sds(tok_sh, BF)] * 5 + [sds((8, width), F32)],
@@ -881,35 +1057,41 @@
         jnp.concatenate([grad_widen, grad_narrow], 0), AXES, scatter_dimension=1, tiled=True
     ).astype(F32)
 
+    zero_row = jnp.zeros((1, width), F32)
     vec_grads = jnp.concatenate(
         [
-            vec_s[4:5], vec_s[5:6], vec_s[2:3], vec_s[0:1], vec_s[1:2], dcb[1:2], vec_s[3:4], dcb[0:1],
+            vec_s[4:5], vec_s[5:6], vec_s[2:3], vec_s[0:1], vec_s[1:2], zero_row, vec_s[3:4], dcb[0:1],
             vec_t[5:6], vec_t[3:4], vec_t[4:5], vec_t[2:3], vec_t[0:1], vec_t[1:2],
         ]
-    ).astype(BF)
-    wb_flat = wb_grad.reshape(chunks, shards, sr).transpose(1, 0, 2).reshape(shards, 1, wr).astype(BF)
-    dwp = dwp.reshape(shards, pr, width)
-    extra_grad = jnp.concatenate(
+    )
+    wb_flat = wb_grad.reshape(chunks, shards, sr).transpose(1, 0, 2).reshape(shards, 1, wr)
+    vec_block = jnp.concatenate(
         [
-            dwp[:, sr:],
             jnp.broadcast_to(vec_grads[None], (shards, nv, width)),
             jnp.pad(wb_flat, ((0, 0), (0, 0), (0, width - wr))),
-            jnp.zeros((shards, er - tails - nv - 1, width), BF),
+            jnp.zeros((shards, er - tails - nv - 1, width), F32),
         ],
         1,
     )
     slabs = [
         wgrad(tokens, dq), wgrad(tokens, dk), wgrad(tokens, dv), wgrad(attended, gb1),
-        wgrad(first_low, dprobe), dwk, dwv, wgrad(mixed, gb2), dwp[:, :sr].reshape(slab),
+        wgrad(first_low, dprobe), dwk, dwv, wgrad(mixed, gb2),
     ]
+    ns = len(slabs)
     if own_rows:
-        slab_shard, grad_projected = reduce_all(jnp.stack(slabs + [extra_grad.reshape(slab)]), dproj)
-        extra_shard = slab_shard[len(slabs)]
+        slab_shard, grad_projected = reduce_all(jnp.stack(slabs), dproj, patches, vec_block)
+        extra_shard = slab_shard[ns + 1]
     else:
         grad_projected = lax.psum_scatter(dproj, "dp", scatter_dimension=0, tiled=True)
+        dwp = lax.dot_general(patches, grad_projected, (((0, 1), (0, 1)), ((), ())), preferred_element_type=F32)
+        dwp = dwp.reshape(shards, pr, width)
+        pbg = jnp.sum(grad_projected.astype(F32), (0, 1))[None, None]
+        vec_block = jnp.where(jnp.arange(vec_block.shape[1])[None, :, None] == 5, pbg, vec_block)
+        slabs.append(dwp[:, :sr].reshape(slab).astype(BF))
         slab_shard = lax.psum_scatter(jnp.stack(slabs), AXES, scatter_dimension=1, tiled=True).astype(F32)
+        extra_grad = jnp.concatenate([dwp[:, sr:], vec_block], 1).astype(BF)
         extra_shard = lax.psum_scatter(extra_grad, AXES, scatter_dimension=0, tiled=True)[0].astype(F32)
-    patch_shard = jnp.concatenate([slab_shard[len(slabs) - 1], extra_shard[:tails]], 0)
+    patch_shard = jnp.concatenate([slab_shard[ns], extra_shard[:tails]], 0)
     patches_grad = lax.dot_general(
         grad_projected, patch_full, (((2,), (1,)), ((), ())), preferred_element_type=F32
     ).astype(BF)

time: 818 us -> 638 us (0.78)
  Pallas kernels: 691 us -> 522 us
  local copies, waits for them, and re-layouts: 66.6 us -> 51.1 us
    pallas_call x4 -> x3, Pallas kernels: 485 us -> 375 us  [the longest x1 159 us: front(): pl.pallas_call(functools.partial(front_kernel, parts, tails, nv, rb), in_...]
    pallas_call x1, Pallas kernels: 99.8 us -> 69.9 us  [on_device(): pl.pallas_call(cross_backward, grid_spec=pltpu.PrefetchScalarGridSpec(num...]
    pallas_call x1, Pallas kernels: 66.1 us -> 45.8 us  [on_device(): pl.pallas_call(cross_forward, grid_spec=pltpu.PrefetchScalarGridSpec(num_...]
    unnamed x100 -> x101, local copies, waits for them, and re-layouts: 46.6 us -> 29.7 us
    pallas_call x1, Pallas kernels: 40.2 us -> 31.9 us  [on_device(): pl.pallas_call(self_backward, grid=grid, in_specs=[tb, tb, tb, tb, tb, tb...]
  transfers between devices with their start and end apart: 2 -> 1, of which waited for: 0 -> 0; matrix products, arithmetic and copies ran while one was open for 4% -> 5% of each run, Pallas kernels for 51% -> 40%
where the time goes in v3:
time: 638 us; the launch traced here: 629 us
  Pallas kernels  522 us (82%)
  local copies, waits for them, and re-layouts  51.1 us (8%)
  matrix products  35.1 us (6%)
  between operations  15 us (2%)
    pallas_call x1, Pallas kernels, front(): pl.pallas_call(functools.partial(front_kernel, parts, tails, nv, rb), in_...  159 us
    pallas_call x1, Pallas kernels, reduce_all(): pl.pallas_call(functools.partial(reduce_kernel, parts), in_specs=[hbm, hb...  148 us
    pallas_call x1, Pallas kernels, on_device(): pl.pallas_call(cross_backward, grid_spec=pltpu.PrefetchScalarGridSpec(num...  69.9 us
    pallas_call x1, Pallas kernels, on_device(): pl.pallas_call(tail_kernel, grid=grid, in_specs=[tb, tb, tb, wspec(CO), c...  67.9 us
    pallas_call x1, Pallas kernels, on_device(): pl.pallas_call(cross_forward, grid_spec=pltpu.PrefetchScalarGridSpec(num_...  45.8 us
    pallas_call x1, Pallas kernels, on_device(): pl.pallas_call(self_backward, grid=grid, in_specs=[tb, tb, tb, tb, tb, tb...  31.9 us
    unnamed x101, local copies, waits for them, and re-layouts  29.7 us
    dot_general x10, matrix products, tn(): lax.dot_general(left, right, (((0,), (0,)), ((), ())), preferred_element_...  25.8 us
  transfers between devices with their start and end apart: 1, of which 0 were waited for; matrix products, arithmetic and copies ran while one was open for 5% of the time, Pallas kernels for 40%

profile of v3, /device:TPU:0, one launch (start us, length us, event | category | flops | bytes accessed | tf_op | source)
XLA Modules:
  0.0 629.1 jit_solution(16257258804239573243)
XLA Ops:
  9.8 1.6 stack.129
  12.6 1.2 pad_maximum_fusion.1.bias
  13.9 1.2 reshape.210
  15.3 1.3 reshape.211
  16.6 1.4 copy.91.pat
  19.2 158.8 %front.1 = (bf16[18,4,2,2,2,24,768]{6,5,4,3,2,1,0:T(8,128)(2,1)}, bf16[4,2,4,145,768]{4,3,2,1,0:T(8,128)(2,1)}, bf16[32,40,768]{2,1,0:T(8,128)(2,1)}, bf16[32,40...) custom-call(bf16[18,24,768]{2,1,0:T(8,128)(2,1)} %copy-done.15, ...), custom_call_target="tpu_custom_call" | custom-call | tf_op jit(solution)/shard_map/front/pallas_call | solution.py:794
  177.9 1.7 fusion.78
  179.7 2.9 fusion.76
  183.5 45.8 %cross_forward.1 = (bf16[32,160,768]{2,1,0:T(8,128)(2,1)}, bf16[32,160,768]{2,1,0:T(8,128)(2,1)}, bf16[32,4,160,120]{3,2,1,0:T(8,128)(2,1)}, bf16[32,40,768]{2,1,0:T(8,128)(2,1)S(1)}) custom-call(s32[33]{0:T(128)S(1)} %convert_reduce_fusion.1.starts, s32[32]{0:T(128)S(1)} %select_reduce_fusion.order, bf16[32,145,768]{2,1,0:T(8,128)(2,1)} %bitcast.231, ...), custom_call_target="tpu_custom_call" | custom-call | flops 10947133440 | bytes 40000000 | tf_op jit(solution)/shard_map/cross_forward/pallas_call | solution.py:969
  229.3 1.3 copy-done.5
  230.6 67.9 %tail.1 = (bf16[32,40,768]{2,1,0:T(8,128)(2,1)}, bf16[4,1280,768]{2,1,0:T(8,128)(2,1)}, bf16[4,1280,768]{2,1,0:T(8,128)(2,1)}, bf16[32,40,768]{2,1,0:T(8,128)(2,...) custom-call(f32[32,40,768]{2,1,0:T(8,128)} %get-tuple-element.67.u1,, ...), custom_call_target="tpu_custom_call" | custom-call | flops 37748736000 | bytes 50000000 | tf_op jit(solution)/shard_map/tail/pallas_call | solution.py:992
  298.5 5.1 fusion.47
  303.6 2.8 fusion.41
  306.4 2.8 fusion.35
  309.2 2.8 fusion.29
  312.1 8.1 %convert_dynamic-update-slice_fusion = bf16[8,768,768]{2,1,0:T(8,128)(2,1)} fusion(bf16[8,768,768]{2,1,0:T(8,128)(2,1)} %fusion.29, bf16[4,1280,768]{2,1,0:T(8,128)(2,1)S(1)} %bitcast.275, bf16[1280,768,1]{1,0,2:T(8,128)(2,1)S(1)} %bitcast.269), kind=kOutput, calls=%fused_computation | convolution fusion | flops 6042157056 | bytes 14548992 | tf_op jit(solution)/shard_map/dot_general | solution.py:1052
  320.2 8.6 %copy.105 = bf16[96,8,8,768]{3,1,2,0:T(8,128)(2,1)} copy(bf16[96,8,8,768]{3,1,0,2:T(8,128)(2,1)} %bitcast.194) | data formatting | bytes 18874368
  329.6 69.9 %cross_backward.1 = (bf16[32,40,768]{2,1,0:T(8,128)(2,1)}, bf16[32,145,768]{2,1,0:T(8,128)(2,1)}, bf16[768,768]{1,0:T(8,128)(2,1)}, bf16[768,768]{1,0:T(8,128)(2,1)}, f32[8,768]{1,0:T(8,128)}) custom-call(s32[33]{0:T(128)} %copy-done.3, s32[32]{0:T(128)} %copy-done.4, bf16[32,145,768]{2,1,0:T(8,128)(2,1)} %bitcast.232, ...), custom_call_target="tpu_custom_call" | custom-call | flops 21894266880 | bytes 50000000 | tf_op jit(solution)/shard_map/cross_backward/pallas_call | solution.py:1014
  400.6 31.9 %self_backward.1 = (bf16[32,40,768]{2,1,0:T(8,128)(2,1)}, bf16[32,40,768]{2,1,0:T(8,128)(2,1)}, bf16[32,40,768]{2,1,0:T(8,128)(2,1)}, bf16[32,40,768]{2,1,0:T(8,...) custom-call(f32[32,40,768]{2,1,0:T(8,128)} %get-tuple-element.74.gm, ...), custom_call_target="tpu_custom_call" | custom-call | flops 10569646080 | bytes 40000000 | tf_op jit(solution)/shard_map/self_backward/pallas_call | solution.py:1035
  432.7 3.3 bitcast_convert_fusion.5
  438.0 1.8 bitcast_convert_fusion.4
  441.8 1.8 bitcast_convert_fusion.3
  445.7 1.8 bitcast_convert_fusion.2
  449.4 1.8 bitcast_convert_fusion.1
  454.0 1.2 constant_dynamic-update-slice_fusion.13
  456.0 1.8 bitcast_convert_fusion
  459.0 1.4 fusion.12.vb_in
  460.5 147.9 %reduce_all.1 = (f32[10,24,768]{2,1,0:T(8,128)}, bf16[4,145,768]{2,1,0:T(8,128)(2,1)}) custom-call(bf16[8,4,2,2,2,24,768]{6,5,4,3,2,1,0:T(8,128)(2,1)} %constant_dynamic-update-slice_fusion.12.w_in, bf16[4,2,4,145,768]{4,3,2,1,0:T(8,128)(2,1)} %bitcast.233, bf16[4,145,1024]{2,1,0:T(8,128)(2,1)} %copy.91.pat, f32[32,16,768]{2,1,0:T(8,128)} %fusion.12.vb_in), custom_call_target="tpu_custom_call" | custom-call | tf_op jit(solution)/shard_map/reduce_all/pallas_call | solution.py:830
  609.5 1.2 convolution_convert_fusion
  610.7 1.9 copy.100
  618.3 1.2 copy.99
  619.5 2.6 reshape.224
  (143 shorter events, 27.3 us)
Async XLA Ops:
  7.2 6.6 %copy-start.16 = (bf16[24,3072]{1,0:T(8,128)(2,1)S(1)}, bf16[24,3072]{1,0:T(8,128)(2,1)}, u32[]{:S(2)}) copy-start(bf16[24,3072]{1,0:T(8,128)(2,1)} %param.58) | copy-start | bytes 442372
  7.2 608.1 %reduce-scatter.4.cloned.1.call-start = ((), (), s32[]{:S(2)}) async-start(), calls=%async_computation.1 | async-start | bytes 9732096
  8.1 175.4 %copy-start.3 = (s32[33]{0:T(128)}, s32[33]{0:T(128)S(1)}, u32[]{:S(2)}) copy-start(s32[33]{0:T(128)S(1)} %convert_reduce_fusion.1.starts) | copy-start | bytes 400
  9.1 174.3 %copy-start.4 = (s32[32]{0:T(128)}, s32[32]{0:T(128)S(1)}, u32[]{:S(2)}) copy-start(s32[32]{0:T(128)S(1)} %select_reduce_fusion.order) | copy-start | bytes 388
  13.9 2.7 copy-start.11
  15.2 2.8 slice-start
  15.2 2.8 copy-start.18
  15.3 2.8 copy-start.19
  15.3 2.9 copy-start.20
  15.3 2.9 copy-start.21
  15.3 2.9 copy-start.22
  15.3 2.9 copy-start.23
  15.3 2.9 copy-start.17
  179.7 3.8 copy-start
  298.5 5.1 copy-start.35
  298.5 5.1 copy-start.36
  306.4 5.7 slice-start.1
  309.2 2.8 copy-start.34
  309.2 2.8 slice-start.2
  329.6 70.6 %copy-start.27 = (f32[4,1,768]{2,1,0:T(1,128)S(1)}, f32[4,1,768]{2,1,0:T(1,128)}, u32[]{:S(2)}) copy-start(f32[4,1,768]{2,1,0:T(1,128)} %get-tuple-element.98) | copy-start | bytes 36868
  329.6 71.0 %copy-start.1 = (bf16[32,4,40,120]{3,2,1,0:T(8,128)(2,1)S(1)}, bf16[32,4,40,120]{3,2,1,0:T(8,128)(2,1)}, u32[]{:S(2)}) copy-start(bf16[32,4,40,120]{3,2,1,0:T(8,128)(2,1)} %get-tuple-element.83.probs) | copy-start | bytes 3686404
  329.6 71.0 %copy-start.2 = (f32[1,768]{1,0:T(1,128)S(1)}, f32[1,768]{1,0:T(1,128)}, u32[]{:S(2)}) copy-start(f32[1,768]{1,0:T(1,128)} %get-tuple-element.257.g1) | copy-start | bytes 9220
  400.6 31.9 %copy-start.26 = (f32[8,768]{1,0:T(8,128)S(1)}, f32[8,768]{1,0:T(8,128)}, u32[]{:S(2)}) copy-start(f32[8,768]{1,0:T(8,128)} %get-tuple-element.97) | copy-start | bytes 73732
  400.6 32.0 %copy-start.9 = (bf16[32,40,768]{2,1,0:T(8,128)(2,1)S(1)}, bf16[32,40,768]{2,1,0:T(8,128)(2,1)}, u32[]{:S(2)}) copy-start(bf16[32,40,768]{2,1,0:T(8,128)(2,1)} %tok.1) | copy-start | bytes 5898244
  436.0 2.0 copy-start.32
  441.8 2.9 copy-start.30
  445.7 2.9 copy-start.28
  451.2 2.8 copy-start.12
  452.9 2.3 copy-start.6
  452.9 3.1 copy-start.37
  460.5 147.9 %copy-start.7 = (bf16[1,4,2,2,2,24,768]{6,5,4,3,2,1,0:T(8,128)(2,1)S(1)}, bf16[1,4,2,2,2,24,768]{6,5,4,3,2,1,0:T(8,128)(2,1)}, u32[]{:S(2)}) copy-start(bf16[1,4,2,2,2,24,768]{6,5,4,3,2,1,0:T(8,128)(2,1)} %get-tuple-element.221) | copy-start | bytes 3538948
  460.5 147.9 %copy-start.10 = (bf16[32,8,768]{2,1,0:T(8,128)(2,1)S(1)}, bf16[32,8,768]{2,1,0:T(8,128)(2,1)}, u32[]{:S(2)}) copy-start(bf16[32,8,768]{2,1,0:T(8,128)(2,1)} %slice.264) | copy-start | bytes 1179652
  (10 other events, 16.3 us)
Sparse Core Ops, SparseCore 0:
  329.0 134.6 reduce-scatter.3

commit v4 on v3

--- a/solution.py
+++ b/solution.py
@@ -342,37 +342,21 @@
         dwv_o[...] = dwv_s[...].astype(BF)
 
 
-def self_backward(
-    gm, dpr, u1, q, k, v, probs, wq, wk, wv, wo, wc, g1,
-    gb1_o, dq_o, dk_o, dv_o, tg_o, vec_o,
-    ga_s, dq_s, dk_s, dv_s,
-):
-    step = pl.program_id(0)
-    rb, length, width = u1.shape
+def self_back_block(gm, dpr32, u1, heads, mats, g1, add, temps):
+    q, k, v, probs = heads
+    wq, wk, wv, wo, wc = mats
+    ga_s, dq_s, dk_s, dv_s = temps
+    rb, length, width = ga_s.shape
     n = rb * length
-
-    @pl.when(step == 0)
-    def _():
-        vec_o[...] = jnp.zeros_like(vec_o)
-
-    def flat(ref):
-        return ref[...].astype(F32).reshape(n, width)
-
-    def fold(value):
-        return value.reshape(rb, length, width)
-
-    dpr32 = flat(dpr)
-    grad_first = flat(gm) + nt(dpr32.astype(BF), wc[...])
-    xhat, inv = norm_parts(flat(u1))
-    low = norm_back(grad_first, g1[...], xhat, inv)
+    grad_first = gm + nt(dpr32.astype(BF), wc())
+    xhat, inv = norm_parts(u1)
+    low = norm_back(grad_first, g1, xhat, inv)
     gb1 = low.astype(BF)
-    gb1f = gb1.astype(F32)
-    gb1_o[...] = fold(gb1f).astype(BF)
-    vec_o[0:1] += jnp.sum(grad_first * xhat, 0, keepdims=True)
-    vec_o[1:2] += jnp.sum(grad_first, 0, keepdims=True)
-    vec_o[2:3] += jnp.sum(gb1f, 0, keepdims=True)
-    vec_o[3:4] += jnp.sum(dpr32, 0, keepdims=True)
-    ga_s[...] = fold(nt(gb1, wo[...]).astype(BF).astype(F32))
+    add(3, grad_first * xhat)
+    add(4, grad_first)
+    add(2, gb1.astype(F32))
+    add(6, dpr32)
+    ga_s[...] = nt(gb1, wo()).astype(BF).astype(F32).reshape(rb, length, width)
 
     def row(r, carry):
         qr = q[r].astype(F32) * 0.125
@@ -398,13 +382,35 @@
     dq = dq_s[...].reshape(n, width).astype(BF)
     dk = dk_s[...].reshape(n, width).astype(BF)
     dv = dv_s[...].reshape(n, width).astype(BF)
-    dq_o[...] = dq_s[...].astype(BF)
-    dk_o[...] = dk_s[...].astype(BF)
-    dv_o[...] = dv_s[...].astype(BF)
-    vec_o[4:5] += jnp.sum(dq.astype(F32), 0, keepdims=True)
-    vec_o[5:6] += jnp.sum(dv.astype(F32), 0, keepdims=True)
-    total = low + nt(dq, wq[...]) + nt(dk, wk[...]) + nt(dv, wv[...])
-    tg_o[...] = fold(total).astype(BF)
+    add(0, dq.astype(F32))
+    add(1, dv.astype(F32))
+    total = low + nt(dq, wq()) + nt(dk, wk()) + nt(dv, wv())
+    return gb1, dq, dk, dv, total.reshape(rb, length, width).astype(BF)
+
+
+def self_backward(
+    gm, dpr, u1, q, k, v, probs, wq, wk, wv, wo, wc, g1, gb1_o, dq_o, dk_o, dv_o, tg_o, vec_o, *temps
+):
+    rb, length, width = u1.shape
+    n = rb * length
+
+    @pl.when(pl.program_id(0) == 0)
+    def _():
+        vec_o[...] = jnp.zeros_like(vec_o)
+
+    def add(row, value):
+        vec_o[row : row + 1] += jnp.sum(value, 0, keepdims=True)
+
+    def flat(ref):
+        return ref[...].astype(F32).reshape(n, width)
+
+    mats = [lambda ref=ref: ref[...] for ref in (wq, wk, wv, wo, wc)]
+    *grads, tokens_grad = self_back_block(
+        flat(gm), flat(dpr), flat(u1), (q, k, v, probs), mats, g1[...], add, temps
+    )
+    for ref, value in zip((gb1_o, dq_o, dk_o, dv_o), grads):
+        ref[...] = value.astype(F32).reshape(rb, length, width).astype(BF)
+    tg_o[...] = tokens_grad
 
 
 def sds(shape, dtype):
@@ -491,7 +497,7 @@
 
 
 PATCH, EXTRA, QUERY, KEY, VALUE, OUT, CQ, CK, W1 = range(9)
-W2, CV, CO = 12, 16, 17
+CV, CO = 12, 13
 
 
 FRONT_ORDER = (
@@ -500,14 +506,15 @@
     "i0", "i0", "F", "Q", "self", "i2", "i3", "G", "self", "R", "i2", "F", "G", "self", "i3", "i1",
     "G", "self", "G", "R", "R", "i1", "F", "i2", "self", "R", "R", "G", "i2", "R",
 )
-REDUCE_ORDER = (
-    "p0", "p1", "w0", "p2", "p3", "w1", "p0", "w0", "p1", "p2", "w0", "p3", "p0", "p1", "w1", "p2",
-    "p3", "v", "w0", "w1", "v", "w0", "v", "w1", "v",
+BACK_ORDER = (
+    "p2", "S", "E", "E", "p0", "p2", "p1", "S", "p0", "S", "p1", "p3", "S", "S", "D1", "D2", "L2",
+    "E", "L2", "p3", "L1", "L1", "L2", "p2", "p0", "L1", "p1", "E", "p3", "V1", "V1", "V2", "L2",
+    "E", "V2", "L1", "V1", "V1", "V2", "V2", "L2", "V1", "L1", "V2",
 )
 
 
 def front_kernel(
-    parts, tails, nv, rb, w_in, pat, tok, bias, w_out, p_out, q_o, k_o, v_o, pr_o, att_o, u1_o, f_o, prb_o, vec_o,
+    parts, tails, nv, rb, w_in, n_in, pat, tok, bias, w_out, n_out, p_out, q_o, k_o, v_o, pr_o, att_o, u1_o, f_o, prb_o, vec_o,
     pw, ex, wm, proj_s, q_s, k_s, v_s, pr_s, att_b, u1_s, f_s, prb_s, att_s, send, recv, local,
 ):
     z, y, x, c = my_place()
@@ -561,17 +568,17 @@
         start = {"own": own, "partner": second, "inner": third, "outer": third}
         return along_z(source, view, lambda which: start[which].start(), local), (own, second, third)
 
-    def slabs(lo, n):
-        pick = pl.ds(lo, n)
+    def slabs(source, out):
+        every = slice(None)
 
         def view(at, many):
-            return w_out.at[pick, pl.ds(at, many) if many else at, y, x, c]
+            return out(pl.ds(at, many) if many else at, y, x, c)
 
         def plane(at, many):
-            return w_out.at[pick, pl.ds(at, many) if many else at, :, x, c]
-
-        local = copies.here(w_in.at[pick], view(z, 0))
-        moving, (own, second, third) = exchanged(w_in.at[pick], view, None)
+            return out(pl.ds(at, many) if many else at, every, x, c)
+
+        local = copies.here(source, view(z, 0))
+        moving, (own, second, third) = exchanged(source, view, None)
         next(moving)
         yield
         own.wait()
@@ -588,7 +595,7 @@
         steps.append(copies.remote(plane(theirs, 2), plane(theirs, 2), device_at(z, y, 1 - x, c)))
         yield
         arrived(steps)
-        half = w_out.at[pick, :, :, :, c]
+        half = out(every, every, every, c)
         step = copies.remote(half, half, device_at(z, y, x, 1 - c))
         yield
         step.wait()
@@ -642,7 +649,12 @@
             yield
         arrived(outgoing)
 
-    jobs = {name: slabs(lo, n) for name, (lo, n) in parts.items()}
+    def stacked(lo, n):
+        pick = pl.ds(lo, n)
+        return slabs(w_in.at[pick], lambda *at: w_out.at[(pick,) + at])
+
+    jobs = {name: stacked(lo, n) for name, (lo, n) in parts.items()}
+    jobs["G"] = slabs(n_in, lambda *at: n_out.at[at])
     jobs["weights"] = patch_weights()
     for i in range(images):
         jobs["i%d" % i] = image(i)
@@ -655,73 +667,92 @@
             copy.wait_send()
 
 
-def reduce_kernel(
-    parts, w_in, p_in, pat, vb_in, w_out, p_out, acc, rc, rx, ry, rz, pacc, pry, prz, dwp, pv, send, recv, local
+def back_kernel(
+    rb, tails, w_in, p_in, gm, dpr, u1, q, k, v, probs, tok, att, w_all, pat, g1, vt_in, wb_in,
+    w_out, p_out, tg_o,
+    wm, gm_s, dpr_s, u1_s, q_s, k_s, v_s, p_s, ga_t, dq_t, dk_t, dv_t, gb1_f, dq_f, dk_f, dv_f, tg_s, vec_s,
+    acc, lw, pv, rc, rx, ry, rz, pacc, pry, prz, send, recv, local,
 ):
     z, y, x, c = my_place()
     meet(z, y, x, c)
     copies = Copies(send, recv, local)
+    rows, length, width = gm.shape
+    images = pat.shape[0]
+    sr = w_out.shape[1]
 
     def up(ref, *at):
         return ref[at].astype(F32)
 
-    def slabs(lo, n, src):
+    def slabs(lo, n, sibling, own, base, own_c):
         pick = pl.ds(lo, n)
-        own = copies.here(src.at[:, :, :, :, c], acc.at[pick])
-        step = copies.remote(src.at[:, :, :, :, 1 - c], rc.at[pick], device_at(z, y, x, 1 - c))
-        yield
-        own.wait()
+        last = (c,) if own_c else ()
+
+        def cell(s, zz, yy, xx):
+            return (s - base, zz, yy, xx) + last
+
+        def view(zz, yy, xx):
+            return own.at[(pl.ds(lo - base, n), zz, yy, xx) + last]
+
+        every = slice(None)
+        step = copies.remote(sibling, rc.at[pick], device_at(z, y, x, 1 - c))
+        yield
         step.wait()
 
         def add_x(i, carry):
             s, zz = lo + i // 4, i % 4
             for yy in range(2):
-                acc[s, zz, yy, 1 - x] = (up(acc, s, zz, yy, 1 - x) + up(rc, s, zz, yy, 1 - x)).astype(BF)
+                at = cell(s, zz, yy, 1 - x)
+                own[at] = (up(own, *at) + up(rc, s, zz, yy, 1 - x)).astype(BF)
             return carry
 
         lax.fori_loop(0, 4 * n, add_x, 0)
-        step = copies.remote(acc.at[pick, :, :, 1 - x], rx.at[pick], device_at(z, y, 1 - x, c))
+        step = copies.remote(view(every, every, 1 - x), rx.at[pick], device_at(z, y, 1 - x, c))
         yield
         step.wait()
 
         def add_y(i, carry):
             s, zz = lo + i // 4, i % 4
-            acc[s, zz, 1 - y, x] = (
-                up(acc, s, zz, 1 - y, x) + up(rc, s, zz, 1 - y, x) + up(rx, s, zz, 1 - y)
-            ).astype(BF)
+            at = cell(s, zz, 1 - y, x)
+            own[at] = (up(own, *at) + up(rc, s, zz, 1 - y, x) + up(rx, s, zz, 1 - y)).astype(BF)
             return carry
 
         lax.fori_loop(0, 4 * n, add_y, 0)
-        step = copies.remote(acc.at[pick, :, 1 - y, x], ry.at[pick], device_at(z, 1 - y, x, c))
+        step = copies.remote(view(every, 1 - y, x), ry.at[pick], device_at(z, 1 - y, x, c))
         yield
         step.wait()
         steps = []
-        for k in (1, 3, 2):
-            zz = (z + k) % 4
+        for hop in (1, 3, 2):
+            zz = (z + hop) % 4
 
             def add_z(i, carry):
                 s = lo + i
-                acc[s, zz, y, x] = (
-                    up(acc, s, zz, y, x) + up(rc, s, zz, y, x) + up(rx, s, zz, y) + up(ry, s, zz)
-                ).astype(BF)
+                at = cell(s, zz, y, x)
+                own[at] = (up(own, *at) + up(rc, s, zz, y, x) + up(rx, s, zz, y) + up(ry, s, zz)).astype(BF)
                 return carry
 
             lax.fori_loop(0, n, add_z, 0)
-            steps.append(
-                copies.remote(acc.at[pick, zz, y, x], rz.at[k - 1, pick], device_at(zz, y, x, c))
-            )
+            steps.append(copies.remote(view(zz, y, x), rz.at[hop - 1, pick], device_at(zz, y, x, c)))
         yield
         arrived(steps)
 
         def add_last(i, carry):
             s = lo + i
             w_out[s] = (
-                up(acc, s, z, y, x) + up(rc, s, z, y, x) + up(rx, s, z, y) + up(ry, s, z)
+                up(own, *cell(s, z, y, x)) + up(rc, s, z, y, x) + up(rx, s, z, y) + up(ry, s, z)
                 + up(rz, 0, s) + up(rz, 1, s) + up(rz, 2, s)
             )
             return carry
 
         lax.fori_loop(0, n, add_last, 0)
+        yield
+
+    def early():
+        own = copies.here(w_in.at[:, :, :, :, c], acc)
+        job = slabs(4, 3, w_in.at[:, :, :, :, 1 - c], acc, 4, False)
+        next(job)
+        yield
+        own.wait()
+        yield from job
 
     def image(i):
         own = copies.here(p_in.at[:, y, i], pacc.at[i])
@@ -730,10 +761,10 @@
         own.wait()
         step.wait()
         steps = []
-        for k in (1, 3, 2):
-            zz = (z + k) % 4
+        for hop in (1, 3, 2):
+            zz = (z + hop) % 4
             pacc[i, zz] = (up(pacc, i, zz) + up(pry, i, zz)).astype(BF)
-            steps.append(copies.remote(pacc.at[i, zz], prz.at[k - 1, i], device_at(zz, y, x, c)))
+            steps.append(copies.remote(pacc.at[i, zz], prz.at[hop - 1, i], device_at(zz, y, x, c)))
         yield
         arrived(steps)
         p_out[i] = (
@@ -741,62 +772,126 @@
         ).astype(BF)
         yield
 
-    def patch_grads(first):
-        sr, width = w_out.shape[1:]
-        images = p_in.shape[2]
-        total = tn(pat[0], p_out[0])
+    def attention():
+        weights = [
+            copies.here(w_all.at[m], wm.at[pl.ds(width * at, width)])
+            for at, m in enumerate((QUERY, KEY, VALUE, OUT, CQ))
+        ]
+        vec_s[...] = vt_in[...]
+        mats = [lambda at=at: wm[pl.ds(width * at, width)] for at in range(5)]
+        streams = ((gm, gm_s), (dpr, dpr_s), (u1, u1_s), (q, q_s), (k, k_s), (v, v_s), (probs, p_s))
+        size = gm_s.shape[0]
+        n = rb * length
+
+        def add(row, value):
+            vec_s[row : row + 1] += jnp.sum(value, 0, keepdims=True)
+
+        leaving = None
+        for stage in range(rows // size):
+            coming = [copies.here(src.at[pl.ds(stage * size, size)], dst) for src, dst in streams]
+            arrived(weights + coming)
+            weights = []
+            if leaving is not None:
+                leaving.wait()
+
+            def block(b, carry):
+                pick = pl.ds(b * rb, rb)
+
+                def flat(ref):
+                    return ref[pick].astype(F32).reshape(n, width)
+
+                heads = tuple(ref.at[pick] for ref in (q_s, k_s, v_s, p_s))
+                *grads, tokens_grad = self_back_block(
+                    flat(gm_s), flat(dpr_s), flat(u1_s), heads, mats, g1[...], add, (ga_t, dq_t, dk_t, dv_t)
+                )
+                at = pl.ds(pl.multiple_of(stage * size * length + b * n, n), n)
+                for ref, value in zip((gb1_f, dq_f, dk_f, dv_f), grads):
+                    ref[at] = value
+                tg_s[pick] = tokens_grad
+                return carry
+
+            lax.fori_loop(0, size // rb, block, 0)
+            leaving = copies.here(tg_s, tg_o.at[pl.ds(stage * size, size)])
+            yield
+        leaving.wait()
+        count = rows * length
+        arrived(
+            [
+                copies.here(tok, wm.at[pl.ds(0, count)]),
+                copies.here(att, wm.at[pl.ds(count, count)]),
+            ]
+        )
+        yield
+
+    def gradient(pairs):
+        count = rows * length
+        for m, first, right in pairs:
+            left = wm[pl.ds(first * count, count)]
+            lw[m] = tn(left, right[...]).reshape(lw.shape[1:]).astype(BF)
+        yield
+
+    def late(lo):
+        yield from slabs(lo, 2, lw.at[pl.ds(lo, 2), :, :, :, 1 - c], lw, 0, True)
+
+    def patch_sums(first):
+        pwidth = pat.shape[2]
+        rows_each = pwidth // 32
+        step = 128
         bias = jnp.sum(p_out[0].astype(F32), 0, keepdims=True)
         for i in range(1, images):
-            total = total + tn(pat[i], p_out[i])
             bias = bias + jnp.sum(p_out[i].astype(F32), 0, keepdims=True)
-        dwp[...] = total.reshape(dwp.shape)
-
-        def fill(d, carry):
-            zz, yy, xx, cc = d // 8, (d // 4) % 2, (d // 2) % 2, d % 2
-            rows = dwp[d]
-            pv[0, zz, yy, xx, cc] = rows[:sr].astype(BF)
-            block = vb_in[d]
-            row = lax.broadcasted_iota(jnp.int32, block.shape, 0)
-            block = jnp.where(row == 5, bias, block)
-            pv[1, zz, yy, xx, cc] = jnp.concatenate([rows[sr:], block], 0).astype(BF)
-            return carry
-
-        lax.fori_loop(0, 32, fill, 0)
-        yield from slabs(first, 2, pv)
-
-    jobs = {}
-    for i in range(p_in.shape[2]):
-        jobs["p%d" % i] = image(i)
-    for j, (lo, n) in enumerate(parts):
-        jobs["w%d" % j] = slabs(lo, n, w_in.at[pl.ds(lo, n)])
-    jobs["v"] = patch_grads(w_in.shape[0])
-    drive(jobs, REDUCE_ORDER)
-
-
-def split_slabs(count):
-    first = (count + 1) // 2
-    return ((0, first), (first, count - first))
-
-
-def front(slabs, patches, tokens, bias, tails, nv):
+        vec_s[5:6] = bias
+
+        for lo in range(0, pwidth, step):
+            total = tn(pat[0, :, lo : lo + step], p_out[0])
+            for i in range(1, images):
+                total = total + tn(pat[i, :, lo : lo + step], p_out[i])
+            for at in range(step // rows_each):
+                d = lo // rows_each + at
+                zz, yy, xx, cc = d // 8, (d // 4) % 2, (d // 2) % 2, d % 2
+                part = total[at * rows_each : (at + 1) * rows_each]
+                pv[0, zz, yy, xx, cc] = part[:sr].astype(BF)
+                vecs = vec_s[...]
+                row = lax.broadcasted_iota(jnp.int32, vecs.shape, 0)
+                vecs = jnp.where(row == vecs.shape[0] - 2, wb_in[d : d + 1], vecs)
+                pv[1, zz, yy, xx, cc] = jnp.concatenate([part[sr:], vecs], 0).astype(BF)
+
+        yield from slabs(first, 1, pv.at[pl.ds(0, 1), :, :, :, 1 - c], pv, first, True)
+
+    def second_patch(first):
+        yield from slabs(first, 1, pv.at[pl.ds(1, 1), :, :, :, 1 - c], pv, first - 1, True)
+
+    jobs = {"p%d" % i: image(i) for i in range(images)}
+    jobs["E"] = early()
+    jobs["S"] = attention()
+    jobs["D1"] = gradient(((0, 0, dq_f), (1, 0, dk_f)))
+    jobs["D2"] = gradient(((2, 0, dv_f), (3, 1, gb1_f)))
+    jobs["L1"], jobs["L2"] = late(0), late(2)
+    jobs["V1"], jobs["V2"] = patch_sums(7), second_patch(8)
+    drive(jobs, BACK_ORDER)
+
+
+def front(slabs, narrow, patches, tokens, bias, tails, nv):
     n, sr, width = slabs.shape
     images, points, pwidth = patches.shape
     rows, length, _ = tokens.shape
     rb = 8 if rows % 8 == 0 else 1
-    parts = {"P": (PATCH, 2), "Q": (QUERY, 6), "F": (W1, 4), "G": (W2, 4), "R": (CV, 2)}
-    remote = 10 * len(parts) + 6 * images
-    near = len(parts) + images + 3 + 5 + len(SELF_OUTS) * (rows // rb)
+    parts = {"P": (PATCH, 2), "Q": (QUERY, 6), "F": (W1, 4), "R": (CV, 2)}
+    nr = narrow.shape[0]
+    remote = 10 * (len(parts) + 1) + 6 * images
+    near = len(parts) + 1 + images + 3 + 5 + len(SELF_OUTS) * (rows // rb)
     tok_sh = (rows, length, width)
     probs = (rows, 4, length, 3 * length)
     kept = [sds(tok_sh, BF), sds(tok_sh, BF), sds(tok_sh, BF), sds(probs, BF), sds(tok_sh, BF), sds(tok_sh, F32), sds(tok_sh, BF), sds(tok_sh, BF)]
     hbm = pl.BlockSpec(memory_space=pl.ANY)
     vmem = pl.BlockSpec(memory_space=pltpu.VMEM)
-    w_all, p_all, *rest = pl.pallas_call(
+    w_all, n_all, p_all, *rest = pl.pallas_call(
         functools.partial(front_kernel, parts, tails, nv, rb),
-        in_specs=[hbm, vmem, vmem, vmem],
-        out_specs=[hbm] * 10 + [vmem],
+        in_specs=[hbm, hbm, vmem, vmem, vmem],
+        out_specs=[hbm] * 11 + [vmem],
         out_shape=[
-            sds((n, 4, 2, 2, 2, sr, width), BF), sds((4, 2, images, points, width), BF), *kept, sds((sr, width), F32),
+            sds((n, 4, 2, 2, 2, sr, width), BF), sds((4, 2, 2, 2, nr, width), BF),
+            sds((4, 2, images, points, width), BF), *kept, sds((sr, width), F32),
         ],
         scratch_shapes=[
             pltpu.VMEM((4, 2, 2, 2, pwidth // 32, width), BF),
@@ -813,46 +908,58 @@
             collective_id=0, has_side_effects=True, vmem_limit_bytes=58 * 1024 * 1024
         ),
         name="front",
-    )(slabs, patches, tokens, bias)
-    return w_all.reshape(n, 32 * sr, width), p_all.reshape(8 * images, points, width), rest[:8], rest[8]
-
-
-def reduce_all(slabs, grads, patches, vec_block):
+    )(slabs, narrow, patches, tokens, bias)
+    return w_all.reshape(n, 32 * sr, width), n_all.reshape(32 * nr, width), p_all.reshape(8 * images, points, width), rest[:8], rest[8]
+
+
+def back(slabs, grads, streams, tok, att, w_all, patches, g1, vecs, wb_rows, tails):
     n, full, width = slabs.shape
     sr = full // 32
     total, points, _ = grads.shape
     images, _, pwidth = patches.shape
-    parts = split_slabs(n)
-    copies = 6 * (len(parts) + 1) + 4 * images
+    rows, length, _ = streams[0].shape
+    m = n + 6
+    size, rb = 8, 4
     hbm = pl.BlockSpec(memory_space=pl.ANY)
     vmem = pl.BlockSpec(memory_space=pltpu.VMEM)
-    m = n + 2
-    w_shard, p_shard = pl.pallas_call(
-        functools.partial(reduce_kernel, parts),
-        in_specs=[hbm, hbm, vmem, vmem],
-        out_specs=[vmem] * 2,
-        out_shape=[sds((m, sr, width), F32), sds((images, points, width), BF)],
+    remote = 6 * 5 + 4 * images
+    near = 1 + images + 5 + 8 * (rows // size) + 2
+    part = (sr, width)
+    w_shard, p_shard, tokens_grad = pl.pallas_call(
+        functools.partial(back_kernel, rb, tails),
+        in_specs=[hbm] * 12 + [vmem] * 4,
+        out_specs=[vmem, vmem, hbm],
+        out_shape=[sds((m, sr, width), F32), sds((images, points, width), BF), sds((rows, length, width), BF)],
         scratch_shapes=[
-            pltpu.VMEM((m, 4, 2, 2, sr, width), BF),
-            pltpu.VMEM((m, 4, 2, 2, sr, width), BF),
-            pltpu.VMEM((m, 4, 2, sr, width), BF),
-            pltpu.VMEM((m, 4, sr, width), BF),
-            pltpu.VMEM((3, m, sr, width), BF),
+            pltpu.VMEM((5 * width, width), BF),
+            *[pltpu.VMEM((size,) + item.shape[1:], item.dtype) for item in streams],
+            *[pltpu.VMEM((rb, length, width), F32)] * 4,
+            *[pltpu.VMEM((rows * length, width), BF)] * 4,
+            pltpu.VMEM((size, length, width), BF),
+            pltpu.VMEM(vecs.shape, F32),
+            pltpu.VMEM((n, 4, 2, 2) + part, BF),
+            pltpu.VMEM((4, 4, 2, 2, 2) + part, BF),
+            pltpu.VMEM((2, 4, 2, 2, 2) + part, BF),
+            pltpu.VMEM((m, 4, 2, 2) + part, BF),
+            pltpu.VMEM((m, 4, 2) + part, BF),
+            pltpu.VMEM((m, 4) + part, BF),
+            pltpu.VMEM((3, m) + part, BF),
             pltpu.VMEM((images, 4, points, width), BF),
             pltpu.VMEM((images, 4, points, width), BF),
             pltpu.VMEM((3, images, points, width), BF),
-            pltpu.VMEM((32, pwidth // 32, width), F32),
-            pltpu.VMEM((2, 4, 2, 2, 2, sr, width), BF),
-            pltpu.SemaphoreType.DMA((copies,)),
-            pltpu.SemaphoreType.DMA((copies,)),
-            pltpu.SemaphoreType.DMA((len(parts) + 1 + images,)),
+            pltpu.SemaphoreType.DMA((remote,)),
+            pltpu.SemaphoreType.DMA((remote,)),
+            pltpu.SemaphoreType.DMA((near,)),
         ],
         compiler_params=pltpu.CompilerParams(
-            collective_id=1, has_side_effects=True, vmem_limit_bytes=58 * 1024 * 1024
+            collective_id=1, has_side_effects=True, vmem_limit_bytes=62 * 1024 * 1024
         ),
-        name="reduce_all",
-    )(slabs.reshape(n, 4, 2, 2, 2, sr, width), grads.reshape(4, 2, images, points, width), patches, vec_block)
-    return w_shard, p_shard
+        name="back",
+    )(
+        slabs.reshape(n, 4, 2, 2, 2, sr, width), grads.reshape(4, 2, images, points, width), *streams,
+        tok, att, w_all, patches, g1, vecs, wb_rows,
+    )
+    return w_shard, p_shard, tokens_grad
 
 
 def gather(value, axis):
@@ -891,17 +998,11 @@
     er = max(sr, extra.shape[0])
     own_rows = er == sr and groups == 8 and shards == 32
     extra = jnp.pad(extra, ((0, er - extra.shape[0]), (0, 0)))
-    widen_slabs = widen_weight.reshape(sr, shards, chunks, sr).transpose(2, 0, 1, 3).reshape(chunks, sr, width)
-    narrow_slabs = narrow_weight.reshape(chunks, sr, width)
-    slabs_in = jnp.concatenate(
+    slabs_in = jnp.stack(
         [
-            jnp.stack(
-                [
-                    patch_proj[:sr], extra[:sr], self_query, self_key, self_value, self_output,
-                    cross_query, cross_key,
-                ]
-            ),
-            widen_slabs, narrow_slabs, jnp.stack([cross_value, cross_output]),
+            patch_proj[:sr], extra[:sr], self_query, self_key, self_value, self_output, cross_query, cross_key,
+            *[widen_weight[:, width * at : width * (at + 1)] for at in range(chunks)],
+            cross_value, cross_output,
         ]
     )
 
@@ -928,16 +1029,19 @@
     tb = rows_block(tok_sh, rb)
     self_p = (rows, 4, length, 3 * length)
     if own_rows:
-        w_a, proj_all, kept, vec_all = front(slabs_in, patches, tokens, bias, tails, nv)
+        w_a, narrow_all, proj_all, kept, vec_all = front(
+            slabs_in, narrow_weight, patches, tokens, bias, tails, nv
+        )
         vec_all = vec_all[tails : tails + nv]
         extra_all = w_a[EXTRA].reshape(shards, er, width)
     else:
         w_a = gather(slabs_in, 1)
+        narrow_all = gather(narrow_weight, 0)
         extra_all = gather(extra, 0).reshape(shards, er, width)
         vec_all = jnp.sum(extra_all[:, tails : tails + nv].astype(F32), 0)
     (qb, vb, ob, g1, b1, pab, prb, cob, crb, g2, s2, nab, g3, s3) = [vec_all[j : j + 1] for j in range(nv)]
-    wb = extra_all[:, tails + nv, :wr].astype(F32)
-    wb = wb.reshape(shards, chunks, sr).transpose(1, 0, 2).reshape(chunks, 1, width)
+    wb = extra_all[:, tails + nv, :wr].astype(F32).reshape(chunks, 1, width)
+    narrow_all = narrow_all.reshape(chunks, width, width)
     patch_full = jnp.concatenate([w_a[PATCH].reshape(shards, sr, width), extra_all[:, :tails]], 1)
     patch_full = patch_full.reshape(shards * pr, width)
     if not own_rows:
@@ -981,18 +1085,16 @@
         name="cross_forward",
     )(starts, order, proj_all, w_a, w_a, cob, probe)
 
-    def chunk_w(j):
-        return pl.BlockSpec(
-            (chunks, width, width), lambda i, *_: (W1 // chunks + j, 0, 0), pipeline_mode=pl.Buffered(1)
-        )
-
+    w1_spec = pl.BlockSpec(
+        (chunks, width, width), lambda i, *_: (W1 // chunks, 0, 0), pipeline_mode=pl.Buffered(1)
+    )
     n_tok = rows * length
     hid_sh = (chunks, n_tok, width)
     hid_spec = pl.BlockSpec((chunks, rb * length, width), lambda i, *_: (0, i, 0))
     (output, active, grad_inner, second, gb3, grad_mid, gb2, grad_crossed, vec_t, wb_grad) = pl.pallas_call(
         tail_kernel,
         grid=grid,
-        in_specs=[tb, tb, tb, wspec(CO), chunk_w(0), chunk_w(1)]
+        in_specs=[tb, tb, tb, wspec(CO), w1_spec, whole((chunks, width, width))]
         + [vspec] * 5
         + [whole((chunks, 1, width))]
         + [vspec] * 3,
@@ -1009,7 +1111,7 @@
         compiler_params=params(56),
         cost_estimate=cost(18 * n_tok * width * width + 8 * n_tok * width * hidden, 50e6),
         name="tail",
-    )(u1, mixed, out_grad, w_a, w_a, w_a, g1, b1, crb, g2, s2, wb, nab, g3, s3)
+    )(u1, mixed, out_grad, w_a, w_a, narrow_all, g1, b1, crb, g2, s2, wb, nab, g3, s3)
 
     dprobe, dproj, dwk, dwv, dcb = pl.pallas_call(
         cross_backward,
@@ -1032,78 +1134,71 @@
         name="cross_backward",
     )(starts, order, proj_all, image_keys, image_values, w_a, w_a, probe, grad_crossed, cprobs)
 
-    gb1, dq, dk, dv, tokens_grad, vec_s = pl.pallas_call(
-        self_backward,
-        grid=grid,
-        in_specs=[tb, tb, tb, tb, tb, tb, rows_block(self_p, rb)]
-        + [wspec(j) for j in (QUERY, KEY, VALUE, OUT, CQ)]
-        + [vspec],
-        out_specs=[tb, tb, tb, tb, tb, whole((8, width))],
-        out_shape=[sds(tok_sh, BF)] * 5 + [sds((8, width), F32)],
-        scratch_shapes=[pltpu.VMEM((rb, length, width), F32)] * 4,
-        compiler_params=params(52),
-        cost_estimate=cost(14 * n_tok * width * width, 40e6),
-        name="self_backward",
-    )(grad_mid, dprobe, u1, q, k, v, probs, w_a, w_a, w_a, w_a, w_a, g1)
-
     def wgrad(left, right):
         return tn(left.reshape(n_tok, width), right.reshape(n_tok, width)).astype(BF)
 
-    grad_narrow = lax.dot_general(
-        active, gb3.reshape(n_tok, width), (((1,), (0,)), ((), ())), preferred_element_type=F32
-    ).astype(BF)
-    grad_widen = jnp.stack([wgrad(second, grad_inner[c]) for c in range(chunks)])
+    ffn = [wgrad(second, grad_inner[at]).reshape(shards, sr, width) for at in range(chunks)]
+    ffn.append(wgrad(mixed, gb2).reshape(shards, sr, width))
+    narrow_grad = [wgrad(active[at], gb3).reshape(shards // chunks, wr, width) for at in range(chunks)]
+    ffn.append(jnp.concatenate(narrow_grad))
     ffn_shard = lax.psum_scatter(
-        jnp.concatenate([grad_widen, grad_narrow], 0), AXES, scatter_dimension=1, tiled=True
+        jnp.concatenate(ffn, 1).reshape(-1, width), AXES, scatter_dimension=0, tiled=True
     ).astype(F32)
-
-    zero_row = jnp.zeros((1, width), F32)
-    vec_grads = jnp.concatenate(
-        [
-            vec_s[4:5], vec_s[5:6], vec_s[2:3], vec_s[0:1], vec_s[1:2], zero_row, vec_s[3:4], dcb[0:1],
-            vec_t[5:6], vec_t[3:4], vec_t[4:5], vec_t[2:3], vec_t[0:1], vec_t[1:2],
-        ]
+    ffn_parts = [ffn_shard[sr * at : sr * (at + 1)] for at in range(chunks + 1)]
+    widen_shard = jnp.concatenate(ffn_parts[:chunks], 1)
+    narrow_shard = ffn_shard[sr * (chunks + 1) :]
+
+    zero = jnp.zeros((1, width), F32)
+    vecs = jnp.concatenate(
+        [zero, zero, zero, zero, zero, zero, zero, dcb[0:1]]
+        + [vec_t[5:6], vec_t[3:4], vec_t[4:5], vec_t[2:3], vec_t[0:1], vec_t[1:2], zero, zero]
     )
-    wb_flat = wb_grad.reshape(chunks, shards, sr).transpose(1, 0, 2).reshape(shards, 1, wr)
-    vec_block = jnp.concatenate(
-        [
-            jnp.broadcast_to(vec_grads[None], (shards, nv, width)),
-            jnp.pad(wb_flat, ((0, 0), (0, 0), (0, width - wr))),
-            jnp.zeros((shards, er - tails - nv - 1, width), F32),
-        ],
-        1,
-    )
-    slabs = [
-        wgrad(tokens, dq), wgrad(tokens, dk), wgrad(tokens, dv), wgrad(attended, gb1),
-        wgrad(first_low, dprobe), dwk, dwv, wgrad(mixed, gb2),
-    ]
-    ns = len(slabs)
+    wb_rows = wb_grad.reshape(shards, wr)
+    wb_rows = jnp.pad(wb_rows, ((0, 0), (0, width - wr)))
+    cross_slabs = [wgrad(first_low, dprobe), dwk, dwv]
+    streams = (grad_mid, dprobe, u1, q, k, v, probs)
     if own_rows:
-        slab_shard, grad_projected = reduce_all(jnp.stack(slabs), dproj, patches, vec_block)
-        extra_shard = slab_shard[ns + 1]
+        slab_shard, grad_projected, tokens_grad = back(
+            jnp.stack(cross_slabs), dproj, streams, tokens.reshape(n_tok, width),
+            attended.reshape(n_tok, width), w_a, patches, g1, vecs, wb_rows, tails,
+        )
+        extra_shard = slab_shard[8]
     else:
+        gb1, dq, dk, dv, tokens_grad, vec_s = pl.pallas_call(
+            self_backward,
+            grid=grid,
+            in_specs=[tb, tb, tb, tb, tb, tb, rows_block(self_p, rb)]
+            + [wspec(j) for j in (QUERY, KEY, VALUE, OUT, CQ)]
+            + [vspec],
+            out_specs=[tb, tb, tb, tb, tb, whole((16, width))],
+            out_shape=[sds(tok_sh, BF)] * 5 + [sds((16, width), F32)],
+            scratch_shapes=[pltpu.VMEM((rb, length, width), F32)] * 4,
+            compiler_params=params(52),
+            cost_estimate=cost(14 * n_tok * width * width, 40e6),
+            name="self_backward",
+        )(grad_mid, dprobe, u1, q, k, v, probs, w_a, w_a, w_a, w_a, w_a, g1)
+        slabs = [wgrad(tokens, dq), wgrad(tokens, dk), wgrad(tokens, dv), wgrad(attended, gb1)] + cross_slabs
         grad_projected = lax.psum_scatter(dproj, "dp", scatter_dimension=0, tiled=True)
         dwp = lax.dot_general(patches, grad_projected, (((0, 1), (0, 1)), ((), ())), preferred_element_type=F32)
         dwp = dwp.reshape(shards, pr, width)
-        pbg = jnp.sum(grad_projected.astype(F32), (0, 1))[None, None]
-        vec_block = jnp.where(jnp.arange(vec_block.shape[1])[None, :, None] == 5, pbg, vec_block)
+        vecs = vecs + vec_s
+        vecs = vecs.at[5].set(jnp.sum(grad_projected.astype(F32), (0, 1)))
+        vecs = jnp.broadcast_to(vecs[None, :nv], (shards, nv, width))
         slabs.append(dwp[:, :sr].reshape(slab).astype(BF))
         slab_shard = lax.psum_scatter(jnp.stack(slabs), AXES, scatter_dimension=1, tiled=True).astype(F32)
-        extra_grad = jnp.concatenate([dwp[:, sr:], vec_block], 1).astype(BF)
+        extra_grad = jnp.concatenate([dwp[:, sr:], vecs, wb_rows[:, None]], 1).astype(BF)
         extra_shard = lax.psum_scatter(extra_grad, AXES, scatter_dimension=0, tiled=True)[0].astype(F32)
-    patch_shard = jnp.concatenate([slab_shard[ns], extra_shard[:tails]], 0)
+    patch_shard = jnp.concatenate([slab_shard[7], extra_shard[:tails]], 0)
     patches_grad = lax.dot_general(
         grad_projected, patch_full, (((2,), (1,)), ((), ())), preferred_element_type=F32
     ).astype(BF)
     vg = lax.dynamic_slice(extra_shard, (tails, place * sr), (nv, sr))
     vg = [vg[j] for j in range(nv)]
     wbg = extra_shard[tails + nv, :wr]
-    widen_shard = ffn_shard[:chunks].reshape(chunks, sr, shards, sr).transpose(1, 2, 0, 3).reshape(sr, hidden)
-    narrow_shard = ffn_shard[chunks:].reshape(chunks * sr, width)
     return (
         output, tokens_grad, patches_grad,
         slab_shard[0], vg[0], slab_shard[1], slab_shard[2], vg[1], slab_shard[3], vg[2], vg[3], vg[4],
-        patch_shard, vg[5], slab_shard[4], vg[6], slab_shard[5], slab_shard[6], vg[7], slab_shard[7],
+        patch_shard, vg[5], slab_shard[4], vg[6], slab_shard[5], slab_shard[6], vg[7], ffn_parts[chunks],
         vg[8], vg[9], vg[10], widen_shard, wbg, narrow_shard, vg[11], vg[12], vg[13],
     )
 

time: 638 us -> 602 us (0.944)
  Pallas kernels: 522 us -> 508 us
  matrix products: 35.1 us -> 23.7 us
  local copies, waits for them, and re-layouts: 51.1 us -> 41.4 us
    pallas_call x3 -> x2, Pallas kernels: 248 us -> 233 us  [the longest x1 165 us: back(): pl.pallas_call(functools.partial(back_kernel, rb, tails), in_specs=[hbm]...]
    dot_general x1 -> x0, matrix products: 8.13 us -> none  [on_device(): lax.dot_general(active, gb3.reshape(n_tok, width), (((1,), (0,)), ((), ()...]
    reshape x9 -> x1, local copies, waits for them, and re-layouts: 7.15 us -> 0.08 us  [on_device(): wb_rows = wb_grad.reshape(shards, wr)]
    unnamed x101 -> x68, local copies, waits for them, and re-layouts: 29.7 us -> 24.9 us
  transfers between devices with their start and end apart: 1 -> 1, of which waited for: 0 -> 0; matrix products, arithmetic and copies ran while one was open for 5% -> 3% of each run, Pallas kernels for 40% -> 39%
where the time goes in v4:
time: 602 us; the launch traced here: 596 us
  Pallas kernels  508 us (84%)
  local copies, waits for them, and re-layouts  41.4 us (7%)
  matrix products  23.7 us (4%)
  between operations  14.8 us (2%)
  other arithmetic  8.5 us (1%)
    pallas_call x1, Pallas kernels, back(): pl.pallas_call(functools.partial(back_kernel, rb, tails), in_specs=[hbm]...  165 us
    pallas_call x1, Pallas kernels, front(): pl.pallas_call(functools.partial(front_kernel, parts, tails, nv, rb), in_...  159 us
    pallas_call x1, Pallas kernels, on_device(): pl.pallas_call(cross_backward, grid_spec=pltpu.PrefetchScalarGridSpec(num...  70 us
    pallas_call x1, Pallas kernels, on_device(): pl.pallas_call(tail_kernel, grid=grid, in_specs=[tb, tb, tb, wspec(CO), w...  67.9 us
    pallas_call x1, Pallas kernels, on_device(): pl.pallas_call(cross_forward, grid_spec=pltpu.PrefetchScalarGridSpec(num_...  46 us
    unnamed x68, local copies, waits for them, and re-layouts  24.9 us
    dot_general x10, matrix products, tn(): lax.dot_general(left, right, (((0,), (0,)), ((), ())), preferred_element_...  22.5 us
  transfers between devices with their start and end apart: 1, of which 0 were waited for; matrix products, arithmetic and copies ran while one was open for 3% of the time, Pallas kernels for 39%

profile of v4, /device:TPU:0, one launch (start us, length us, event | category | flops | bytes accessed | tf_op | source)
XLA Modules:
  0.0 596.3 jit_solution(16388910640633350906)
XLA Ops:
  9.8 1.6 stack.117
  20.0 1.4 copy.69.pat
  21.7 1.2 pad_maximum_fusion.2.bias
  23.7 158.8 %front.1 = (bf16[14,4,2,2,2,24,768]{6,5,4,3,2,1,0:T(8,128)(2,1)}, bf16[4,2,2,2,96,768]{5,4,3,2,1,0:T(8,128)(2,1)}, bf16[4,2,4,145,768]{4,3,2,1,0:T(8,128)(2,1)},...) custom-call(bf16[14,24,768]{2,1,0:T(8,128)(2,1)} %copy-done.11, ...), custom_call_target="tpu_custom_call" | custom-call | tf_op jit(solution)/shard_map/front/pallas_call | solution.py:888
  182.5 1.8 fusion.76
  184.4 1.9 fusion.74
  188.1 46.0 %cross_forward.1 = (bf16[32,160,768]{2,1,0:T(8,128)(2,1)}, bf16[32,160,768]{2,1,0:T(8,128)(2,1)}, bf16[32,4,160,120]{3,2,1,0:T(8,128)(2,1)}, bf16[32,40,768]{2,1,0:T(8,128)(2,1)S(1)}) custom-call(s32[33]{0:T(128)S(1)} %convert_reduce_fusion.1.starts, s32[32]{0:T(128)S(1)} %select_reduce_fusion.order, bf16[32,145,768]{2,1,0:T(8,128)(2,1)} %bitcast.188, ...), custom_call_target="tpu_custom_call" | custom-call | flops 10947133440 | bytes 40000000 | tf_op jit(solution)/shard_map/cross_forward/pallas_call | solution.py:1073
  234.2 1.3 copy-done.3
  235.5 67.9 %tail.1 = (bf16[32,40,768]{2,1,0:T(8,128)(2,1)}, bf16[4,1280,768]{2,1,0:T(8,128)(2,1)}, bf16[4,1280,768]{2,1,0:T(8,128)(2,1)}, bf16[32,40,768]{2,1,0:T(8,128)(2,...) custom-call(f32[32,40,768]{2,1,0:T(8,128)} %get-tuple-element.63.u1,, ...), custom_call_target="tpu_custom_call" | custom-call | flops 37748736000 | bytes 50000000 | tf_op jit(solution)/shard_map/tail/pallas_call | solution.py:1094
  303.4 4.0 fusion.36
  308.4 1.8 fusion.39
  310.2 1.8 fusion.42
  312.0 1.8 fusion.45
  314.7 1.8 fusion.33
  316.5 1.8 fusion.30
  318.2 1.8 fusion.27
  320.0 2.0 fusion.24
  322.2 1.8 bitcast_convert_fusion
  325.1 1.2 constant_dynamic-update-slice_fusion.17
  327.4 1.1 constant_dynamic-update-slice_fusion.15
  328.5 1.1 constant_dynamic-update-slice_fusion.14
  329.6 2.3 maximum_dynamic-update-slice_fusion
  333.0 70.0 %cross_backward.1 = (bf16[32,40,768]{2,1,0:T(8,128)(2,1)}, bf16[32,145,768]{2,1,0:T(8,128)(2,1)}, bf16[768,768]{1,0:T(8,128)(2,1)}, bf16[768,768]{1,0:T(8,128)(2,1)}, f32[8,768]{1,0:T(8,128)}) custom-call(s32[33]{0:T(128)} %copy-done.1, s32[32]{0:T(128)} %copy-done.2, bf16[32,145,768]{2,1,0:T(8,128)(2,1)} %bitcast.189, ...), custom_call_target="tpu_custom_call" | custom-call | flops 21894266880 | bytes 50000000 | tf_op jit(solution)/shard_map/cross_backward/pallas_call | solution.py:1116
  404.6 1.3 concatenate.35.vt_in
  405.8 4.1 bitcast_convert_fusion.1
  409.9 2.0 pad_maximum_fusion.w_in
  412.0 165.2 %back.1 = (f32[9,24,768]{2,1,0:T(8,128)}, bf16[4,145,768]{2,1,0:T(8,128)(2,1)}, bf16[32,40,768]{2,1,0:T(8,128)(2,1)}) custom-call(bf16[3,4,2,2,2,24,768]{6,5,4,3,2,1,0:T(8,128)(2,1)} %pad_maximum_fusion.w_in, bf16[4,2,4,145,768]{4,3,2,1,0:T(8,128)(2,1)} %bitcast.190, f32[32,40,768]{2,1,0:T(8,128)} %get-tuple-element.80.gm, ...), custom_call_target="tpu_custom_call" | custom-call | tf_op jit(solution)/shard_map/back/pallas_call | solution.py:928
  578.4 1.2 convolution_convert_fusion
  579.5 1.9 copy.72
  584.1 1.5 fusion.75
  586.3 1.6 slice.295
  588.0 1.3 copy.94
  (98 shorter events, 25.3 us)
Async XLA Ops:
  7.2 12.8 %copy-start.7 = (bf16[4,145,1024]{2,0,1:T(4,128)(2,1)S(1)}, bf16[4,145,1024]{2,0,1:T(4,128)(2,1)}, u32[]{:S(2)}) copy-start(bf16[4,145,1024]{2,0,1:T(4,128)(2,1)} %param.33) | copy-start | bytes 3563524
  7.2 14.2 %copy-start.12 = (s32[32,40]{1,0:T(8,128)S(1)}, s32[32,40]{1,0:T(8,128)}, u32[]{:S(2)}) copy-start(s32[32,40]{1,0:T(8,128)} %param.34) | copy-start | bytes 15364
  7.2 576.9 %reduce-scatter.2.cloned.1.call-start = ((), (), s32[]{:S(2)}) async-start(), calls=%async_computation.1 | async-start | bytes 10948608 | tf_op jit(solution)/shard_map/reduce_scatter | solution.py:1144
  9.8 178.3 %copy-start.1 = (s32[33]{0:T(128)}, s32[33]{0:T(128)S(1)}, u32[]{:S(2)}) copy-start(s32[33]{0:T(128)S(1)} %convert_reduce_fusion.1.starts) | copy-start | bytes 400
  20.0 2.9 copy-start.13
  20.0 2.9 copy-start.14
  22.9 0.8 copy-start.11
  184.4 3.7 copy-start.2
  184.4 3.7 copy-start
  186.4 1.0 copy-start.5
  234.2 1.3 copy-start.3
  303.4 4.1 copy-start.19
  303.4 5.0 copy-start.20
  310.2 3.6 slice-start
  312.0 1.8 copy-start.18
  312.0 2.7 slice-start.1
  320.0 2.0 copy-start.4
  320.0 2.1 copy-start.21
  333.0 70.8 %copy-start.16 = (f32[4,1,768]{2,1,0:T(1,128)S(1)}, f32[4,1,768]{2,1,0:T(1,128)}, u32[]{:S(2)}) copy-start(f32[4,1,768]{2,1,0:T(1,128)} %get-tuple-element.88) | copy-start | bytes 36868
  333.0 71.5 %copy-start.15 = (f32[8,768]{1,0:T(8,128)S(1)}, f32[8,768]{1,0:T(8,128)}, u32[]{:S(2)}) copy-start(f32[8,768]{1,0:T(8,128)} %get-tuple-element.87) | copy-start | bytes 73732
  405.8 4.1 copy-start.8
  405.8 4.1 copy-start.9
  577.2 1.2 copy-start.17
  579.5 2.0 copy-start.10
  581.5 6.5 %copy-start.6 = (bf16[32,40,768]{2,1,0:T(8,128)(2,1)S(1)}, bf16[32,40,768]{2,1,0:T(8,128)(2,1)}, u32[]{:S(2)}) copy-start(bf16[32,40,768]{2,1,0:T(8,128)(2,1)} %get-tuple-element.258) | copy-start | bytes 5898244
Sparse Core Ops, SparseCore 0:
  332.1 175.5 reduce-scatter.1

commit v5 on v4

--- a/solution.py
+++ b/solution.py
@@ -237,18 +237,17 @@
     second = (xhat2 * g2[...] + s2[...]).astype(BF)
     sec32 = second.astype(F32)
     sec_o[...] = fold(sec32).astype(BF)
-    acc_s[...] = sec32 + nb[...]
-
-    def up(c, carry):
-        inner = nn(second, w1[c]) + wb[c]
+    total = sec32 + nb[...]
+    inner = nn(second, w1[0]) + wb[0]
+    for at in range(chunks):
+        following = nn(second, w1[at + 1]) + wb[at + 1] if at + 1 < chunks else None
         act, slope = gelu_parts(inner)
         act = act.astype(BF)
-        gp_s[c] = slope
-        act_o[c] = act
-        acc_s[...] += nn(act, w2[c])
-        return carry
-
-    lax.fori_loop(0, chunks, up, 0)
+        gp_s[at] = slope
+        act_o[at] = act
+        total = total + nn(act, w2[at])
+        inner = following
+    acc_s[...] = total
     xhat3, inv3 = norm_parts(acc_s[...])
     out_o[...] = fold(xhat3 * g3[...] + s3[...]).astype(BF)
     y = flat(og)
@@ -259,16 +258,16 @@
     vec_o[0:1] += jnp.sum(y * xhat3, 0, keepdims=True)
     vec_o[1:2] += jnp.sum(y, 0, keepdims=True)
     vec_o[2:3] += jnp.sum(gb3f, 0, keepdims=True)
-    acc_s[...] = grad_summed
-
-    def down(c, carry):
-        gi = (nt(gb3, w2[c]) * gp_s[c]).astype(BF)
-        gi_o[c] = gi
-        wbg_o[c] += jnp.sum(gi.astype(F32), 0, keepdims=True)
-        acc_s[...] += nt(gi, w1[c])
-        return carry
-
-    lax.fori_loop(0, chunks, down, 0)
+    total = grad_summed
+    back = nt(gb3, w2[0])
+    for at in range(chunks):
+        following = nt(gb3, w2[at + 1]) if at + 1 < chunks else None
+        gi = (back * gp_s[at]).astype(BF)
+        gi_o[at] = gi
+        wbg_o[at] += jnp.sum(gi.astype(F32), 0, keepdims=True)
+        total = total + nt(gi, w1[at])
+        back = following
+    acc_s[...] = total
     y2 = acc_s[...].astype(BF).astype(F32)
     gm = norm_back(y2, g2[...], xhat2, inv2)
     gm_o[...] = fold(gm)
@@ -962,6 +961,33 @@
     return w_shard, p_shard, tokens_grad
 
 
+def pack_kernel(chunks, patch, extra, *refs):
+    *mats, out = refs
+    sr, width = extra.shape
+    out[PATCH] = patch[0:sr]
+    out[EXTRA] = extra[...]
+    for at, ref in enumerate(mats[: W1 - QUERY]):
+        out[QUERY + at] = ref[...]
+    for at in range(chunks):
+        out[W1 + at] = mats[W1 - QUERY][:, width * at : width * (at + 1)]
+    for at, ref in enumerate(mats[W1 - QUERY + 1 :]):
+        out[CV + at] = ref[...]
+
+
+def pack(patch, extra, before, widen, after):
+    sr, width = extra.shape
+    chunks = widen.shape[1] // width
+    count = 2 + len(before) + chunks + len(after)
+    vmem = pl.BlockSpec(memory_space=pltpu.VMEM)
+    return pl.pallas_call(
+        functools.partial(pack_kernel, chunks),
+        in_specs=[vmem] * (3 + len(before) + len(after)),
+        out_specs=vmem,
+        out_shape=sds((count, sr, width), BF),
+        name="pack",
+    )(patch, extra, *before, widen, *after)
+
+
 def gather(value, axis):
     return lax.all_gather(value, AXES, axis=axis, tiled=True)
 
@@ -998,12 +1024,9 @@
     er = max(sr, extra.shape[0])
     own_rows = er == sr and groups == 8 and shards == 32
     extra = jnp.pad(extra, ((0, er - extra.shape[0]), (0, 0)))
-    slabs_in = jnp.stack(
-        [
-            patch_proj[:sr], extra[:sr], self_query, self_key, self_value, self_output, cross_query, cross_key,
-            *[widen_weight[:, width * at : width * (at + 1)] for at in range(chunks)],
-            cross_value, cross_output,
-        ]
+    slabs_in = pack(
+        patch_proj, extra[:sr], (self_query, self_key, self_value, self_output, cross_query, cross_key),
+        widen_weight, (cross_value, cross_output),
     )
 
     image = owner * images + image_slot

time: 602 us -> 584 us (0.970)
  local copies, waits for them, and re-layouts: 41.4 us -> 31 us
  Pallas kernels: 508 us -> 499 us
    pallas_call x1, Pallas kernels: 67.9 us -> 56.6 us  [on_device(): pl.pallas_call(tail_kernel, grid=grid, in_specs=[tb, tb, tb, wspec(CO), w...]
    unnamed x68 -> x48, local copies, waits for them, and re-layouts: 24.9 us -> 15.5 us
  transfers between devices with their start and end apart: 1 -> 1, of which waited for: 0 -> 0; matrix products, arithmetic and copies ran while one was open for 3% -> 3% of each run, Pallas kernels for 39% -> 41%
where the time goes in v5:
time: 584 us; the launch traced here: 578 us
  Pallas kernels  499 us (85%)
  local copies, waits for them, and re-layouts  31 us (5%)
  matrix products  23.7 us (4%)
  between operations  14.7 us (3%)
  other arithmetic  10 us (2%)
    pallas_call x1, Pallas kernels, back(): pl.pallas_call(functools.partial(back_kernel, rb, tails), in_specs=[hbm]...  165 us
    pallas_call x1, Pallas kernels, front(): pl.pallas_call(functools.partial(front_kernel, parts, tails, nv, rb), in_...  159 us
    pallas_call x1, Pallas kernels, on_device(): pl.pallas_call(cross_backward, grid_spec=pltpu.PrefetchScalarGridSpec(num...  72.2 us
    pallas_call x1, Pallas kernels, on_device(): pl.pallas_call(tail_kernel, grid=grid, in_specs=[tb, tb, tb, wspec(CO), w...  56.6 us
    pallas_call x1, Pallas kernels, on_device(): pl.pallas_call(cross_forward, grid_spec=pltpu.PrefetchScalarGridSpec(num_...  44.2 us
    dot_general x10, matrix products, tn(): lax.dot_general(left, right, (((0,), (0,)), ((), ())), preferred_element_...  22.6 us
    unnamed x48, local copies, waits for them, and re-layouts  15.5 us
  transfers between devices with their start and end apart: 1, of which 0 were waited for; matrix products, arithmetic and copies ran while one was open for 3% of the time, Pallas kernels for 41%

profile of v5, /device:TPU:0, one launch (start us, length us, event | category | flops | bytes accessed | tf_op | source)
XLA Modules:
  0.0 578.4 jit_solution(2807788113139507033)
XLA Ops:
  9.1 1.6 stack.71
  11.9 1.2 pad_maximum_fusion.2.bias
  13.2 1.4 copy.69.pat
  15.2 1.9 pack.1.w_in
  17.1 158.8 %front.1 = (bf16[14,4,2,2,2,24,768]{6,5,4,3,2,1,0:T(8,128)(2,1)}, bf16[4,2,2,2,96,768]{5,4,3,2,1,0:T(8,128)(2,1)}, bf16[4,2,4,145,768]{4,3,2,1,0:T(8,128)(2,1)},...) custom-call(bf16[14,24,768]{2,1,0:T(8,128)(2,1)} %pack.1.w_in, ...), custom_call_target="tpu_custom_call" | custom-call | tf_op jit(solution)/shard_map/front/pallas_call | solution.py:887
  176.0 1.6 fusion.75
  177.5 1.9 fusion.73
  181.2 44.2 %cross_forward.1 = (bf16[32,160,768]{2,1,0:T(8,128)(2,1)}, bf16[32,160,768]{2,1,0:T(8,128)(2,1)}, bf16[32,4,160,120]{3,2,1,0:T(8,128)(2,1)}, bf16[32,40,768]{2,1,0:T(8,128)(2,1)S(1)}) custom-call(s32[33]{0:T(128)S(1)} %convert_reduce_fusion.1.starts, s32[32]{0:T(128)S(1)} %select_reduce_fusion.order, bf16[32,145,768]{2,1,0:T(8,128)(2,1)} %bitcast.158, ...), custom_call_target="tpu_custom_call" | custom-call | flops 10947133440 | bytes 40000000 | tf_op jit(solution)/shard_map/cross_forward/pallas_call | solution.py:1096
  225.5 1.3 copy-done.3
  226.7 56.6 %tail.1 = (bf16[32,40,768]{2,1,0:T(8,128)(2,1)}, bf16[4,1280,768]{2,1,0:T(8,128)(2,1)}, bf16[4,1280,768]{2,1,0:T(8,128)(2,1)}, bf16[32,40,768]{2,1,0:T(8,128)(2,...) custom-call(f32[32,40,768]{2,1,0:T(8,128)} %get-tuple-element.63.u1,, ...), custom_call_target="tpu_custom_call" | custom-call | flops 37748736000 | bytes 50000000 | tf_op jit(solution)/shard_map/tail/pallas_call | solution.py:1117
  283.3 4.0 fusion.33
  288.3 1.8 fusion.30
  290.2 1.8 fusion.27
  292.0 1.8 fusion.24
  294.6 1.8 fusion.45
  296.4 1.8 fusion.42
  298.2 1.8 fusion.39
  300.0 2.0 fusion.36
  302.1 1.8 bitcast_convert_fusion
  303.9 1.1 constant_dynamic-update-slice_fusion.4
  306.2 1.2 constant_dynamic-update-slice_fusion.2
  309.5 2.3 maximum_dynamic-update-slice_fusion
  312.9 72.2 %cross_backward.1 = (bf16[32,40,768]{2,1,0:T(8,128)(2,1)}, bf16[32,145,768]{2,1,0:T(8,128)(2,1)}, bf16[768,768]{1,0:T(8,128)(2,1)}, bf16[768,768]{1,0:T(8,128)(2,1)}, f32[8,768]{1,0:T(8,128)}) custom-call(s32[33]{0:T(128)} %copy-done.1, s32[32]{0:T(128)} %copy-done.2, bf16[32,145,768]{2,1,0:T(8,128)(2,1)} %bitcast.159, ...), custom_call_target="tpu_custom_call" | custom-call | flops 21894266880 | bytes 50000000 | tf_op jit(solution)/shard_map/cross_backward/pallas_call | solution.py:1139
  386.7 1.3 concatenate.35.vt_in
  388.0 4.1 bitcast_convert_fusion.1
  392.1 2.0 pad_maximum_fusion.w_in
  394.1 165.2 %back.1 = (f32[9,24,768]{2,1,0:T(8,128)}, bf16[4,145,768]{2,1,0:T(8,128)(2,1)}, bf16[32,40,768]{2,1,0:T(8,128)(2,1)}) custom-call(bf16[3,4,2,2,2,24,768]{6,5,4,3,2,1,0:T(8,128)(2,1)} %pad_maximum_fusion.w_in, bf16[4,2,4,145,768]{4,3,2,1,0:T(8,128)(2,1)} %bitcast.160, f32[32,40,768]{2,1,0:T(8,128)} %get-tuple-element.80.gm, ...), custom_call_target="tpu_custom_call" | custom-call | tf_op jit(solution)/shard_map/back/pallas_call | solution.py:927
  560.5 1.2 convolution_convert_fusion
  561.7 1.9 copy.72
  566.2 1.5 fusion.74
  568.5 1.6 slice.275
  570.1 1.3 copy.81
  (79 shorter events, 17.8 us)
Async XLA Ops:
  7.2 5.9 %copy-start.7 = (bf16[4,145,1024]{2,0,1:T(4,128)(2,1)S(1)}, bf16[4,145,1024]{2,0,1:T(4,128)(2,1)}, u32[]{:S(2)}) copy-start(bf16[4,145,1024]{2,0,1:T(4,128)(2,1)} %param.33) | copy-start | bytes 3563524
  7.2 559.0 %reduce-scatter.2.cloned.1.call-start = ((), (), s32[]{:S(2)}) async-start(), calls=%async_computation.1 | async-start | bytes 10948608 | tf_op jit(solution)/shard_map/reduce_scatter | solution.py:1167
  8.1 173.1 %copy-start.1 = (s32[33]{0:T(128)}, s32[33]{0:T(128)S(1)}, u32[]{:S(2)}) copy-start(s32[33]{0:T(128)S(1)} %convert_reduce_fusion.1.starts) | copy-start | bytes 400
  8.4 172.8 %copy-start.2 = (s32[32]{0:T(128)}, s32[32]{0:T(128)S(1)}, u32[]{:S(2)}) copy-start(s32[32]{0:T(128)S(1)} %select_reduce_fusion.order) | copy-start | bytes 388
  11.9 2.7 slice-start
  177.5 3.7 copy-start
  179.5 1.0 copy-start.5
  225.5 1.3 copy-start.3
  283.3 4.1 copy-start.15
  283.3 5.0 copy-start.16
  290.1 3.6 slice-start.1
  291.9 1.8 copy-start.14
  292.0 2.7 slice-start.2
  300.0 2.0 copy-start.4
  300.0 2.1 copy-start.17
  312.9 73.0 %copy-start.12 = (f32[4,1,768]{2,1,0:T(1,128)S(1)}, f32[4,1,768]{2,1,0:T(1,128)}, u32[]{:S(2)}) copy-start(f32[4,1,768]{2,1,0:T(1,128)} %get-tuple-element.88) | copy-start | bytes 36868
  312.9 73.7 %copy-start.11 = (f32[8,768]{1,0:T(8,128)S(1)}, f32[8,768]{1,0:T(8,128)}, u32[]{:S(2)}) copy-start(f32[8,768]{1,0:T(8,128)} %get-tuple-element.87) | copy-start | bytes 73732
  388.0 4.1 copy-start.8
  388.0 4.1 copy-start.9
  559.3 1.2 copy-start.13
  561.7 2.0 copy-start.10
  563.6 6.5 %copy-start.6 = (bf16[32,40,768]{2,1,0:T(8,128)(2,1)S(1)}, bf16[32,40,768]{2,1,0:T(8,128)(2,1)}, u32[]{:S(2)}) copy-start(bf16[32,40,768]{2,1,0:T(8,128)(2,1)} %get-tuple-element.258) | copy-start | bytes 5898244
Sparse Core Ops, SparseCore 0:
  312.0 179.1 reduce-scatter.1

commit v6 on v5

--- a/solution.py
+++ b/solution.py
@@ -244,7 +244,7 @@
         act, slope = gelu_parts(inner)
         act = act.astype(BF)
         gp_s[at] = slope
-        act_o[at] = act
+        act_o[:, width * at : width * (at + 1)] = act
         total = total + nn(act, w2[at])
         inner = following
     acc_s[...] = total
@@ -263,7 +263,7 @@
     for at in range(chunks):
         following = nt(gb3, w2[at + 1]) if at + 1 < chunks else None
         gi = (back * gp_s[at]).astype(BF)
-        gi_o[at] = gi
+        gi_o[:, width * at : width * (at + 1)] = gi
         wbg_o[at] += jnp.sum(gi.astype(F32), 0, keepdims=True)
         total = total + nt(gi, w1[at])
         back = following
@@ -506,9 +506,10 @@
     "G", "self", "G", "R", "R", "i1", "F", "i2", "self", "R", "R", "G", "i2", "R",
 )
 BACK_ORDER = (
-    "p2", "S", "E", "E", "p0", "p2", "p1", "S", "p0", "S", "p1", "p3", "S", "S", "D1", "D2", "L2",
-    "E", "L2", "p3", "L1", "L1", "L2", "p2", "p0", "L1", "p1", "E", "p3", "V1", "V1", "V2", "L2",
-    "E", "V2", "L1", "V1", "V1", "V2", "V2", "L2", "V1", "L1", "V2",
+    "E", "p0", "S", "p1", "E", "S", "p0", "p2", "S", "S", "p1", "S", "D1", "L1", "p0", "p0", "p3",
+    "p1", "D2", "p2", "L1", "p2", "p0", "p1", "p3", "L2", "p1", "E", "p2", "p3", "L2", "p2", "L1",
+    "p3", "L2", "p3", "E", "V1", "L2", "V1", "V2", "L1", "V2", "V1", "V2", "L2", "E", "V1", "L1",
+    "V2", "V1", "S", "V2",
 )
 
 
@@ -753,22 +754,62 @@
         own.wait()
         yield from job
 
+    inner = (z + 1) % 4 >= 2
+    outer = jnp.logical_not(inner)
+    partner = z + 1 - 2 * (z % 2)
+    ours, theirs = 2 * (z // 2), 2 - 2 * (z // 2)
+
     def image(i):
-        own = copies.here(p_in.at[:, y, i], pacc.at[i])
+        mine = copies.here(p_in.at[:, y, i], pacc.at[i])
         step = copies.remote(p_in.at[:, 1 - y, i], pry.at[i], device_at(z, 1 - y, x, c))
         yield
-        own.wait()
+        mine.wait()
         step.wait()
-        steps = []
-        for hop in (1, 3, 2):
-            zz = (z + hop) % 4
-            pacc[i, zz] = (up(pacc, i, zz) + up(pry, i, zz)).astype(BF)
-            steps.append(copies.remote(pacc.at[i, zz], prz.at[hop - 1, i], device_at(zz, y, x, c)))
-        yield
-        arrived(steps)
-        p_out[i] = (
-            up(pacc, i, z) + up(pry, i, z) + up(prz, 0, i) + up(prz, 1, i) + up(prz, 2, i)
-        ).astype(BF)
+        pair = pacc.at[i, pl.ds(theirs, 2)]
+        inward = copies.prepare(pair, prz.at[i, pl.ds(0, 2)], device_at(partner, y, x, c))
+        middle = copies.prepare(pair, prz.at[i, pl.ds(2, 2)], device_at(3 - z, y, x, c))
+        swap = copies.prepare(pacc.at[i, partner], prz.at[i, 4], device_at(partner, y, x, c))
+
+        def own(zz):
+            return up(pacc, i, zz) + up(pry, i, zz)
+
+        @pl.when(outer)
+        def _():
+            for at in range(2):
+                pacc[i, theirs + at] = own(theirs + at).astype(BF)
+            inward.start()
+            pacc[i, partner] = own(partner).astype(BF)
+            swap.start()
+
+        yield
+
+        @pl.when(inner)
+        def _():
+            inward.wait_recv()
+            for at in range(2):
+                pacc[i, theirs + at] = (own(theirs + at) + up(prz, i, at)).astype(BF)
+            middle.start()
+
+        yield
+
+        @pl.when(inner)
+        def _():
+            middle.wait()
+            pacc[i, partner] = (own(partner) + up(prz, i, 2 + partner - ours)).astype(BF)
+            swap.start()
+
+        yield
+        swap.wait()
+
+        @pl.when(inner)
+        def _():
+            p_out[i] = (own(z) + up(prz, i, 2 + z - ours) + up(prz, i, 4)).astype(BF)
+
+        @pl.when(outer)
+        def _():
+            inward.wait_send()
+            p_out[i] = (own(z) + up(prz, i, 4)).astype(BF)
+
         yield
 
     def attention():
@@ -945,7 +986,7 @@
             pltpu.VMEM((3, m) + part, BF),
             pltpu.VMEM((images, 4, points, width), BF),
             pltpu.VMEM((images, 4, points, width), BF),
-            pltpu.VMEM((3, images, points, width), BF),
+            pltpu.VMEM((images, 5, points, width), BF),
             pltpu.SemaphoreType.DMA((remote,)),
             pltpu.SemaphoreType.DMA((remote,)),
             pltpu.SemaphoreType.DMA((near,)),
@@ -1112,8 +1153,8 @@
         (chunks, width, width), lambda i, *_: (W1 // chunks, 0, 0), pipeline_mode=pl.Buffered(1)
     )
     n_tok = rows * length
-    hid_sh = (chunks, n_tok, width)
-    hid_spec = pl.BlockSpec((chunks, rb * length, width), lambda i, *_: (0, i, 0))
+    hid_sh = (n_tok, hidden)
+    hid_spec = pl.BlockSpec((rb * length, hidden), lambda i, *_: (i, 0))
     (output, active, grad_inner, second, gb3, grad_mid, gb2, grad_crossed, vec_t, wb_grad) = pl.pallas_call(
         tail_kernel,
         grid=grid,
@@ -1160,9 +1201,9 @@
     def wgrad(left, right):
         return tn(left.reshape(n_tok, width), right.reshape(n_tok, width)).astype(BF)
 
-    ffn = [wgrad(second, grad_inner[at]).reshape(shards, sr, width) for at in range(chunks)]
+    ffn = [wgrad(second, grad_inner[:, width * at : width * (at + 1)]).reshape(shards, sr, width) for at in range(chunks)]
     ffn.append(wgrad(mixed, gb2).reshape(shards, sr, width))
-    narrow_grad = [wgrad(active[at], gb3).reshape(shards // chunks, wr, width) for at in range(chunks)]
+    narrow_grad = [wgrad(active[:, width * at : width * (at + 1)], gb3).reshape(shards // chunks, wr, width) for at in range(chunks)]
     ffn.append(jnp.concatenate(narrow_grad))
     ffn_shard = lax.psum_scatter(
         jnp.concatenate(ffn, 1).reshape(-1, width), AXES, scatter_dimension=0, tiled=True

time: 584 us -> 582 us (level)
    pallas_call x1, Pallas kernels: 165 us -> 159 us  [back(): pl.pallas_call(functools.partial(back_kernel, rb, tails), in_specs=[hbm]...]
where the time goes in v6:
time: 582 us; the launch traced here: 577 us
  Pallas kernels  497 us (85%)
  local copies, waits for them, and re-layouts  31 us (5%)
  matrix products  23.9 us (4%)
  between operations  14.7 us (3%)
  other arithmetic  9.96 us (2%)
    pallas_call x1, Pallas kernels, front(): pl.pallas_call(functools.partial(front_kernel, parts, tails, nv, rb), in_...  159 us
    pallas_call x1, Pallas kernels, back(): pl.pallas_call(functools.partial(back_kernel, rb, tails), in_specs=[hbm]...  159 us
    pallas_call x1, Pallas kernels, on_device(): pl.pallas_call(cross_backward, grid_spec=pltpu.PrefetchScalarGridSpec(num...  75 us
    pallas_call x1, Pallas kernels, on_device(): pl.pallas_call(tail_kernel, grid=grid, in_specs=[tb, tb, tb, wspec(CO), w...  55.3 us
    pallas_call x1, Pallas kernels, on_device(): pl.pallas_call(cross_forward, grid_spec=pltpu.PrefetchScalarGridSpec(num_...  47.4 us
    dot_general x10, matrix products, tn(): lax.dot_general(left, right, (((0,), (0,)), ((), ())), preferred_element_...  22.7 us
    unnamed x48, local copies, waits for them, and re-layouts  15.5 us
  transfers between devices with their start and end apart: 1, of which 0 were waited for; matrix products, arithmetic and copies ran while one was open for 3% of the time, Pallas kernels for 41%

profile of v6, /device:TPU:0, one launch (start us, length us, event | category | flops | bytes accessed | tf_op | source)
XLA Modules:
  0.0 576.6 jit_solution(2026412444170900259)
XLA Ops:
  9.1 1.6 stack.71
  11.9 1.2 pad_maximum_fusion.2.bias
  13.2 1.4 copy.69.pat
  15.2 1.9 pack.1.w_in
  17.1 158.8 %front.1 = (bf16[14,4,2,2,2,24,768]{6,5,4,3,2,1,0:T(8,128)(2,1)}, bf16[4,2,2,2,96,768]{5,4,3,2,1,0:T(8,128)(2,1)}, bf16[4,2,4,145,768]{4,3,2,1,0:T(8,128)(2,1)},...) custom-call(bf16[14,24,768]{2,1,0:T(8,128)(2,1)} %pack.1.w_in, ...), custom_call_target="tpu_custom_call" | custom-call | tf_op jit(solution)/shard_map/front/pallas_call | solution.py:928
  176.0 1.6 fusion.67
  177.5 1.9 fusion.65
  181.2 47.4 %cross_forward.1 = (bf16[32,160,768]{2,1,0:T(8,128)(2,1)}, bf16[32,160,768]{2,1,0:T(8,128)(2,1)}, bf16[32,4,160,120]{3,2,1,0:T(8,128)(2,1)}, bf16[32,40,768]{2,1,0:T(8,128)(2,1)S(1)}) custom-call(s32[33]{0:T(128)S(1)} %convert_reduce_fusion.1.starts, s32[32]{0:T(128)S(1)} %select_reduce_fusion.order, bf16[32,145,768]{2,1,0:T(8,128)(2,1)} %bitcast.118, ...), custom_call_target="tpu_custom_call" | custom-call | flops 10947133440 | bytes 40000000 | tf_op jit(solution)/shard_map/cross_forward/pallas_call | solution.py:1137
  228.6 1.3 copy-done.3
  229.9 55.3 %tail.1 = (bf16[32,40,768]{2,1,0:T(8,128)(2,1)}, bf16[1280,3072]{1,0:T(8,128)(2,1)}, bf16[1280,3072]{1,0:T(8,128)(2,1)}, bf16[32,40,768]{2,1,0:T(8,128)(2,1)}, b...) custom-call(f32[32,40,768]{2,1,0:T(8,128)} %get-tuple-element.63.u1,, ...), custom_call_target="tpu_custom_call" | custom-call | flops 37748736000 | bytes 50000000 | tf_op jit(solution)/shard_map/tail/pallas_call | solution.py:1158
  285.2 4.0 fusion.25
  290.2 1.8 fusion.22
  292.1 1.8 fusion.19
  293.9 1.8 fusion.16
  296.6 1.8 fusion.37
  298.4 1.8 fusion.34
  300.2 1.8 fusion.31
  302.0 2.0 fusion.28
  304.1 1.8 bitcast_convert_fusion
  305.9 1.1 constant_dynamic-update-slice_fusion.4
  308.1 1.2 constant_dynamic-update-slice_fusion.2
  311.5 2.3 maximum_dynamic-update-slice_fusion
  314.9 75.0 %cross_backward.1 = (bf16[32,40,768]{2,1,0:T(8,128)(2,1)}, bf16[32,145,768]{2,1,0:T(8,128)(2,1)}, bf16[768,768]{1,0:T(8,128)(2,1)}, bf16[768,768]{1,0:T(8,128)(2,1)}, f32[8,768]{1,0:T(8,128)}) custom-call(s32[33]{0:T(128)} %copy-done.1, s32[32]{0:T(128)} %copy-done.2, bf16[32,145,768]{2,1,0:T(8,128)(2,1)} %bitcast.119, ...), custom_call_target="tpu_custom_call" | custom-call | flops 21894266880 | bytes 50000000 | tf_op jit(solution)/shard_map/cross_backward/pallas_call | solution.py:1180
  391.5 1.3 concatenate.35.vt_in
  392.7 4.1 bitcast_convert_fusion.1
  396.8 2.0 pad_maximum_fusion.w_in
  398.8 158.7 %back.1 = (f32[9,24,768]{2,1,0:T(8,128)}, bf16[4,145,768]{2,1,0:T(8,128)(2,1)}, bf16[32,40,768]{2,1,0:T(8,128)(2,1)}) custom-call(bf16[3,4,2,2,2,24,768]{6,5,4,3,2,1,0:T(8,128)(2,1)} %pad_maximum_fusion.w_in, bf16[4,2,4,145,768]{4,3,2,1,0:T(8,128)(2,1)} %bitcast.120, f32[32,40,768]{2,1,0:T(8,128)} %get-tuple-element.80.gm, ...), custom_call_target="tpu_custom_call" | custom-call | tf_op jit(solution)/shard_map/back/pallas_call | solution.py:968
  558.7 1.2 convolution_convert_fusion
  559.9 1.9 copy.72
  564.4 1.5 fusion.66
  566.6 1.6 slice.275
  568.3 1.3 copy.81
  (79 shorter events, 17.8 us)
Async XLA Ops:
  7.2 5.9 %copy-start.7 = (bf16[4,145,1024]{2,0,1:T(4,128)(2,1)S(1)}, bf16[4,145,1024]{2,0,1:T(4,128)(2,1)}, u32[]{:S(2)}) copy-start(bf16[4,145,1024]{2,0,1:T(4,128)(2,1)} %param.33) | copy-start | bytes 3563524
  7.2 557.2 %reduce-scatter.2.cloned.1.call-start = ((), (), s32[]{:S(2)}) async-start(), calls=%async_computation.1 | async-start | bytes 10948608 | tf_op jit(solution)/shard_map/reduce_scatter | solution.py:1208
  8.1 173.1 %copy-start.1 = (s32[33]{0:T(128)}, s32[33]{0:T(128)S(1)}, u32[]{:S(2)}) copy-start(s32[33]{0:T(128)S(1)} %convert_reduce_fusion.1.starts) | copy-start | bytes 400
  8.4 172.8 %copy-start.2 = (s32[32]{0:T(128)}, s32[32]{0:T(128)S(1)}, u32[]{:S(2)}) copy-start(s32[32]{0:T(128)S(1)} %select_reduce_fusion.order) | copy-start | bytes 388
  11.9 2.7 slice-start
  177.5 3.7 copy-start
  179.5 1.0 copy-start.5
  228.6 1.3 copy-start.3
  285.2 4.1 copy-start.15
  285.2 5.0 copy-start.16
  292.1 3.7 slice-start.1
  293.9 1.8 copy-start.14
  293.9 2.7 slice-start.2
  302.0 2.0 copy-start.4
  302.0 2.1 copy-start.17
  314.9 75.7 %copy-start.12 = (f32[4,1,768]{2,1,0:T(1,128)S(1)}, f32[4,1,768]{2,1,0:T(1,128)}, u32[]{:S(2)}) copy-start(f32[4,1,768]{2,1,0:T(1,128)} %get-tuple-element.88) | copy-start | bytes 36868
  314.9 76.5 %copy-start.11 = (f32[8,768]{1,0:T(8,128)S(1)}, f32[8,768]{1,0:T(8,128)}, u32[]{:S(2)}) copy-start(f32[8,768]{1,0:T(8,128)} %get-tuple-element.87) | copy-start | bytes 73732
  392.7 4.1 copy-start.8
  392.7 4.1 copy-start.9
  557.5 1.2 copy-start.13
  559.9 2.0 copy-start.10
  561.8 6.5 %copy-start.6 = (bf16[32,40,768]{2,1,0:T(8,128)(2,1)S(1)}, bf16[32,40,768]{2,1,0:T(8,128)(2,1)}, u32[]{:S(2)}) copy-start(bf16[32,40,768]{2,1,0:T(8,128)(2,1)} %get-tuple-element.258) | copy-start | bytes 5898244
Sparse Core Ops, SparseCore 0:
  314.0 158.7 reduce-scatter.1
